TPU v7x, 32 devices: a whole 2x2x4 slice. The times are simulated.
32 devices in a mesh: section: 4 (over y, x), member: 8 (over z, core).
Axes of the slice: x: 2, y: 2, z: 4, core: 2. Of those that a mesh axis runs over, the one named last changes fastest.
Arguments:
- populations: float32 [64, 19, 4096], P(('section', 'member'))
- fluid_mask: int32 [64, 4096], P(('section', 'member')), may hold values 0 or 1
- section_level: int32 [4], replicated, may hold values from 0 to 2, as said below
- neighbours: int32 [64, 18], P(('section', 'member')), may hold values from -1 to 63, as said below
- interface: int32 [64, 6, 4], P(('section', 'member')), may hold values from -1 to 63, as said below
Outputs:
- final_populations: float32 [64, 19, 4096], P(('section', 'member'))
Inputs may be any that keep to these rules, and one draw needn't show every extreme that they name: `section_level`: levels never fall along the section axis and each of 0, 1, 2 is held by some section. `neighbours`: A neighbour lies in the same section as the block, on the same member index or one beside it. `interface`: entries stand only on faces whose neighbour is -1; the named blocks lie in a section whose level differs from the block's by one, on the same member index or one beside it. Where that level is below the block's, exactly one quadrant of the face is named, else all four.
All inputs are finite; a program needn't handle non-finite values. No bound on the sum of `fluid_mask` on one device may be relied on, other than what follows from the above.
Results may differ from a plain program's by a relative error of at most 0.0003.
Values sent between devices are 32-bit elements; how exact they have to be, the bound alone decides.
No kernel may reach another device: no remote copies, remote signals or barrier semaphores. Data moves between devices by JAX's collectives and lax.ppermute only.
A program may use at most 64 MiB of HBM per device.

v0:
```python
import functools

import jax
import jax.numpy as jnp
from jax import lax
from jax.experimental import pallas as pl
from jax.experimental.pallas import tpu as pltpu
from jax.sharding import PartitionSpec as P

VELOCITIES = (
    (0, 0, 0), (1, 0, 0), (-1, 0, 0), (0, 1, 0), (0, -1, 0), (0, 0, 1), (0, 0, -1),
    (1, 1, 0), (-1, -1, 0), (1, -1, 0), (-1, 1, 0), (1, 0, 1), (-1, 0, -1), (1, 0, -1),
    (-1, 0, 1), (0, 1, 1), (0, -1, -1), (0, 1, -1), (0, -1, 1),
)
WEIGHTS = (1.0 / 3.0,) + (1.0 / 18.0,) * 6 + (1.0 / 36.0,) * 12
OPPOSITE = (0, 2, 1, 4, 3, 6, 5, 8, 7, 10, 9, 12, 11, 14, 13, 16, 15, 18, 17)
LISTS = [
    [q for q in range(19) if sum(a * b for a, b in zip(VELOCITIES[q], VELOCITIES[1 + j])) == 1]
    for j in range(6)
]
ROWS = 64
TILES = 8


def iotas():
    sub = lax.broadcasted_iota(jnp.int32, (8, 128), 0)
    lane = lax.broadcasted_iota(jnp.int32, (8, 128), 1)
    return sub, lane


def pick(x, index):
    return jnp.take_along_axis(x, index, axis=1, mode="promise_in_bounds")


def lanes(x, shift):
    return pltpu.roll(x, shift % 128, 1)


def subs(x, shift):
    return pltpu.roll(x, shift % 8, 0)


def tile(ref, q, t):
    return ref[q, 8 * t : 8 * t + 8, :]


def bulk(ref, row):
    return jnp.broadcast_to(ref[row : row + 1, :], (8, 128))


def relax_rate(level):
    return jnp.where(
        level == 0, jnp.float32(1.0 / 0.55), jnp.where(level == 1, jnp.float32(1.0 / 0.6), jnp.float32(1.0 / 0.7))
    )


def collide(src, dst, mask, rate):
    for t in range(TILES):
        f = [tile(src, q, t) for q in range(19)]
        density = f[0]
        for q in range(1, 19):
            density = density + f[q]
        velocity = []
        for a in range(3):
            plus = [q for q in range(19) if VELOCITIES[q][a] > 0]
            total = f[plus[0]] - f[OPPOSITE[plus[0]]]
            for q in plus[1:]:
                total = total + (f[q] - f[OPPOSITE[q]])
            velocity.append(total / density)
        speed = velocity[0] * velocity[0] + velocity[1] * velocity[1] + velocity[2] * velocity[2]
        base = 1.0 - 1.5 * speed
        fluid = mask[8 * t : 8 * t + 8, :] == 1
        keep = 1.0 - rate
        scaled = [rate * jnp.float32(w) * density for w in (WEIGHTS[0], WEIGHTS[1], WEIGHTS[7])]
        out = keep * f[0] + scaled[0] * base
        dst[0, 8 * t : 8 * t + 8, :] = jnp.where(fluid, out, f[0])
        for q in range(1, 19, 2):
            o = OPPOSITE[q]
            along = None
            for a in range(3):
                c = VELOCITIES[q][a]
                if c:
                    term = velocity[a] if c > 0 else -velocity[a]
                    along = term if along is None else along + term
            weight = scaled[1] if q < 7 else scaled[2]
            even = base + 4.5 * along * along
            odd = 3.0 * along
            dst[q, 8 * t : 8 * t + 8, :] = jnp.where(fluid, keep * f[q] + weight * (even + odd), f[o])
            dst[o, 8 * t : 8 * t + 8, :] = jnp.where(fluid, keep * f[o] + weight * (even - odd), f[q])


def export(src, out):
    sub, lane = iotas()
    xl, yh = sub // 4, (sub // 2) % 2
    for j in range(6):
        axis, high = j // 2, j % 2 == 0
        for i, q in enumerate(LISTS[j]):
            if axis == 0:
                v = tile(src, q, TILES - 1 if high else 0)
                first = 4 if high else 0
                for h in range(2):
                    for b in range(2):
                        s = first + 2 * h + b
                        r = 10 * j + 5 * h + i
                        out[b, r : r + 1, :] = v[s : s + 1, :]
                continue
            for h in range(2):
                total = jnp.zeros((8, 128), jnp.float32)
                for k in range(4):
                    if axis == 1:
                        index = (lane & 15) + (112 if high else 0)
                        here = (lane >> 4 == 2 * k + xl) & (yh == (1 if high else 0))
                    else:
                        index = (lane & 7) * 16 + (15 if high else 0)
                        here = lane >> 3 == (2 * k + xl) * 2 + yh
                    total = jnp.where(here, pick(tile(src, q, 4 * h + k), index), total)
                total = total + subs(total, 4)
                total = total + subs(total, 2)
                for b in range(2):
                    r = 10 * j + 5 * h + i
                    out[b, r : r + 1, :] = total[b : b + 1, :]


def slots(block_id, me, sections, members, blocks):
    safe = jnp.maximum(block_id, 0)
    section = safe // (members * blocks)
    member = (safe // blocks) % members
    offset = member - me[1]
    chip = jnp.where(me[1] % 2 == 0, 1, -1)
    which = jnp.where(offset == 0, 0, jnp.where(offset == chip, 1, 2))
    if sections & (sections - 1) == 0:
        apart = section ^ me[0]
    else:
        apart = (me[0] + sections - section) % sections
    slot = (which * sections + apart) * blocks + safe % blocks
    return jnp.where(block_id >= 0, slot, 0), section


def arrived(level_ref, near_ref, link_ref, table, halo, me, sizes):
    sections, members, blocks = sizes
    sub, lane = iotas()
    level = level_ref[me[0]]
    for block in range(blocks):
        for j in range(6):
            first = 10 * (j ^ 1)

            def rows(slot, part):
                return table[slot, first + 5 * part : first + 5 * part + 5, :]

            near_id = near_ref[block, j]
            near, _ = slots(near_id, me, sections, members, blocks)
            ids = [link_ref[block, k, j] for k in range(4)]
            placed = [slots(i, me, sections, members, blocks) for i in ids]
            coarse = [(ids[k] >= 0) & (level_ref[placed[k][1]] < level) for k in range(4)]
            fine = [(ids[k] >= 0) & (level_ref[placed[k][1]] >= level) for k in range(4)]
            any_coarse = coarse[0] | coarse[1] | coarse[2] | coarse[3]
            any_fine = fine[0] | fine[1] | fine[2] | fine[3]
            rest = [WEIGHTS[q] for q in LISTS[j ^ 1]]

            @pl.when(near_id >= 0)
            def _():
                halo[block, 10 * j : 10 * j + 10, :] = table[near, first : first + 10, :]

            @pl.when((near_id < 0) & any_coarse)
            def _():
                slot = jnp.where(
                    coarse[0], placed[0][0], jnp.where(coarse[1], placed[1][0], jnp.where(coarse[2], placed[2][0], placed[3][0]))
                )
                a = jnp.where(coarse[0] | coarse[1], 0, 1)
                b = jnp.where(coarse[0] | (coarse[2] & jnp.logical_not(coarse[1])), 0, 1)
                source = jnp.where(a == 0, rows(slot, 0), rows(slot, 1))
                for h in range(2):
                    index = (4 * h + (lane[:5] >> 5)) * 16 + 8 * b + ((lane[:5] & 15) >> 1)
                    halo[block, 10 * j + 5 * h : 10 * j + 5 * h + 5, :] = pick(source, index)

            @pl.when((near_id < 0) & jnp.logical_not(any_coarse) & any_fine)
            def _():
                index = (lane[:5] >> 4) % 4 * 32 + 2 * (lane[:5] & 7)
                quads = []
                for k in range(4):
                    parts = []
                    for h in range(2):
                        v = rows(placed[k][0], h)
                        v = v + lanes(v, -1)
                        v = v + lanes(v, -16)
                        parts.append(pick(v, index))
                    quad = jnp.where(lane[:5] >= 64, parts[1], parts[0])
                    quads.append(quad * jnp.where(fine[k], jnp.float32(0.25), jnp.float32(0.0)))
                for a in range(2):
                    halo[block, 10 * j + 5 * a : 10 * j + 5 * a + 5, :] = jnp.where(
                        lane[:5] & 8 == 0, quads[2 * a], quads[2 * a + 1]
                    )

            @pl.when((near_id < 0) & jnp.logical_not(any_coarse | any_fine))
            def _():
                for h in range(2):
                    for i in range(5):
                        r = 10 * j + 5 * h + i
                        halo[block, r : r + 1, :] = jnp.full((1, 128), rest[i], jnp.float32)


def stream(src, dst, near_ref, table, halo, me, sizes):
    sections, members, blocks = sizes
    sub, lane = iotas()
    odd = (sub & 1) == 1
    xl, yh = sub // 4, (sub // 2) % 2
    z = lane & 15
    bases = [(2 * k + xl) * 16 for k in range(4)]

    def plane(j, i, h):
        return jnp.where(odd, bulk(halo.at[1], 10 * j + 5 * h + i), bulk(halo.at[0], 10 * j + 5 * h + i))

    for q in range(19):
        c = VELOCITIES[q]
        moving = [a for a in range(3) if c[a]]
        values = [tile(src, q, t) for t in range(TILES)]
        planes = {}
        for a in moving:
            j = 2 * a + (0 if c[a] < 0 else 1)
            i = LISTS[j ^ 1].index(q)
            planes[a] = [plane(j, i, h) for h in range(2)]
        line = None
        if len(moving) == 2:
            e = VELOCITIES.index(tuple(-v for v in c)) - 1
            j = 2 * moving[0] + (0 if c[moving[0]] > 0 else 1)
            i = LISTS[j].index(q)
            found = []
            for block in range(blocks):
                block_id = near_ref[block, e]
                slot, _ = slots(block_id, me, sections, members, blocks)
                good = jnp.full((8, 128), block_id, jnp.int32) >= 0
                found.append(
                    [jnp.where(good, bulk(table.at[slot], 10 * j + 5 * h + i), jnp.float32(WEIGHTS[q])) for h in range(2)]
                )
            line = [jnp.where(odd, found[1][h], found[0][h]) for h in range(2)]
        outside = jnp.where(yh == 1, planes[0][1], planes[0][0]) if c[0] else None

        if c[2]:
            up = c[2] > 0
            edge = z == (0 if up else 15)
            if not c[0] or c[2]:
                values = [
                    jnp.where(edge, pick(planes[2][t // 4], bases[t % 4] + yh * 8 + (lane >> 4)), lanes(v, c[2]))
                    for t, v in enumerate(values)
                ]
            if c[0]:
                spread = jnp.where(yh == 1, line[1], line[0])
                outside = jnp.where(edge, lanes(spread, -15 if up else 15), lanes(outside, c[2]))
        if c[1]:
            up = c[1] > 0
            edge = lane < 16 if up else lane >= 112
            inner = yh == (1 if up else 0)

            def moved(v, border):
                rolled = lanes(v, 16 * c[1])
                return jnp.where(edge, jnp.where(inner, subs(rolled, 2 * c[1]), border), rolled)

            for t in range(TILES):
                base, source = bases[t % 4], planes[1][t // 4]
                if c[2]:
                    if c[2] > 0:
                        border = jnp.where(z == 0, pick(line[t // 4], base + 15), pick(source, base + jnp.maximum(z - 1, 0)))
                    else:
                        border = jnp.where(z == 15, pick(line[t // 4], base), pick(source, base + jnp.minimum(z + 1, 15)))
                else:
                    border = pick(source, base + z)
                values[t] = moved(values[t], border)
            if c[0]:
                outside = moved(outside, lanes(line[1 if up else 0], 16 * c[1]))
        if c[0]:
            rolled = [subs(v, 4) for v in values]
            if c[0] > 0:
                values = [jnp.where(sub < 4, rolled[t - 1] if t else outside, rolled[t]) for t in range(TILES)]
            else:
                values = [
                    jnp.where(sub >= 4, rolled[t + 1] if t < TILES - 1 else outside, rolled[t]) for t in range(TILES)
                ]
        for t in range(TILES):
            dst[q, 8 * t : 8 * t + 8, :] = values[t]


def first_kernel(sizes, level_ref, pops, mask, star, out):
    level = level_ref[lax.axis_index("section")]

    @pl.when(level >= 1)
    def _():
        collide(pops, star, mask, relax_rate(level))

    @pl.when(level < 1)
    def _():
        star[...] = pops[...]

    export(star, out)


def fetch(sizes, parts, table, sems):
    sections, _, blocks = sizes
    each = sections * blocks
    copies = [
        pltpu.make_async_copy(part, table.at[pl.ds(each * i, each)], sems.at[i]) for i, part in enumerate(parts)
    ]
    for copy in copies:
        copy.start()
    for copy in copies:
        copy.wait()


def next_kernel(sizes, last, level_ref, near_ref, link_ref, star, mask, own, chip, far, dst, *rest):
    out = None if last else rest[0]
    table, halo, sems = rest[-3:]
    me = (lax.axis_index("section"), lax.axis_index("member"))
    level = level_ref[me[0]]
    fetch(sizes, (own, chip, far), table, sems)
    moves = level == 2 if last else level >= 1

    @pl.when(moves)
    def _():
        arrived(level_ref, near_ref, link_ref, table, halo, me, sizes)
        stream(star, dst, near_ref, table, halo, me, sizes)

    @pl.when(jnp.logical_not(moves))
    def _():
        dst[...] = star[...]

    if not last:

        @pl.when(level == 2)
        def _():
            collide(dst, dst, mask, relax_rate(level))

        export(dst, out)


def swap(x, sections, members, target):
    pairs = []
    for s in range(sections):
        for m in range(members):
            t = target(s, m)
            if 0 <= t[1] < members:
                pairs.append((s * members + m, t[0] * members + t[1]))
    return lax.ppermute(x, ("section", "member"), pairs)


def exchange(exports, sections, members):
    power = sections & (sections - 1) == 0

    def across(d):
        return lambda s, m: (s ^ d if power else (s + d) % sections, m)

    parts = [exports] + [swap(exports, sections, members, across(d)) for d in range(1, sections)]
    own = jnp.concatenate(parts, axis=0)
    chip = swap(own, sections, members, lambda s, m: (s, m ^ 1))
    far = swap(own, sections, members, lambda s, m: (s, ((m + 1) ^ 1) - 1))
    return own, chip, far


def packed(x):
    n, cells = x.shape[0], x.shape[-1]
    x = x.reshape(n, -1, cells // 128, 128)
    return x.transpose(1, 2, 0, 3).reshape(-1, n * cells // 128, 128)


VMEM = pl.BlockSpec(memory_space=pltpu.VMEM)
SMEM = pl.BlockSpec(memory_space=pltpu.SMEM)
ANY = pl.BlockSpec(memory_space=pl.ANY)


def body(populations, fluid_mask, section_level, neighbours, interface):
    sections, members = lax.axis_size("section"), lax.axis_size("member")
    blocks, _, cells = populations.shape
    sizes = (sections, members, blocks)
    params = pltpu.CompilerParams(vmem_limit_bytes=16 << 20)
    pops = packed(populations)
    mask = packed(fluid_mask)[0]
    links = interface.transpose(0, 2, 1)
    field = jax.ShapeDtypeStruct(pops.shape, jnp.float32)
    planes = jax.ShapeDtypeStruct((blocks, ROWS, 128), jnp.float32)
    star, exports = pl.pallas_call(
        functools.partial(first_kernel, sizes),
        out_shape=(field, planes),
        in_specs=[SMEM, VMEM, VMEM],
        out_specs=(VMEM, VMEM),
        compiler_params=params,
        name="first",
    )(section_level, pops, mask)
    scratch = [
        pltpu.VMEM((3 * sections * blocks, ROWS, 128), jnp.float32),
        pltpu.VMEM((blocks, ROWS, 128), jnp.float32),
        pltpu.SemaphoreType.DMA((3,)),
    ]
    for last in (False, True):
        own, chip, far = exchange(exports, sections, members)
        result = pl.pallas_call(
            functools.partial(next_kernel, sizes, last),
            out_shape=(field,) if last else (field, planes),
            in_specs=[SMEM, SMEM, SMEM, VMEM, VMEM, ANY, ANY, ANY],
            out_specs=(VMEM,) if last else (VMEM, VMEM),
            scratch_shapes=scratch,
            compiler_params=params,
            name="last" if last else "middle",
        )(section_level, neighbours, links, star, mask, own, chip, far)
        if last:
            (star,) = result
        else:
            star, exports = result
    out = star.reshape(19, cells // 128, blocks, 128).transpose(2, 0, 1, 3)
    return out.reshape(blocks, 19, cells)


def solution(mesh):
    return jax.shard_map(
        body,
        mesh=mesh,
        in_specs=(
            P(("section", "member"), None, None),
            P(("section", "member"), None),
            P(),
            P(("section", "member"), None),
            P(("section", "member"), None, None),
        ),
        out_specs=P(("section", "member"), None, None),
        check_vma=False,
    )
```

profile of v0, /device:TPU:15, one launch (start us, length us, event | category | flops | bytes accessed | tf_op | source)
XLA Modules:
  0.0 40.7 jit_solution(17509665933024620179)
XLA Ops:
  0.0 0.0 copy-start.3
  0.0 0.7 %copy-done.3 = s32[4]{0:T(128)S(1)} copy-done((s32[4]{0:T(128)S(1)}, s32[4]{0:T(128)}, u32[]{:S(2)}) %copy-start.3) | copy-done | bytes 40
  0.7 0.0 copy-start
  0.7 1.1 %copy-done = f32[2,19,4096]{2,0,1:T(2,128)S(1)} copy-done((f32[2,19,4096]{2,0,1:T(2,128)S(1)}, f32[2,19,4096]{2,0,1:T(2,128)}, u32[]{:S(2)}) %copy-start) | copy-done | bytes 622616
  1.7 0.0 copy-start.1
  1.7 0.8 %copy-done.1 = s32[2,4096]{1,0:T(2,128)S(1)} copy-done((s32[2,4096]{1,0:T(2,128)S(1)}, s32[2,4096]{1,0:T(2,128)}, u32[]{:S(2)}) %copy-start.1) | copy-done | bytes 32792
  2.5 1.1 %first.1 = (f32[19,64,128]{2,1,0:T(8,128)S(1)}, f32[2,64,128]{2,1,0:T(8,128)S(1)}) custom-call(s32[4]{0:T(128)S(1)} %copy-done.3, f32[19,64,128]{2,1,0:T(8,128)S(1)} %bitcast.16, s32[64,128]{1,0:T(8,128)S(1)} %bitcast.17), custom_call_target="tpu_custom_call" | custom-call | tf_op jit(solution)/shard_map/first/pallas_call | solution.py:378
  3.6 0.1 collective-permute-start.2
  3.6 1.4 %collective-permute-start.1 = (f32[2,64,128]{2,1,0:T(8,128)S(1)}, f32[2,64,128]{2,1,0:T(8,128)S(1)}, u32[]{:S(2)}, u32[]{:S(2)}) collective-permute-start(f32[2,64,128]{2,1,0:T(8,128)S(1)} %get-tuple-element.10), channel_id=1, source_target_pairs={{0,16},{1,17},{2,18},{3,19},{4,20},{5,21},{6,22},{7,23},{8,24},{9,... | collective-permute-start | bytes 196616 | tf_op jit(solution)/shard_map/ppermute | solution.py:341
  5.1 1.2 %collective-permute-start = (f32[2,64,128]{2,1,0:T(8,128)S(1)}, f32[2,64,128]{2,1,0:T(8,128)S(1)}, u32[]{:S(2)}, u32[]{:S(2)}) collective-permute-start(f32[2,64,128]{2,1,0:T(8,128)S(1)} %get-tuple-element.10), channel_id=1, source_target_pairs={{0,8},{1,9},{2,10},{3,11},{4,12},{5,13},{6,14},{7,15},{8,0},{9,1},... | collective-permute-start | bytes 196616 | tf_op jit(solution)/shard_map/ppermute | solution.py:341
  6.3 2.3 %collective-permute-done = f32[2,64,128]{2,1,0:T(8,128)S(1)} collective-permute-done((f32[2,64,128]{2,1,0:T(8,128)S(1)}, f32[2,64,128]{2,1,0:T(8,128)S(1)}, u32[]{:S(2)}, u32[]{:S(2)}) %collective-permute-start) | collective-permute-done | bytes 65568 | tf_op jit(solution)/shard_map/ppermute | solution.py:341
  8.6 0.0 collective-permute-done.1
  8.6 0.0 collective-permute-done.2
  8.6 0.0 copy-start.2
  8.7 5.1 %collective-permute-start.4 = (f32[8,64,128]{2,1,0:T(8,128)S(1)}, f32[8,64,128]{2,1,0:T(8,128)S(1)}, u32[]{:S(2)}, u32[]{:S(2)}) collective-permute-start(f32[8,64,128]{2,1,0:T(8,128)S(1)} %constant_dynamic-update-slice_fusion.own), channel_id=1, source_target_pairs={{1,2},{2,1},{3,4},{4,3},{5,6},{6,5},{9,10},{10,9},{11,12},{12,11},... | collective-permute-start | bytes 786440 | tf_op jit(solution)/shard_map/ppermute | solution.py:341
  13.7 0.1 collective-permute-start.3
  13.8 4.1 %collective-permute-done.4.far = f32[8,64,128]{2,1,0:T(8,128)S(1)} collective-permute-done((f32[8,64,128]{2,1,0:T(8,128)S(1)}, f32[8,64,128]{2,1,0:T(8,128)S(1)}, u32[]{:S(2)}, u32[]{:S(2)}) %collective-permute-start.4) | collective-permute-done | bytes 262176 | tf_op jit(solution)/shard_map/ppermute | solution.py:341
  17.9 0.0 collective-permute-done.3.chip
  17.9 0.0 copy-start.4
  17.9 0.0 copy-done.2
  17.9 0.7 %copy-done.4 = s32[2,18]{1,0:T(2,128)S(1)} copy-done((s32[2,18]{1,0:T(2,128)S(1)}, s32[2,18]{1,0:T(2,128)}, u32[]{:S(2)}) %copy-start.4) | copy-done | bytes 168
  18.6 3.3 %middle.1 = (f32[19,64,128]{2,1,0:T(8,128)S(1)}, f32[2,64,128]{2,1,0:T(8,128)S(1)}) custom-call(s32[4]{0:T(128)S(1)} %copy-done.3, s32[2,18]{1,0:T(2,128)S(1)} %copy-done.4, s32[2,4,6]{2,1,0:T(4,128)S(1)} %bitcast.20, f32[19,64,128]{2,1,0:T(8,128)S(1)} %get-tuple-element.9.star, s32[64,128]{1,0:T(8,128)S(1)} %bitcast.18, ...), custom_call_target="tpu_custom_call" | custom-call | tf_op jit(solution)/shard_map/middle/pallas_call | solution.py:393
  21.9 0.1 collective-permute-start.7
  22.0 2.1 %collective-permute-start.6 = (f32[2,64,128]{2,1,0:T(8,128)S(1)}, f32[2,64,128]{2,1,0:T(8,128)S(1)}, u32[]{:S(2)}, u32[]{:S(2)}) collective-permute-start(f32[2,64,128]{2,1,0:T(8,128)S(1)} %get-tuple-element.12), channel_id=1, source_target_pairs={{0,16},{1,17},{2,18},{3,19},{4,20},{5,21},{6,22},{7,23},{8,24},{9,... | collective-permute-start | bytes 196616 | tf_op jit(solution)/shard_map/ppermute | solution.py:341
  24.1 0.5 %collective-permute-start.5 = (f32[2,64,128]{2,1,0:T(8,128)S(1)}, f32[2,64,128]{2,1,0:T(8,128)S(1)}, u32[]{:S(2)}, u32[]{:S(2)}) collective-permute-start(f32[2,64,128]{2,1,0:T(8,128)S(1)} %get-tuple-element.12), channel_id=1, source_target_pairs={{0,8},{1,9},{2,10},{3,11},{4,12},{5,13},{6,14},{7,15},{8,0},{9,1},... | collective-permute-start | bytes 196616 | tf_op jit(solution)/shard_map/ppermute | solution.py:341
  24.7 2.9 %collective-permute-done.5 = f32[2,64,128]{2,1,0:T(8,128)S(1)} collective-permute-done((f32[2,64,128]{2,1,0:T(8,128)S(1)}, f32[2,64,128]{2,1,0:T(8,128)S(1)}, u32[]{:S(2)}, u32[]{:S(2)}) %collective-permute-start.5) | collective-permute-done | bytes 65568 | tf_op jit(solution)/shard_map/ppermute | solution.py:341
  27.6 0.3 collective-permute-done.6
  27.9 0.0 collective-permute-done.7
  27.9 5.1 %collective-permute-start.9 = (f32[8,64,128]{2,1,0:T(8,128)S(1)}, f32[8,64,128]{2,1,0:T(8,128)S(1)}, u32[]{:S(2)}, u32[]{:S(2)}) collective-permute-start(f32[8,64,128]{2,1,0:T(8,128)S(1)} %constant_dynamic-update-slice_fusion.4.own), channel_id=1, source_target_pairs={{1,2},{2,1},{3,4},{4,3},{5,6},{6,5},{9,10},{10,9},{11,12},{12,11},... | collective-permute-start | bytes 786440 | tf_op jit(solution)/shard_map/ppermute | solution.py:341
  33.0 0.1 collective-permute-start.8
  33.1 4.0 %collective-permute-done.9.far = f32[8,64,128]{2,1,0:T(8,128)S(1)} collective-permute-done((f32[8,64,128]{2,1,0:T(8,128)S(1)}, f32[8,64,128]{2,1,0:T(8,128)S(1)}, u32[]{:S(2)}, u32[]{:S(2)}) %collective-permute-start.9) | collective-permute-done | bytes 262176 | tf_op jit(solution)/shard_map/ppermute | solution.py:341
  37.0 0.0 collective-permute-done.8.chip
  37.0 3.6 %last.1 = f32[19,64,128]{2,1,0:T(8,128)} custom-call(s32[4]{0:T(128)S(1)} %copy-done.3, s32[2,18]{1,0:T(2,128)S(1)} %copy-done.4, s32[2,4,6]{2,1,0:T(4,128)S(1)} %bitcast.21, f32[19,64,128]{2,1,0:T(8,128)S(1)} %get-tuple-element.11.star, s32[64,128]{1,0:T(8,128)S(1)} %bitcast.19, f32[8,64,128]{2,1,0:T(8,128)S(1)} %constant_dynamic-update-slice_fusion.4.own, ...), custom_call_target="tpu_custom_call" | custom-call | tf_op jit(solution)/shard_map/last/pallas_call | solution.py:393
  (8 shorter events, 0.0 us)
Async XLA Ops:
  0.0 0.7 %copy-start.3 = (s32[4]{0:T(128)S(1)}, s32[4]{0:T(128)}, u32[]{:S(2)}) copy-start(s32[4]{0:T(128)} %level_ref.5) | copy-start | bytes 52
  0.7 1.1 %copy-start = (f32[2,19,4096]{2,0,1:T(2,128)S(1)}, f32[2,19,4096]{2,0,1:T(2,128)}, u32[]{:S(2)}) copy-start(f32[2,19,4096]{2,0,1:T(2,128)} %param.5) | copy-start | bytes 1867780
  1.7 0.8 %copy-start.1 = (s32[2,4096]{1,0:T(2,128)S(1)}, s32[2,4096]{1,0:T(2,128)}, u32[]{:S(2)}) copy-start(s32[2,4096]{1,0:T(2,128)} %param.6) | copy-start | bytes 98308
  3.6 5.1 %collective-permute-start.2 = (f32[2,64,128]{2,1,0:T(8,128)S(1)}, f32[2,64,128]{2,1,0:T(8,128)S(1)}, u32[]{:S(2)}, u32[]{:S(2)}) collective-permute-start(f32[2,64,128]{2,1,0:T(8,128)S(1)} %get-tuple-element.10), channel_id=1, source_target_pairs={{0,24},{1,25},{2,26},{3,27},{4,28},{5,29},{6,30},{7,31},{8,16},{9,... | collective-permute-start | bytes 196616 | tf_op jit(solution)/shard_map/ppermute | solution.py:341
  3.6 5.0 %collective-permute-start.1 = (f32[2,64,128]{2,1,0:T(8,128)S(1)}, f32[2,64,128]{2,1,0:T(8,128)S(1)}, u32[]{:S(2)}, u32[]{:S(2)}) collective-permute-start(f32[2,64,128]{2,1,0:T(8,128)S(1)} %get-tuple-element.10), channel_id=1, source_target_pairs={{0,16},{1,17},{2,18},{3,19},{4,20},{5,21},{6,22},{7,23},{8,24},{9,... | collective-permute-start | bytes 196616 | tf_op jit(solution)/shard_map/ppermute | solution.py:341
  5.1 3.5 %collective-permute-start = (f32[2,64,128]{2,1,0:T(8,128)S(1)}, f32[2,64,128]{2,1,0:T(8,128)S(1)}, u32[]{:S(2)}, u32[]{:S(2)}) collective-permute-start(f32[2,64,128]{2,1,0:T(8,128)S(1)} %get-tuple-element.10), channel_id=1, source_target_pairs={{0,8},{1,9},{2,10},{3,11},{4,12},{5,13},{6,14},{7,15},{8,0},{9,1},... | collective-permute-start | bytes 196616 | tf_op jit(solution)/shard_map/ppermute | solution.py:341
  8.6 9.3 %copy-start.2 = (s32[2,6,4]{1,2,0:T(4,128)S(1)}, s32[2,6,4]{1,2,0:T(4,128)}, u32[]{:S(2)}) copy-start(s32[2,6,4]{1,2,0:T(4,128)} %param.9) | copy-start | bytes 580
  8.7 9.3 %collective-permute-start.4 = (f32[8,64,128]{2,1,0:T(8,128)S(1)}, f32[8,64,128]{2,1,0:T(8,128)S(1)}, u32[]{:S(2)}, u32[]{:S(2)}) collective-permute-start(f32[8,64,128]{2,1,0:T(8,128)S(1)} %constant_dynamic-update-slice_fusion.own), channel_id=1, source_target_pairs={{1,2},{2,1},{3,4},{4,3},{5,6},{6,5},{9,10},{10,9},{11,12},{12,11},... | collective-permute-start | bytes 786440 | tf_op jit(solution)/shard_map/ppermute | solution.py:341
  13.7 4.2 %collective-permute-start.3 = (f32[8,64,128]{2,1,0:T(8,128)S(1)}, f32[8,64,128]{2,1,0:T(8,128)S(1)}, u32[]{:S(2)}, u32[]{:S(2)}) collective-permute-start(f32[8,64,128]{2,1,0:T(8,128)S(1)} %constant_dynamic-update-slice_fusion.own), channel_id=1, source_target_pairs={{0,1},{1,0},{2,3},{3,2},{4,5},{5,4},{6,7},{7,6},{8,9},{9,8},{10,11... | collective-permute-start | bytes 786440 | tf_op jit(solution)/shard_map/ppermute | solution.py:341
  17.9 0.7 %copy-start.4 = (s32[2,18]{1,0:T(2,128)S(1)}, s32[2,18]{1,0:T(2,128)}, u32[]{:S(2)}) copy-start(s32[2,18]{1,0:T(2,128)} %near_ref.3) | copy-start | bytes 436
  21.9 5.9 %collective-permute-start.7 = (f32[2,64,128]{2,1,0:T(8,128)S(1)}, f32[2,64,128]{2,1,0:T(8,128)S(1)}, u32[]{:S(2)}, u32[]{:S(2)}) collective-permute-start(f32[2,64,128]{2,1,0:T(8,128)S(1)} %get-tuple-element.12), channel_id=1, source_target_pairs={{0,24},{1,25},{2,26},{3,27},{4,28},{5,29},{6,30},{7,31},{8,16},{9,... | collective-permute-start | bytes 196616 | tf_op jit(solution)/shard_map/ppermute | solution.py:341
  22.0 5.8 %collective-permute-start.6 = (f32[2,64,128]{2,1,0:T(8,128)S(1)}, f32[2,64,128]{2,1,0:T(8,128)S(1)}, u32[]{:S(2)}, u32[]{:S(2)}) collective-permute-start(f32[2,64,128]{2,1,0:T(8,128)S(1)} %get-tuple-element.12), channel_id=1, source_target_pairs={{0,16},{1,17},{2,18},{3,19},{4,20},{5,21},{6,22},{7,23},{8,24},{9,... | collective-permute-start | bytes 196616 | tf_op jit(solution)/shard_map/ppermute | solution.py:341
  24.1 3.4 %collective-permute-start.5 = (f32[2,64,128]{2,1,0:T(8,128)S(1)}, f32[2,64,128]{2,1,0:T(8,128)S(1)}, u32[]{:S(2)}, u32[]{:S(2)}) collective-permute-start(f32[2,64,128]{2,1,0:T(8,128)S(1)} %get-tuple-element.12), channel_id=1, source_target_pairs={{0,8},{1,9},{2,10},{3,11},{4,12},{5,13},{6,14},{7,15},{8,0},{9,1},... | collective-permute-start | bytes 196616 | tf_op jit(solution)/shard_map/ppermute | solution.py:341
  27.9 9.1 %collective-permute-start.9 = (f32[8,64,128]{2,1,0:T(8,128)S(1)}, f32[8,64,128]{2,1,0:T(8,128)S(1)}, u32[]{:S(2)}, u32[]{:S(2)}) collective-permute-start(f32[8,64,128]{2,1,0:T(8,128)S(1)} %constant_dynamic-update-slice_fusion.4.own), channel_id=1, source_target_pairs={{1,2},{2,1},{3,4},{4,3},{5,6},{6,5},{9,10},{10,9},{11,12},{12,11},... | collective-permute-start | bytes 786440 | tf_op jit(solution)/shard_map/ppermute | solution.py:341
  33.0 4.0 %collective-permute-start.8 = (f32[8,64,128]{2,1,0:T(8,128)S(1)}, f32[8,64,128]{2,1,0:T(8,128)S(1)}, u32[]{:S(2)}, u32[]{:S(2)}) collective-permute-start(f32[8,64,128]{2,1,0:T(8,128)S(1)} %constant_dynamic-update-slice_fusion.4.own), channel_id=1, source_target_pairs={{0,1},{1,0},{2,3},{3,2},{4,5},{5,4},{6,7},{7,6},{8,9},{9,8},{10,11... | collective-permute-start | bytes 786440 | tf_op jit(solution)/shard_map/ppermute | solution.py:341
where the time goes:
time: 40.8 us; the launch traced here: 40.7 us
  starting transfers between devices  15.7 us (38%)
  waiting for transfers between devices  13.6 us (33%)
  Pallas kernels  8.02 us (20%)
  local copies, waits for them, and re-layouts  3.22 us (8%)
    ppermute x10, starting transfers between devices, swap(): return lax.ppermute(x, ('section', 'member'), pairs)  15.7 us
    ppermute x10, waiting for transfers between devices, swap(): return lax.ppermute(x, ('section', 'member'), pairs)  13.6 us
    pallas_call x2, Pallas kernels, body(): pl.pallas_call(functools.partial(next_kernel, sizes, last), out_shape=(fi...  6.95 us
    unnamed x16, local copies, waits for them, and re-layouts  3.2 us
    pallas_call x1, Pallas kernels, body(): pl.pallas_call(functools.partial(first_kernel, sizes), out_shape=(field,...  1.07 us
  transfers between devices with their start and end apart: 10, of which 5 were waited for; matrix products, arithmetic and copies ran while one was open for 0% of the time, Pallas kernels for 0%

commit v1 on v0

v1 whole, which is shorter than its diff:
```python
import functools

import jax
import jax.numpy as jnp
from jax import lax
from jax.experimental import pallas as pl
from jax.experimental.pallas import tpu as pltpu
from jax.sharding import PartitionSpec as P

VELOCITIES = (
    (0, 0, 0), (1, 0, 0), (-1, 0, 0), (0, 1, 0), (0, -1, 0), (0, 0, 1), (0, 0, -1),
    (1, 1, 0), (-1, -1, 0), (1, -1, 0), (-1, 1, 0), (1, 0, 1), (-1, 0, -1), (1, 0, -1),
    (-1, 0, 1), (0, 1, 1), (0, -1, -1), (0, 1, -1), (0, -1, 1),
)
WEIGHTS = (1.0 / 3.0,) + (1.0 / 18.0,) * 6 + (1.0 / 36.0,) * 12
OPPOSITE = (0, 2, 1, 4, 3, 6, 5, 8, 7, 10, 9, 12, 11, 14, 13, 16, 15, 18, 17)
LISTS = [
    [q for q in range(19) if sum(a * b for a, b in zip(VELOCITIES[q], VELOCITIES[1 + j])) == 1]
    for j in range(6)
]
ROWS = 64
TILES = 8


def iotas():
    sub = lax.broadcasted_iota(jnp.int32, (8, 128), 0)
    lane = lax.broadcasted_iota(jnp.int32, (8, 128), 1)
    return sub, lane


def pick(x, index):
    return jnp.take_along_axis(x, index, axis=1, mode="promise_in_bounds")


def lanes(x, shift):
    return pltpu.roll(x, shift % 128, 1)


def subs(x, shift):
    return pltpu.roll(x, shift % 8, 0)


def tile(ref, q, t):
    return ref[q, 8 * t : 8 * t + 8, :]


def bulk(ref, row):
    return jnp.broadcast_to(ref[row : row + 1, :], (8, 128))


def relax_rate(level):
    return jnp.where(
        level == 0, jnp.float32(1.0 / 0.55), jnp.where(level == 1, jnp.float32(1.0 / 0.6), jnp.float32(1.0 / 0.7))
    )


def collide(src, dst, mask, rate, ready):
    for t in range(TILES):
        ready(t)
        f = [tile(src, q, t) for q in range(19)]
        density = f[0]
        for q in range(1, 19):
            density = density + f[q]
        velocity = []
        for a in range(3):
            plus = [q for q in range(19) if VELOCITIES[q][a] > 0]
            total = f[plus[0]] - f[OPPOSITE[plus[0]]]
            for q in plus[1:]:
                total = total + (f[q] - f[OPPOSITE[q]])
            velocity.append(total / density)
        speed = velocity[0] * velocity[0] + velocity[1] * velocity[1] + velocity[2] * velocity[2]
        base = 1.0 - 1.5 * speed
        fluid = mask[8 * t : 8 * t + 8, :] == 1
        keep = 1.0 - rate
        scaled = [rate * jnp.float32(w) * density for w in (WEIGHTS[0], WEIGHTS[1], WEIGHTS[7])]
        out = keep * f[0] + scaled[0] * base
        dst[0, 8 * t : 8 * t + 8, :] = jnp.where(fluid, out, f[0])
        for q in range(1, 19, 2):
            o = OPPOSITE[q]
            along = None
            for a in range(3):
                c = VELOCITIES[q][a]
                if c:
                    term = velocity[a] if c > 0 else -velocity[a]
                    along = term if along is None else along + term
            weight = scaled[1] if q < 7 else scaled[2]
            even = base + 4.5 * along * along
            odd = 3.0 * along
            dst[q, 8 * t : 8 * t + 8, :] = jnp.where(fluid, keep * f[q] + weight * (even + odd), f[o])
            dst[o, 8 * t : 8 * t + 8, :] = jnp.where(fluid, keep * f[o] + weight * (even - odd), f[q])


def export(src, out):
    sub, lane = iotas()
    xl, yh = sub // 4, (sub // 2) % 2
    for j in range(6):
        axis, high = j // 2, j % 2 == 0
        for i, q in enumerate(LISTS[j]):
            if axis == 0:
                v = tile(src, q, TILES - 1 if high else 0)
                first = 4 if high else 0
                for h in range(2):
                    for b in range(2):
                        s = first + 2 * h + b
                        r = 10 * j + 5 * h + i
                        out[b, r : r + 1, :] = v[s : s + 1, :]
                continue
            for h in range(2):
                total = jnp.zeros((8, 128), jnp.float32)
                for k in range(4):
                    if axis == 1:
                        index = (lane & 15) + (112 if high else 0)
                        here = (lane >> 4 == 2 * k + xl) & (yh == (1 if high else 0))
                    else:
                        index = (lane & 7) * 16 + (15 if high else 0)
                        here = lane >> 3 == (2 * k + xl) * 2 + yh
                    total = jnp.where(here, pick(tile(src, q, 4 * h + k), index), total)
                total = total + subs(total, 4)
                total = total + subs(total, 2)
                for b in range(2):
                    r = 10 * j + 5 * h + i
                    out[b, r : r + 1, :] = total[b : b + 1, :]


def divide(x, n):
    return x >> (n.bit_length() - 1) if n & (n - 1) == 0 else lax.div(x, jnp.int32(n))


def plan_rows(level_ref, near_ref, link_ref, plan, me, sizes):
    sections, members, blocks = sizes
    level = level_ref[me[0]]
    chip = jnp.where(me[1] % 2 == 0, 1, -1)

    def placed(ids):
        safe = jnp.maximum(ids, 0)
        local = divide(safe, blocks)
        within = safe - local * blocks
        section = divide(local, members)
        offset = local - section * members - me[1]
        which = jnp.where(offset == 0, 0, jnp.where(offset == chip, 1, 2))
        if sections & (sections - 1) == 0:
            apart = section ^ me[0]
        else:
            apart = me[0] - section
            apart = jnp.where(apart < 0, apart + sections, apart)
        one = (which * sections + apart) * blocks + within
        two = jnp.maximum((which * (sections - 1) + section - 1) * blocks + within, 0)
        source = jnp.zeros_like(ids)
        for s in range(sections):
            source = jnp.where(section == s, level_ref[s], source)
        return (one, two), source

    plan[0:1, 64:65] = jnp.full((1, 1), level, jnp.int32)
    for block in range(blocks):
        near = near_ref[block : block + 1, :]
        near_slots, _ = placed(near)
        links = link_ref[block]
        link_slots, source = placed(links)
        coarse = (links >= 0) & (source < level)
        fine = (links >= 0) & (source >= level)
        place = lax.broadcasted_iota(jnp.int32, links.shape, 0)
        quadrant = jnp.max(jnp.where(coarse, place, -1), axis=0, keepdims=True)
        any_fine = jnp.max(jnp.where(fine, 1, 0), axis=0, keepdims=True)
        kind = jnp.where(quadrant >= 0, 1, jnp.where(any_fine > 0, 2, 3))
        kind = jnp.where(near[:, :6] >= 0, 0, kind)
        for r in range(2):
            first = 32 * r
            plan[block : block + 1, first : first + 18] = jnp.where(near >= 0, near_slots[r], -1)
            plan[2 + 4 * block : 6 + 4 * block, first : first + 6] = jnp.where(fine, link_slots[r], -1)
            chosen = jnp.max(jnp.where(coarse, link_slots[r], -1), axis=0, keepdims=True)
            plan[10 + block : 11 + block, first : first + 6] = chosen
            plan[12 + block : 13 + block, first : first + 6] = kind
            plan[14 + block : 15 + block, first : first + 6] = quadrant


def arrived(plan, base, table, halo, blocks):
    sub, lane = iotas()
    sub, lane = sub[:5], lane[:5]
    for block in range(blocks):
        for j in range(6):
            first = 10 * (j ^ 1)
            kind = plan[12 + block, base + j]

            def rows(slot, part):
                return table[slot, first + 5 * part : first + 5 * part + 5, :]

            @pl.when(kind == 0)
            def _():
                halo[block, 10 * j : 10 * j + 10, :] = table[plan[block, base + j], first : first + 10, :]

            @pl.when(kind == 1)
            def _():
                slot = plan[10 + block, base + j]
                quadrant = plan[14 + block, base + j]
                low = jnp.full((5, 128), quadrant, jnp.int32) < 2
                source = jnp.where(low, rows(slot, 0), rows(slot, 1))
                shift = 8 * (quadrant & 1)
                for h in range(2):
                    index = (4 * h + (lane >> 5)) * 16 + shift + ((lane & 15) >> 1)
                    halo[block, 10 * j + 5 * h : 10 * j + 5 * h + 5, :] = pick(source, index)

            @pl.when(kind == 2)
            def _():
                index = ((lane >> 4) & 3) * 32 + 2 * (lane & 7)
                quads = []
                for k in range(4):
                    slot = plan[2 + 4 * block + k, base + j]
                    scale = jnp.where(slot >= 0, jnp.float32(0.25), jnp.float32(0.0))
                    slot = jnp.maximum(slot, 0)
                    parts = []
                    for h in range(2):
                        v = rows(slot, h)
                        v = v + lanes(v, -1)
                        v = v + lanes(v, -16)
                        parts.append(pick(v, index))
                    quads.append(jnp.where(lane >= 64, parts[1], parts[0]) * scale)
                for a in range(2):
                    halo[block, 10 * j + 5 * a : 10 * j + 5 * a + 5, :] = jnp.where(
                        lane & 8 == 0, quads[2 * a], quads[2 * a + 1]
                    )

            @pl.when(kind == 3)
            def _():
                rest = [WEIGHTS[q] for q in LISTS[j ^ 1]]
                straight = rest.index(WEIGHTS[1])
                value = jnp.where(sub == straight, jnp.float32(WEIGHTS[1]), jnp.float32(WEIGHTS[7]))
                halo[block, 10 * j : 10 * j + 5, :] = value
                halo[block, 10 * j + 5 : 10 * j + 10, :] = value


def stream(src, dst, plan, base, table, halo, blocks, done):
    sub, lane = iotas()
    odd = (sub & 1) == 1
    xl, yh = sub // 4, (sub // 2) % 2
    z = lane & 15
    starts = [(2 * k + xl) * 16 for k in range(4)]

    def plane(j, i, h):
        return jnp.where(odd, bulk(halo.at[1], 10 * j + 5 * h + i), bulk(halo.at[0], 10 * j + 5 * h + i))

    for q in range(19):
        c = VELOCITIES[q]
        moving = [a for a in range(3) if c[a]]
        values = [tile(src, q, t) for t in range(TILES)]
        planes = {}
        for a in moving:
            j = 2 * a + (0 if c[a] < 0 else 1)
            i = LISTS[j ^ 1].index(q)
            planes[a] = [plane(j, i, h) for h in range(2)]
        line = None
        if len(moving) == 2:
            e = VELOCITIES.index(tuple(-v for v in c)) - 1
            j = 2 * moving[0] + (0 if c[moving[0]] > 0 else 1)
            i = LISTS[j].index(q)
            found = []
            for block in range(blocks):
                slot = plan[block, base + e]
                good = jnp.full((8, 128), slot, jnp.int32) >= 0
                slot = jnp.maximum(slot, 0)
                found.append(
                    [jnp.where(good, bulk(table.at[slot], 10 * j + 5 * h + i), jnp.float32(WEIGHTS[q])) for h in range(2)]
                )
            line = [jnp.where(odd, found[1][h], found[0][h]) for h in range(2)]
        outside = jnp.where(yh == 1, planes[0][1], planes[0][0]) if c[0] else None

        if c[2]:
            up = c[2] > 0
            edge = z == (0 if up else 15)
            values = [
                jnp.where(edge, pick(planes[2][t // 4], starts[t % 4] + yh * 8 + (lane >> 4)), lanes(v, c[2]))
                for t, v in enumerate(values)
            ]
            if c[0]:
                spread = jnp.where(yh == 1, line[1], line[0])
                outside = jnp.where(edge, lanes(spread, -15 if up else 15), lanes(outside, c[2]))
        if c[1]:
            up = c[1] > 0
            edge = lane < 16 if up else lane >= 112
            inner = yh == (1 if up else 0)

            def moved(v, border):
                rolled = lanes(v, 16 * c[1])
                return jnp.where(edge, jnp.where(inner, subs(rolled, 2 * c[1]), border), rolled)

            for t in range(TILES):
                start, source = starts[t % 4], planes[1][t // 4]
                if c[2]:
                    if c[2] > 0:
                        border = jnp.where(z == 0, pick(line[t // 4], start + 15), pick(source, start + jnp.maximum(z - 1, 0)))
                    else:
                        border = jnp.where(z == 15, pick(line[t // 4], start), pick(source, start + jnp.minimum(z + 1, 15)))
                else:
                    border = pick(source, start + z)
                values[t] = moved(values[t], border)
            if c[0]:
                outside = moved(outside, lanes(line[1 if up else 0], 16 * c[1]))
        if c[0]:
            rolled = [subs(v, 4) for v in values]
            if c[0] > 0:
                values = [jnp.where(sub < 4, rolled[t - 1] if t else outside, rolled[t]) for t in range(TILES)]
            else:
                values = [
                    jnp.where(sub >= 4, rolled[t + 1] if t < TILES - 1 else outside, rolled[t]) for t in range(TILES)
                ]
        for t in range(TILES):
            dst[q, 8 * t : 8 * t + 8, :] = values[t]
        done(q)


def nothing(_):
    pass


def first_kernel(sizes, level_hbm, near_hbm, link_hbm, pops_hbm, mask_hbm, star, out, plan, mask, level_ref, near, links, pops, sems):
    me = (lax.axis_index("section"), lax.axis_index("member"))
    small = [
        pltpu.make_async_copy(level_hbm, level_ref, sems.at[TILES]),
        pltpu.make_async_copy(near_hbm, near, sems.at[TILES + 1]),
        pltpu.make_async_copy(link_hbm, links, sems.at[TILES + 2]),
        pltpu.make_async_copy(mask_hbm, mask, sems.at[TILES + 3]),
    ]
    parts = [
        pltpu.make_async_copy(pops_hbm.at[:, 8 * t : 8 * t + 8, :], pops.at[:, 8 * t : 8 * t + 8, :], sems.at[t])
        for t in range(TILES)
    ]
    for copy in small + parts:
        copy.start()
    for copy in small:
        copy.wait()
    level = level_ref[me[0]]
    plan_rows(level_ref, near, links, plan, me, sizes)

    @pl.when(level >= 1)
    def _():
        collide(pops, star, mask, relax_rate(level), lambda t: parts[t].wait())

    @pl.when(level < 1)
    def _():
        for t in range(TILES):
            parts[t].wait()
        star[...] = pops[...]

    export(star, out)


def gathered(plan_ref, plan, sem, parts, table):
    copy = pltpu.make_async_copy(plan_ref, plan, sem)
    copy.start()
    for i, part in enumerate(parts):
        for k in range(part.shape[0]):
            table[part.shape[0] * i + k] = part[k]
    copy.wait()


def middle_kernel(sizes, plan_ref, star, mask, own, chip, far, dst, out, plan, table, halo, sems):
    gathered(plan_ref, plan, sems.at[0], (own, chip, far), table)
    level = plan[0, 64]

    @pl.when(level >= 1)
    def _():
        arrived(plan, 0, table, halo, sizes[2])
        stream(star, dst, plan, 0, table, halo, sizes[2], nothing)

    @pl.when(level < 1)
    def _():
        dst[...] = star[...]

    @pl.when(level == 2)
    def _():
        collide(dst, dst, mask, relax_rate(level), nothing)

    export(dst, out)


def last_kernel(sizes, plan_ref, star, own, chip, far, result, plan, table, halo, moved, sems):
    gathered(plan_ref, plan, sems.at[19], (own, chip, far), table)
    level = plan[0, 64]

    @pl.when(level == 2)
    def _():
        copies = [pltpu.make_async_copy(moved.at[q], result.at[q], sems.at[q]) for q in range(19)]
        arrived(plan, 32, table, halo, sizes[2])
        stream(star, moved, plan, 32, table, halo, sizes[2], lambda q: copies[q].start())
        for copy in copies:
            copy.wait()

    @pl.when(level < 2)
    def _():
        copy = pltpu.make_async_copy(star, result, sems.at[0])
        copy.start()
        copy.wait()


def swap(x, sections, members, target):
    pairs = []
    for s in range(sections):
        for m in range(members):
            t = target(s, m)
            if 0 <= t[1] < members:
                pairs.append((s * members + m, t[0] * members + t[1]))
    return lax.ppermute(x, ("section", "member"), pairs)


def exchange(exports, sections, members, last):
    power = sections & (sections - 1) == 0
    me = lax.axis_index("section")

    def across(d):
        return lambda s, m: (s ^ d if power else (s + d) % sections, m)

    def beside(s, m):
        t = ((m + 1) ^ 1) - 1
        return (s, t) if 0 <= t < members or sections % 2 else (s ^ 1, m)

    parts = [swap(exports, sections, members, across(d)) for d in range(1, sections)]
    if last:
        blocks = exports.shape[0]
        own = jnp.zeros(((sections - 1) * blocks,) + exports.shape[1:], exports.dtype)
        for d, part in enumerate(parts, 1):
            source = me ^ d if power else (me + sections - d) % sections
            own = lax.dynamic_update_slice(own, part, (jnp.where(source == 0, me - 1, source - 1) * blocks, 0, 0))
        own = lax.dynamic_update_slice(own, exports, ((me - 1) * blocks, 0, 0))
    else:
        own = jnp.concatenate([exports] + parts, axis=0)
    chip = swap(own, sections, members, lambda s, m: (s, m ^ 1))
    far = swap(own, sections, members, beside)
    return own, chip, far


def packed(x):
    n, cells = x.shape[0], x.shape[-1]
    x = x.reshape(n, -1, cells // 128, 128)
    return x.transpose(1, 2, 0, 3).reshape(-1, n * cells // 128, 128)


VMEM = pl.BlockSpec(memory_space=pltpu.VMEM)
ANY = pl.BlockSpec(memory_space=pl.ANY)
HBM = pl.BlockSpec(memory_space=pltpu.HBM)


def body(populations, fluid_mask, section_level, neighbours, interface):
    sections, members = lax.axis_size("section"), lax.axis_size("member")
    blocks, _, cells = populations.shape
    sizes = (sections, members, blocks)
    params = pltpu.CompilerParams(vmem_limit_bytes=16 << 20)
    pops = packed(populations)
    mask = packed(fluid_mask)[0]
    links = interface.transpose(0, 2, 1)
    field = jax.ShapeDtypeStruct(pops.shape, jnp.float32)
    planes = jax.ShapeDtypeStruct((blocks, ROWS, 128), jnp.float32)
    plan = jax.ShapeDtypeStruct((16, 128), jnp.int32)
    plan_scratch = pltpu.SMEM((16, 128), jnp.int32)
    halo = pltpu.VMEM((blocks, ROWS, 128), jnp.float32)
    star, exports, plan, mask = pl.pallas_call(
        functools.partial(first_kernel, sizes),
        out_shape=(field, planes, plan, jax.ShapeDtypeStruct(mask.shape, jnp.int32)),
        in_specs=[HBM] * 5,
        out_specs=(VMEM,) * 4,
        scratch_shapes=[
            pltpu.SMEM(section_level.shape, jnp.int32),
            pltpu.VMEM(neighbours.shape, jnp.int32),
            pltpu.VMEM(links.shape, jnp.int32),
            pltpu.VMEM(pops.shape, jnp.float32),
            pltpu.SemaphoreType.DMA((TILES + 4,)),
        ],
        compiler_params=params,
        name="first",
    )(*(pltpu.with_memory_space_constraint(x, pltpu.HBM) for x in (section_level, neighbours, links, pops, mask)))
    own, chip, far = exchange(exports, sections, members, False)
    star, exports = pl.pallas_call(
        functools.partial(middle_kernel, sizes),
        out_shape=(field, planes),
        in_specs=[ANY] + [VMEM] * 5,
        out_specs=(VMEM, VMEM),
        scratch_shapes=[
            plan_scratch,
            pltpu.VMEM((3 * sections * blocks, ROWS, 128), jnp.float32),
            halo,
            pltpu.SemaphoreType.DMA((1,)),
        ],
        compiler_params=params,
        name="middle",
    )(plan, star, mask, own, chip, far)
    own, chip, far = exchange(exports, sections, members, True)
    result = pl.pallas_call(
        functools.partial(last_kernel, sizes),
        out_shape=field,
        in_specs=[ANY] + [VMEM] * 4,
        out_specs=HBM,
        scratch_shapes=[
            plan_scratch,
            pltpu.VMEM((3 * (sections - 1) * blocks, ROWS, 128), jnp.float32),
            halo,
            pltpu.VMEM(pops.shape, jnp.float32),
            pltpu.SemaphoreType.DMA((20,)),
        ],
        compiler_params=params,
        name="last",
    )(plan, star, own, chip, far)
    out = result.reshape(19, cells // 128, blocks, 128).transpose(2, 0, 1, 3)
    return out.reshape(blocks, 19, cells)


def solution(mesh):
    return jax.shard_map(
        body,
        mesh=mesh,
        in_specs=(
            P(("section", "member"), None, None),
            P(("section", "member"), None),
            P(),
            P(("section", "member"), None),
            P(("section", "member"), None, None),
        ),
        out_specs=P(("section", "member"), None, None),
        check_vma=False,
    )
```

time: 40.8 us -> 34.2 us (0.84)
  the two profiles are of different devices: /device:TPU:15 before, /device:TPU:0 now
where the time goes in v1:
time: 34.2 us; the launch traced here: 34 us
  waiting for transfers between devices  19.1 us (56%)
  starting transfers between devices  10.4 us (30%)
  Pallas kernels  4.27 us (12%)
    ppermute x10, waiting for transfers between devices, swap(): return lax.ppermute(x, ('section', 'member'), pairs)  19.1 us
    ppermute x10, starting transfers between devices, swap(): return lax.ppermute(x, ('section', 'member'), pairs)  10.4 us
    pallas_call x1, Pallas kernels, body(): pl.pallas_call(functools.partial(last_kernel, sizes), out_shape=field, in...  1.68 us
    pallas_call x1, Pallas kernels, body(): pl.pallas_call(functools.partial(first_kernel, sizes), out_shape=(field,...  1.61 us
    pallas_call x1, Pallas kernels, body(): pl.pallas_call(functools.partial(middle_kernel, sizes), out_shape=(field,...  0.98 us
  transfers between devices with their start and end apart: 10, of which 9 were waited for; matrix products, arithmetic and copies ran while one was open for 0% of the time, Pallas kernels for 0%

profile of v1, /device:TPU:0, one launch (start us, length us, event | category | flops | bytes accessed | tf_op | source)
XLA Modules:
  0.0 34.0 jit_solution(11648405050649827986)
XLA Ops:
  0.0 1.6 %first.1 = (f32[19,64,128]{2,1,0:T(8,128)S(1)}, f32[2,64,128]{2,1,0:T(8,128)S(1)}, s32[16,128]{1,0:T(8,128)S(1)}, s32[64,128]{1,0:T(8,128)S(1)}) custom-call(s32[4]{0:T(128)} %level_hbm.1, s32[2,18]{1,0:T(2,128)} %near_hbm.1, s32[2,4,6]{2,1,0:T(4,128)} %bitcast.18, f32[19,64,128]{2,1,0:T(8,128)} %bitcast.16, s32[64,128]{1,0:T(8,128)} %bitcast.17), custom_call_target="tpu_custom_call" | custom-call | tf_op jit(solution)/shard_map/first/pallas_call | solution.py:454
  1.6 3.0 %collective-permute-start = (f32[2,64,128]{2,1,0:T(8,128)S(1)}, f32[2,64,128]{2,1,0:T(8,128)S(1)}, u32[]{:S(2)}, u32[]{:S(2)}) collective-permute-start(f32[2,64,128]{2,1,0:T(8,128)S(1)} %get-tuple-element.14), channel_id=1, source_target_pairs={{0,8},{1,9},{2,10},{3,11},{4,12},{5,13},{6,14},{7,15},{8,0},{9,1},... | collective-permute-start | bytes 196616 | tf_op jit(solution)/shard_map/ppermute | solution.py:401
  4.6 1.6 %collective-permute-start.1 = (f32[2,64,128]{2,1,0:T(8,128)S(1)}, f32[2,64,128]{2,1,0:T(8,128)S(1)}, u32[]{:S(2)}, u32[]{:S(2)}) collective-permute-start(f32[2,64,128]{2,1,0:T(8,128)S(1)} %get-tuple-element.14), channel_id=1, source_target_pairs={{0,16},{1,17},{2,18},{3,19},{4,20},{5,21},{6,22},{7,23},{8,24},{9,... | collective-permute-start | bytes 196616 | tf_op jit(solution)/shard_map/ppermute | solution.py:401
  6.3 0.0 collective-permute-start.2
  6.3 0.7 %collective-permute-done = f32[2,64,128]{2,1,0:T(8,128)S(1)} collective-permute-done((f32[2,64,128]{2,1,0:T(8,128)S(1)}, f32[2,64,128]{2,1,0:T(8,128)S(1)}, u32[]{:S(2)}, u32[]{:S(2)}) %collective-permute-start) | collective-permute-done | bytes 65568 | tf_op jit(solution)/shard_map/ppermute | solution.py:401
  6.9 2.0 %collective-permute-done.1 = f32[2,64,128]{2,1,0:T(8,128)S(1)} collective-permute-done((f32[2,64,128]{2,1,0:T(8,128)S(1)}, f32[2,64,128]{2,1,0:T(8,128)S(1)}, u32[]{:S(2)}, u32[]{:S(2)}) %collective-permute-start.1) | collective-permute-done | bytes 65568 | tf_op jit(solution)/shard_map/ppermute | solution.py:401
  8.9 2.5 %collective-permute-done.2 = f32[2,64,128]{2,1,0:T(8,128)S(1)} collective-permute-done((f32[2,64,128]{2,1,0:T(8,128)S(1)}, f32[2,64,128]{2,1,0:T(8,128)S(1)}, u32[]{:S(2)}, u32[]{:S(2)}) %collective-permute-start.2) | collective-permute-done | bytes 65568 | tf_op jit(solution)/shard_map/ppermute | solution.py:401
  11.4 0.0 collective-permute-start.3
  11.4 0.6 %collective-permute-start.4 = (f32[8,64,128]{2,1,0:T(8,128)S(1)}, f32[8,64,128]{2,1,0:T(8,128)S(1)}, u32[]{:S(2)}, u32[]{:S(2)}) collective-permute-start(f32[8,64,128]{2,1,0:T(8,128)S(1)} %constant_dynamic-update-slice_fusion.own), channel_id=1, source_target_pairs={{0,8},{1,2},{2,1},{3,4},{4,3},{5,6},{6,5},{7,15},{8,0},{9,10},{10,... | collective-permute-start | bytes 786440 | tf_op jit(solution)/shard_map/ppermute | solution.py:401
  12.0 0.9 %collective-permute-done.3.chip = f32[8,64,128]{2,1,0:T(8,128)S(1)} collective-permute-done((f32[8,64,128]{2,1,0:T(8,128)S(1)}, f32[8,64,128]{2,1,0:T(8,128)S(1)}, u32[]{:S(2)}, u32[]{:S(2)}) %collective-permute-start.3) | collective-permute-done | bytes 262176 | tf_op jit(solution)/shard_map/ppermute | solution.py:401
  13.0 4.9 %collective-permute-done.4.far = f32[8,64,128]{2,1,0:T(8,128)S(1)} collective-permute-done((f32[8,64,128]{2,1,0:T(8,128)S(1)}, f32[8,64,128]{2,1,0:T(8,128)S(1)}, u32[]{:S(2)}, u32[]{:S(2)}) %collective-permute-start.4) | collective-permute-done | bytes 262176 | tf_op jit(solution)/shard_map/ppermute | solution.py:401
  17.9 1.0 %middle.1 = (f32[19,64,128]{2,1,0:T(8,128)S(1)}, f32[2,64,128]{2,1,0:T(8,128)S(1)}) custom-call(s32[16,128]{1,0:T(8,128)S(1)} %get-tuple-element.11.plan_ref, f32[19,64,128]{2,1,0:T(8,128)S(1)} %get-tuple-element.12.star, s32[64,128]{1,0:T(8,128)S(1)} %get-tuple-element.13.mask, f32[8,64,128]{2,1,0:T(8,128)S(1)} %constant_dynamic-update-slice_fusion.own, ...), custom_call_target="tpu_custom_call" | custom-call | tf_op jit(solution)/shard_map/middle/pallas_call | solution.py:470
  18.9 0.6 %collective-permute-start.5 = (f32[2,64,128]{2,1,0:T(8,128)S(1)}, f32[2,64,128]{2,1,0:T(8,128)S(1)}, u32[]{:S(2)}, u32[]{:S(2)}) collective-permute-start(f32[2,64,128]{2,1,0:T(8,128)S(1)} %get-tuple-element.16), channel_id=1, source_target_pairs={{0,8},{1,9},{2,10},{3,11},{4,12},{5,13},{6,14},{7,15},{8,0},{9,1},... | collective-permute-start | bytes 196616 | tf_op jit(solution)/shard_map/ppermute | solution.py:401
  19.5 1.8 %collective-permute-start.6 = (f32[2,64,128]{2,1,0:T(8,128)S(1)}, f32[2,64,128]{2,1,0:T(8,128)S(1)}, u32[]{:S(2)}, u32[]{:S(2)}) collective-permute-start(f32[2,64,128]{2,1,0:T(8,128)S(1)} %get-tuple-element.16), channel_id=1, source_target_pairs={{0,16},{1,17},{2,18},{3,19},{4,20},{5,21},{6,22},{7,23},{8,24},{9,... | collective-permute-start | bytes 196616 | tf_op jit(solution)/shard_map/ppermute | solution.py:401
  21.3 1.1 %collective-permute-start.7 = (f32[2,64,128]{2,1,0:T(8,128)S(1)}, f32[2,64,128]{2,1,0:T(8,128)S(1)}, u32[]{:S(2)}, u32[]{:S(2)}) collective-permute-start(f32[2,64,128]{2,1,0:T(8,128)S(1)} %get-tuple-element.16), channel_id=1, source_target_pairs={{0,24},{1,25},{2,26},{3,27},{4,28},{5,29},{6,30},{7,31},{8,16},{9,... | collective-permute-start | bytes 196616 | tf_op jit(solution)/shard_map/ppermute | solution.py:401
  22.4 0.8 %collective-permute-done.5 = f32[2,64,128]{2,1,0:T(8,128)S(1)} collective-permute-done((f32[2,64,128]{2,1,0:T(8,128)S(1)}, f32[2,64,128]{2,1,0:T(8,128)S(1)}, u32[]{:S(2)}, u32[]{:S(2)}) %collective-permute-start.5) | collective-permute-done | bytes 65568 | tf_op jit(solution)/shard_map/ppermute | solution.py:401
  23.2 0.5 %collective-permute-done.6 = f32[2,64,128]{2,1,0:T(8,128)S(1)} collective-permute-done((f32[2,64,128]{2,1,0:T(8,128)S(1)}, f32[2,64,128]{2,1,0:T(8,128)S(1)}, u32[]{:S(2)}, u32[]{:S(2)}) %collective-permute-start.6) | collective-permute-done | bytes 65568 | tf_op jit(solution)/shard_map/ppermute | solution.py:401
  23.7 2.7 %collective-permute-done.7 = f32[2,64,128]{2,1,0:T(8,128)S(1)} collective-permute-done((f32[2,64,128]{2,1,0:T(8,128)S(1)}, f32[2,64,128]{2,1,0:T(8,128)S(1)}, u32[]{:S(2)}, u32[]{:S(2)}) %collective-permute-start.7) | collective-permute-done | bytes 65568 | tf_op jit(solution)/shard_map/ppermute | solution.py:401
  26.5 0.1 collective-permute-start.8
  26.6 1.6 %collective-permute-start.9 = (f32[6,64,128]{2,1,0:T(8,128)S(1)}, f32[6,64,128]{2,1,0:T(8,128)S(1)}, u32[]{:S(2)}, u32[]{:S(2)}) collective-permute-start(f32[6,64,128]{2,1,0:T(8,128)S(1)} %constant_dynamic-update-slice_fusion.4.own), channel_id=1, source_target_pairs={{0,8},{1,2},{2,1},{3,4},{4,3},{5,6},{6,5},{7,15},{8,0},{9,10},{10,... | collective-permute-start | bytes 589832 | tf_op jit(solution)/shard_map/ppermute | solution.py:401
  28.1 0.0 collective-permute-done.8.chip
  28.2 4.2 %collective-permute-done.9.far = f32[6,64,128]{2,1,0:T(8,128)S(1)} collective-permute-done((f32[6,64,128]{2,1,0:T(8,128)S(1)}, f32[6,64,128]{2,1,0:T(8,128)S(1)}, u32[]{:S(2)}, u32[]{:S(2)}) %collective-permute-start.9) | collective-permute-done | bytes 196640 | tf_op jit(solution)/shard_map/ppermute | solution.py:401
  32.3 1.7 %last.1 = f32[19,64,128]{2,1,0:T(8,128)} custom-call(s32[16,128]{1,0:T(8,128)S(1)} %get-tuple-element.11.plan_ref, f32[19,64,128]{2,1,0:T(8,128)S(1)} %get-tuple-element.15.star, f32[6,64,128]{2,1,0:T(8,128)S(1)} %constant_dynamic-update-slice_fusion.4.own, f32[6,64,128]{2,1,0:T(8,128)S(1)} %collective-permute-done.8.chip, ...), custom_call_target="tpu_custom_call" | custom-call | tf_op jit(solution)/shard_map/last/pallas_call | solution.py:485
  (9 shorter events, 0.1 us)
Async XLA Ops:
  1.6 5.3 %collective-permute-start = (f32[2,64,128]{2,1,0:T(8,128)S(1)}, f32[2,64,128]{2,1,0:T(8,128)S(1)}, u32[]{:S(2)}, u32[]{:S(2)}) collective-permute-start(f32[2,64,128]{2,1,0:T(8,128)S(1)} %get-tuple-element.14), channel_id=1, source_target_pairs={{0,8},{1,9},{2,10},{3,11},{4,12},{5,13},{6,14},{7,15},{8,0},{9,1},... | collective-permute-start | bytes 196616 | tf_op jit(solution)/shard_map/ppermute | solution.py:401
  4.6 4.3 %collective-permute-start.1 = (f32[2,64,128]{2,1,0:T(8,128)S(1)}, f32[2,64,128]{2,1,0:T(8,128)S(1)}, u32[]{:S(2)}, u32[]{:S(2)}) collective-permute-start(f32[2,64,128]{2,1,0:T(8,128)S(1)} %get-tuple-element.14), channel_id=1, source_target_pairs={{0,16},{1,17},{2,18},{3,19},{4,20},{5,21},{6,22},{7,23},{8,24},{9,... | collective-permute-start | bytes 196616 | tf_op jit(solution)/shard_map/ppermute | solution.py:401
  6.3 5.2 %collective-permute-start.2 = (f32[2,64,128]{2,1,0:T(8,128)S(1)}, f32[2,64,128]{2,1,0:T(8,128)S(1)}, u32[]{:S(2)}, u32[]{:S(2)}) collective-permute-start(f32[2,64,128]{2,1,0:T(8,128)S(1)} %get-tuple-element.14), channel_id=1, source_target_pairs={{0,24},{1,25},{2,26},{3,27},{4,28},{5,29},{6,30},{7,31},{8,16},{9,... | collective-permute-start | bytes 196616 | tf_op jit(solution)/shard_map/ppermute | solution.py:401
  11.4 1.5 %collective-permute-start.3 = (f32[8,64,128]{2,1,0:T(8,128)S(1)}, f32[8,64,128]{2,1,0:T(8,128)S(1)}, u32[]{:S(2)}, u32[]{:S(2)}) collective-permute-start(f32[8,64,128]{2,1,0:T(8,128)S(1)} %constant_dynamic-update-slice_fusion.own), channel_id=1, source_target_pairs={{0,1},{1,0},{2,3},{3,2},{4,5},{5,4},{6,7},{7,6},{8,9},{9,8},{10,11... | collective-permute-start | bytes 786440 | tf_op jit(solution)/shard_map/ppermute | solution.py:401
  11.4 6.4 %collective-permute-start.4 = (f32[8,64,128]{2,1,0:T(8,128)S(1)}, f32[8,64,128]{2,1,0:T(8,128)S(1)}, u32[]{:S(2)}, u32[]{:S(2)}) collective-permute-start(f32[8,64,128]{2,1,0:T(8,128)S(1)} %constant_dynamic-update-slice_fusion.own), channel_id=1, source_target_pairs={{0,8},{1,2},{2,1},{3,4},{4,3},{5,6},{6,5},{7,15},{8,0},{9,10},{10,... | collective-permute-start | bytes 786440 | tf_op jit(solution)/shard_map/ppermute | solution.py:401
  18.9 4.3 %collective-permute-start.5 = (f32[2,64,128]{2,1,0:T(8,128)S(1)}, f32[2,64,128]{2,1,0:T(8,128)S(1)}, u32[]{:S(2)}, u32[]{:S(2)}) collective-permute-start(f32[2,64,128]{2,1,0:T(8,128)S(1)} %get-tuple-element.16), channel_id=1, source_target_pairs={{0,8},{1,9},{2,10},{3,11},{4,12},{5,13},{6,14},{7,15},{8,0},{9,1},... | collective-permute-start | bytes 196616 | tf_op jit(solution)/shard_map/ppermute | solution.py:401
  19.5 4.3 %collective-permute-start.6 = (f32[2,64,128]{2,1,0:T(8,128)S(1)}, f32[2,64,128]{2,1,0:T(8,128)S(1)}, u32[]{:S(2)}, u32[]{:S(2)}) collective-permute-start(f32[2,64,128]{2,1,0:T(8,128)S(1)} %get-tuple-element.16), channel_id=1, source_target_pairs={{0,16},{1,17},{2,18},{3,19},{4,20},{5,21},{6,22},{7,23},{8,24},{9,... | collective-permute-start | bytes 196616 | tf_op jit(solution)/shard_map/ppermute | solution.py:401
  21.3 5.2 %collective-permute-start.7 = (f32[2,64,128]{2,1,0:T(8,128)S(1)}, f32[2,64,128]{2,1,0:T(8,128)S(1)}, u32[]{:S(2)}, u32[]{:S(2)}) collective-permute-start(f32[2,64,128]{2,1,0:T(8,128)S(1)} %get-tuple-element.16), channel_id=1, source_target_pairs={{0,24},{1,25},{2,26},{3,27},{4,28},{5,29},{6,30},{7,31},{8,16},{9,... | collective-permute-start | bytes 196616 | tf_op jit(solution)/shard_map/ppermute | solution.py:401
  26.5 1.7 %collective-permute-start.8 = (f32[6,64,128]{2,1,0:T(8,128)S(1)}, f32[6,64,128]{2,1,0:T(8,128)S(1)}, u32[]{:S(2)}, u32[]{:S(2)}) collective-permute-start(f32[6,64,128]{2,1,0:T(8,128)S(1)} %constant_dynamic-update-slice_fusion.4.own), channel_id=1, source_target_pairs={{0,1},{1,0},{2,3},{3,2},{4,5},{5,4},{6,7},{7,6},{8,9},{9,8},{10,11... | collective-permute-start | bytes 589832 | tf_op jit(solution)/shard_map/ppermute | solution.py:401
  26.6 5.7 %collective-permute-start.9 = (f32[6,64,128]{2,1,0:T(8,128)S(1)}, f32[6,64,128]{2,1,0:T(8,128)S(1)}, u32[]{:S(2)}, u32[]{:S(2)}) collective-permute-start(f32[6,64,128]{2,1,0:T(8,128)S(1)} %constant_dynamic-update-slice_fusion.4.own), channel_id=1, source_target_pairs={{0,8},{1,2},{2,1},{3,4},{4,3},{5,6},{6,5},{7,15},{8,0},{9,10},{10,... | collective-permute-start | bytes 589832 | tf_op jit(solution)/shard_map/ppermute | solution.py:401

commit v2 on v1

--- a/solution.py
+++ b/solution.py
@@ -6,6 +6,7 @@
 from jax.experimental import pallas as pl
 from jax.experimental.pallas import tpu as pltpu
 from jax.sharding import PartitionSpec as P
+
 
 VELOCITIES = (
     (0, 0, 0), (1, 0, 0), (-1, 0, 0), (0, 1, 0), (0, -1, 0), (0, 0, 1), (0, 0, -1),
@@ -138,13 +139,10 @@
         section = divide(local, members)
         offset = local - section * members - me[1]
         which = jnp.where(offset == 0, 0, jnp.where(offset == chip, 1, 2))
-        if sections & (sections - 1) == 0:
-            apart = section ^ me[0]
-        else:
-            apart = me[0] - section
-            apart = jnp.where(apart < 0, apart + sections, apart)
+        apart = section ^ me[0]
         one = (which * sections + apart) * blocks + within
-        two = jnp.maximum((which * (sections - 1) + section - 1) * blocks + within, 0)
+        later = jnp.clip(section + 1, 2, max(sections - 2, 2))
+        two = (which * (sections - 1) + jnp.where(apart < 2, apart, later)) * blocks + within
         source = jnp.zeros_like(ids)
         for s in range(sections):
             source = jnp.where(section == s, level_ref[s], source)
@@ -346,14 +344,16 @@
 def gathered(plan_ref, plan, sem, parts, table):
     copy = pltpu.make_async_copy(plan_ref, plan, sem)
     copy.start()
-    for i, part in enumerate(parts):
+    row = 0
+    for part in parts:
         for k in range(part.shape[0]):
-            table[part.shape[0] * i + k] = part[k]
+            table[row] = part[k]
+            row += 1
     copy.wait()
 
 
-def middle_kernel(sizes, plan_ref, star, mask, own, chip, far, dst, out, plan, table, halo, sems):
-    gathered(plan_ref, plan, sems.at[0], (own, chip, far), table)
+def middle_kernel(sizes, plan_ref, star, mask, own, chip, near, far, dst, out, plan, table, halo, sems):
+    gathered(plan_ref, plan, sems.at[0], (own, chip, near, far), table)
     level = plan[0, 64]
 
     @pl.when(level >= 1)
@@ -372,8 +372,8 @@
     export(dst, out)
 
 
-def last_kernel(sizes, plan_ref, star, own, chip, far, result, plan, table, halo, moved, sems):
-    gathered(plan_ref, plan, sems.at[19], (own, chip, far), table)
+def last_kernel(sizes, plan_ref, star, own, chip, near, far, result, plan, table, halo, moved, sems):
+    gathered(plan_ref, plan, sems.at[19], (own, chip, near, far), table)
     level = plan[0, 64]
 
     @pl.when(level == 2)
@@ -402,29 +402,32 @@
 
 
 def exchange(exports, sections, members, last):
-    power = sections & (sections - 1) == 0
     me = lax.axis_index("section")
 
-    def across(d):
-        return lambda s, m: (s ^ d if power else (s + d) % sections, m)
+    def named(x, target):
+        return swap(x, sections, members, target)
 
     def beside(s, m):
         t = ((m + 1) ^ 1) - 1
-        return (s, t) if 0 <= t < members or sections % 2 else (s ^ 1, m)
-
-    parts = [swap(exports, sections, members, across(d)) for d in range(1, sections)]
+        return (s, t) if 0 <= t < members else (s ^ 1, m)
+
+    parts = [exports] + [named(exports, lambda s, m, d=d: (s ^ d, m)) for d in range(1, sections)]
+    first = jnp.concatenate(parts[:2], axis=0)
     if last:
-        blocks = exports.shape[0]
-        own = jnp.zeros(((sections - 1) * blocks,) + exports.shape[1:], exports.dtype)
-        for d, part in enumerate(parts, 1):
-            source = me ^ d if power else (me + sections - d) % sections
-            own = lax.dynamic_update_slice(own, part, (jnp.where(source == 0, me - 1, source - 1) * blocks, 0, 0))
-        own = lax.dynamic_update_slice(own, exports, ((me - 1) * blocks, 0, 0))
+        second = []
+        for t in range(1, sections - 2):
+            value = parts[sections - 1]
+            for d in range(2, sections - 1):
+                value = jnp.where(me ^ d == t, parts[d], value)
+            second.append(value)
+        second = jnp.concatenate(second, axis=0)
     else:
-        own = jnp.concatenate([exports] + parts, axis=0)
-    chip = swap(own, sections, members, lambda s, m: (s, m ^ 1))
-    far = swap(own, sections, members, beside)
-    return own, chip, far
+        second = jnp.concatenate(parts[2:], axis=0)
+    own = jnp.concatenate([first, second], axis=0)
+    near = named(first, beside)
+    far = named(second, beside)
+    chip = named(own, lambda s, m: (s, m ^ 1))
+    return own, chip, near, far
 
 
 def packed(x):
@@ -466,11 +469,11 @@
         compiler_params=params,
         name="first",
     )(*(pltpu.with_memory_space_constraint(x, pltpu.HBM) for x in (section_level, neighbours, links, pops, mask)))
-    own, chip, far = exchange(exports, sections, members, False)
+    parts = exchange(exports, sections, members, False)
     star, exports = pl.pallas_call(
         functools.partial(middle_kernel, sizes),
         out_shape=(field, planes),
-        in_specs=[ANY] + [VMEM] * 5,
+        in_specs=[ANY] + [VMEM] * 6,
         out_specs=(VMEM, VMEM),
         scratch_shapes=[
             plan_scratch,
@@ -480,12 +483,12 @@
         ],
         compiler_params=params,
         name="middle",
-    )(plan, star, mask, own, chip, far)
-    own, chip, far = exchange(exports, sections, members, True)
+    )(plan, star, mask, *parts)
+    parts = exchange(exports, sections, members, True)
     result = pl.pallas_call(
         functools.partial(last_kernel, sizes),
         out_shape=field,
-        in_specs=[ANY] + [VMEM] * 4,
+        in_specs=[ANY] + [VMEM] * 5,
         out_specs=HBM,
         scratch_shapes=[
             plan_scratch,
@@ -496,7 +499,7 @@
         ],
         compiler_params=params,
         name="last",
-    )(plan, star, own, chip, far)
+    )(plan, star, *parts)
     out = result.reshape(19, cells // 128, blocks, 128).transpose(2, 0, 1, 3)
     return out.reshape(blocks, 19, cells)
 

time: 34.2 us -> 34.5 us (level)
  starting transfers between devices: 10.4 us -> 12.6 us
  waiting for transfers between devices: 19.1 us -> 17.3 us
    ppermute x10 -> x12, starting transfers between devices: 10.4 us -> 12.6 us  [swap(): return lax.ppermute(x, ('section', 'member'), pairs)]
    ppermute x10 -> x12, waiting for transfers between devices: 19.1 us -> 17.3 us  [swap(): return lax.ppermute(x, ('section', 'member'), pairs)]
  transfers between devices with their start and end apart: 10 -> 12, of which waited for: 9 -> 9; matrix products, arithmetic and copies ran while one was open for 0% -> 0% of each run, Pallas kernels for 0% -> 0%
where the time goes in v2:
time: 34.5 us; the launch traced here: 34.3 us
  waiting for transfers between devices  17.3 us (50%)
  starting transfers between devices  12.6 us (37%)
  Pallas kernels  4.27 us (12%)
    ppermute x12, waiting for transfers between devices, swap(): return lax.ppermute(x, ('section', 'member'), pairs)  17.3 us
    ppermute x12, starting transfers between devices, swap(): return lax.ppermute(x, ('section', 'member'), pairs)  12.6 us
    pallas_call x1, Pallas kernels, body(): pl.pallas_call(functools.partial(last_kernel, sizes), out_shape=field, in...  1.68 us
    pallas_call x1, Pallas kernels, body(): pl.pallas_call(functools.partial(first_kernel, sizes), out_shape=(field,...  1.61 us
    pallas_call x1, Pallas kernels, body(): pl.pallas_call(functools.partial(middle_kernel, sizes), out_shape=(field,...  0.98 us
  transfers between devices with their start and end apart: 12, of which 9 were waited for; matrix products, arithmetic and copies ran while one was open for 0% of the time, Pallas kernels for 0%

profile of v2, /device:TPU:0, one launch (start us, length us, event | category | flops | bytes accessed | tf_op | source)
XLA Modules:
  0.0 34.3 jit_solution(10320210234301706039)
XLA Ops:
  0.0 1.6 %first.1 = (f32[19,64,128]{2,1,0:T(8,128)S(1)}, f32[2,64,128]{2,1,0:T(8,128)S(1)}, s32[16,128]{1,0:T(8,128)S(1)}, s32[64,128]{1,0:T(8,128)S(1)}) custom-call(s32[4]{0:T(128)} %level_hbm.1, s32[2,18]{1,0:T(2,128)} %near_hbm.1, s32[2,4,6]{2,1,0:T(4,128)} %bitcast.18, f32[19,64,128]{2,1,0:T(8,128)} %bitcast.16, s32[64,128]{1,0:T(8,128)} %bitcast.17), custom_call_target="tpu_custom_call" | custom-call | tf_op jit(solution)/shard_map/first/pallas_call | solution.py:457
  1.6 3.1 %collective-permute-start = (f32[2,64,128]{2,1,0:T(8,128)S(1)}, f32[2,64,128]{2,1,0:T(8,128)S(1)}, u32[]{:S(2)}, u32[]{:S(2)}) collective-permute-start(f32[2,64,128]{2,1,0:T(8,128)S(1)} %get-tuple-element.14), channel_id=1, source_target_pairs={{0,8},{1,9},{2,10},{3,11},{4,12},{5,13},{6,14},{7,15},{8,0},{9,1},... | collective-permute-start | bytes 196616 | tf_op jit(solution)/shard_map/ppermute | solution.py:401
  4.7 1.5 %collective-permute-start.1 = (f32[2,64,128]{2,1,0:T(8,128)S(1)}, f32[2,64,128]{2,1,0:T(8,128)S(1)}, u32[]{:S(2)}, u32[]{:S(2)}) collective-permute-start(f32[2,64,128]{2,1,0:T(8,128)S(1)} %get-tuple-element.14), channel_id=1, source_target_pairs={{0,16},{1,17},{2,18},{3,19},{4,20},{5,21},{6,22},{7,23},{8,24},{9,... | collective-permute-start | bytes 196616 | tf_op jit(solution)/shard_map/ppermute | solution.py:401
  6.2 0.0 collective-permute-start.2
  6.3 0.8 %collective-permute-done = f32[2,64,128]{2,1,0:T(8,128)S(1)} collective-permute-done((f32[2,64,128]{2,1,0:T(8,128)S(1)}, f32[2,64,128]{2,1,0:T(8,128)S(1)}, u32[]{:S(2)}, u32[]{:S(2)}) %collective-permute-start) | collective-permute-done | bytes 65568 | tf_op jit(solution)/shard_map/ppermute | solution.py:401
  7.1 1.9 %collective-permute-done.1 = f32[2,64,128]{2,1,0:T(8,128)S(1)} collective-permute-done((f32[2,64,128]{2,1,0:T(8,128)S(1)}, f32[2,64,128]{2,1,0:T(8,128)S(1)}, u32[]{:S(2)}, u32[]{:S(2)}) %collective-permute-start.1) | collective-permute-done | bytes 65568 | tf_op jit(solution)/shard_map/ppermute | solution.py:401
  9.0 2.4 %collective-permute-done.2 = f32[2,64,128]{2,1,0:T(8,128)S(1)} collective-permute-done((f32[2,64,128]{2,1,0:T(8,128)S(1)}, f32[2,64,128]{2,1,0:T(8,128)S(1)}, u32[]{:S(2)}, u32[]{:S(2)}) %collective-permute-start.2) | collective-permute-done | bytes 65568 | tf_op jit(solution)/shard_map/ppermute | solution.py:401
  11.4 0.0 collective-permute-start.3
  11.4 0.6 %collective-permute-start.5 = (f32[4,64,128]{2,1,0:T(8,128)S(1)}, f32[4,64,128]{2,1,0:T(8,128)S(1)}, u32[]{:S(2)}, u32[]{:S(2)}) collective-permute-start(f32[4,64,128]{2,1,0:T(8,128)S(1)} %pad_maximum_fusion.2), channel_id=1, source_target_pairs={{0,8},{1,2},{2,1},{3,4},{4,3},{5,6},{6,5},{7,15},{8,0},{9,10},{10,... | collective-permute-start | bytes 393224 | tf_op jit(solution)/shard_map/ppermute | solution.py:401
  12.1 1.6 %collective-permute-start.4 = (f32[4,64,128]{2,1,0:T(8,128)S(1)}, f32[4,64,128]{2,1,0:T(8,128)S(1)}, u32[]{:S(2)}, u32[]{:S(2)}) collective-permute-start(f32[4,64,128]{2,1,0:T(8,128)S(1)} %pad_maximum_fusion.1), channel_id=1, source_target_pairs={{0,8},{1,2},{2,1},{3,4},{4,3},{5,6},{6,5},{7,15},{8,0},{9,10},{10,... | collective-permute-start | bytes 393224 | tf_op jit(solution)/shard_map/ppermute | solution.py:401
  13.6 2.9 %collective-permute-done.5.far = f32[4,64,128]{2,1,0:T(8,128)S(1)} collective-permute-done((f32[4,64,128]{2,1,0:T(8,128)S(1)}, f32[4,64,128]{2,1,0:T(8,128)S(1)}, u32[]{:S(2)}, u32[]{:S(2)}) %collective-permute-start.5) | collective-permute-done | bytes 131104 | tf_op jit(solution)/shard_map/ppermute | solution.py:401
  16.5 1.4 %collective-permute-done.4.near = f32[4,64,128]{2,1,0:T(8,128)S(1)} collective-permute-done((f32[4,64,128]{2,1,0:T(8,128)S(1)}, f32[4,64,128]{2,1,0:T(8,128)S(1)}, u32[]{:S(2)}, u32[]{:S(2)}) %collective-permute-start.4) | collective-permute-done | bytes 131104 | tf_op jit(solution)/shard_map/ppermute | solution.py:401
  17.9 0.0 collective-permute-done.3.chip
  17.9 1.0 %middle.1 = (f32[19,64,128]{2,1,0:T(8,128)S(1)}, f32[2,64,128]{2,1,0:T(8,128)S(1)}) custom-call(s32[16,128]{1,0:T(8,128)S(1)} %get-tuple-element.11.plan_ref, f32[19,64,128]{2,1,0:T(8,128)S(1)} %get-tuple-element.12.star, s32[64,128]{1,0:T(8,128)S(1)} %get-tuple-element.13.mask, f32[8,64,128]{2,1,0:T(8,128)S(1)} %constant_dynamic-update-slice_fusion.own, ...), custom_call_target="tpu_custom_call" | custom-call | tf_op jit(solution)/shard_map/middle/pallas_call | solution.py:473
  18.9 1.9 %collective-permute-start.7 = (f32[2,64,128]{2,1,0:T(8,128)S(1)}, f32[2,64,128]{2,1,0:T(8,128)S(1)}, u32[]{:S(2)}, u32[]{:S(2)}) collective-permute-start(f32[2,64,128]{2,1,0:T(8,128)S(1)} %get-tuple-element.16), channel_id=1, source_target_pairs={{0,16},{1,17},{2,18},{3,19},{4,20},{5,21},{6,22},{7,23},{8,24},{9,... | collective-permute-start | bytes 196616 | tf_op jit(solution)/shard_map/ppermute | solution.py:401
  20.8 1.7 %collective-permute-start.8 = (f32[2,64,128]{2,1,0:T(8,128)S(1)}, f32[2,64,128]{2,1,0:T(8,128)S(1)}, u32[]{:S(2)}, u32[]{:S(2)}) collective-permute-start(f32[2,64,128]{2,1,0:T(8,128)S(1)} %get-tuple-element.16), channel_id=1, source_target_pairs={{0,24},{1,25},{2,26},{3,27},{4,28},{5,29},{6,30},{7,31},{8,16},{9,... | collective-permute-start | bytes 196616 | tf_op jit(solution)/shard_map/ppermute | solution.py:401
  22.5 0.0 collective-permute-start.6
  22.5 1.5 %collective-permute-done.7 = f32[2,64,128]{2,1,0:T(8,128)S(1)} collective-permute-done((f32[2,64,128]{2,1,0:T(8,128)S(1)}, f32[2,64,128]{2,1,0:T(8,128)S(1)}, u32[]{:S(2)}, u32[]{:S(2)}) %collective-permute-start.7) | collective-permute-done | bytes 65568 | tf_op jit(solution)/shard_map/ppermute | solution.py:401
  24.0 2.1 %collective-permute-done.8 = f32[2,64,128]{2,1,0:T(8,128)S(1)} collective-permute-done((f32[2,64,128]{2,1,0:T(8,128)S(1)}, f32[2,64,128]{2,1,0:T(8,128)S(1)}, u32[]{:S(2)}, u32[]{:S(2)}) %collective-permute-start.8) | collective-permute-done | bytes 65568 | tf_op jit(solution)/shard_map/ppermute | solution.py:401
  26.1 0.7 %collective-permute-done.6 = f32[2,64,128]{2,1,0:T(8,128)S(1)} collective-permute-done((f32[2,64,128]{2,1,0:T(8,128)S(1)}, f32[2,64,128]{2,1,0:T(8,128)S(1)}, u32[]{:S(2)}, u32[]{:S(2)}) %collective-permute-start.6) | collective-permute-done | bytes 65568 | tf_op jit(solution)/shard_map/ppermute | solution.py:401
  26.8 0.1 collective-permute-start.9
  26.9 1.2 %collective-permute-start.10 = (f32[4,64,128]{2,1,0:T(8,128)S(1)}, f32[4,64,128]{2,1,0:T(8,128)S(1)}, u32[]{:S(2)}, u32[]{:S(2)}) collective-permute-start(f32[4,64,128]{2,1,0:T(8,128)S(1)} %pad_maximum_fusion.3), channel_id=1, source_target_pairs={{0,8},{1,2},{2,1},{3,4},{4,3},{5,6},{6,5},{7,15},{8,0},{9,10},{10,... | collective-permute-start | bytes 393224 | tf_op jit(solution)/shard_map/ppermute | solution.py:401
  28.1 0.9 %collective-permute-start.11 = (f32[2,64,128]{2,1,0:T(8,128)S(1)}, f32[2,64,128]{2,1,0:T(8,128)S(1)}, u32[]{:S(2)}, u32[]{:S(2)}) collective-permute-start(f32[2,64,128]{2,1,0:T(8,128)S(1)} %broadcast_select_fusion), channel_id=1, source_target_pairs={{0,8},{1,2},{2,1},{3,4},{4,3},{5,6},{6,5},{7,15},{8,0},{9,10},{10,... | collective-permute-start | bytes 196616 | tf_op jit(solution)/shard_map/ppermute | solution.py:401
  29.0 3.6 %collective-permute-done.11.far = f32[2,64,128]{2,1,0:T(8,128)S(1)} collective-permute-done((f32[2,64,128]{2,1,0:T(8,128)S(1)}, f32[2,64,128]{2,1,0:T(8,128)S(1)}, u32[]{:S(2)}, u32[]{:S(2)}) %collective-permute-start.11) | collective-permute-done | bytes 65568 | tf_op jit(solution)/shard_map/ppermute | solution.py:401
  32.6 0.0 collective-permute-done.10.near
  32.6 0.0 collective-permute-done.9.chip
  32.6 1.7 %last.1 = f32[19,64,128]{2,1,0:T(8,128)} custom-call(s32[16,128]{1,0:T(8,128)S(1)} %get-tuple-element.11.plan_ref, f32[19,64,128]{2,1,0:T(8,128)S(1)} %get-tuple-element.15.star, f32[6,64,128]{2,1,0:T(8,128)S(1)} %pad_maximum_fusion.own, f32[6,64,128]{2,1,0:T(8,128)S(1)} %collective-permute-done.9.chip, f32[4,64,128]{2,1,0:T(8,128)S(1)} %collective-permute-done.10.near, ...), custom_call_target="tpu_custom_call" | custom-call | tf_op jit(solution)/shard_map/last/pallas_call | solution.py:488
  (9 shorter events, 0.1 us)
Async XLA Ops:
  1.6 5.5 %collective-permute-start = (f32[2,64,128]{2,1,0:T(8,128)S(1)}, f32[2,64,128]{2,1,0:T(8,128)S(1)}, u32[]{:S(2)}, u32[]{:S(2)}) collective-permute-start(f32[2,64,128]{2,1,0:T(8,128)S(1)} %get-tuple-element.14), channel_id=1, source_target_pairs={{0,8},{1,9},{2,10},{3,11},{4,12},{5,13},{6,14},{7,15},{8,0},{9,1},... | collective-permute-start | bytes 196616 | tf_op jit(solution)/shard_map/ppermute | solution.py:401
  4.7 4.3 %collective-permute-start.1 = (f32[2,64,128]{2,1,0:T(8,128)S(1)}, f32[2,64,128]{2,1,0:T(8,128)S(1)}, u32[]{:S(2)}, u32[]{:S(2)}) collective-permute-start(f32[2,64,128]{2,1,0:T(8,128)S(1)} %get-tuple-element.14), channel_id=1, source_target_pairs={{0,16},{1,17},{2,18},{3,19},{4,20},{5,21},{6,22},{7,23},{8,24},{9,... | collective-permute-start | bytes 196616 | tf_op jit(solution)/shard_map/ppermute | solution.py:401
  6.2 5.2 %collective-permute-start.2 = (f32[2,64,128]{2,1,0:T(8,128)S(1)}, f32[2,64,128]{2,1,0:T(8,128)S(1)}, u32[]{:S(2)}, u32[]{:S(2)}) collective-permute-start(f32[2,64,128]{2,1,0:T(8,128)S(1)} %get-tuple-element.14), channel_id=1, source_target_pairs={{0,24},{1,25},{2,26},{3,27},{4,28},{5,29},{6,30},{7,31},{8,16},{9,... | collective-permute-start | bytes 196616 | tf_op jit(solution)/shard_map/ppermute | solution.py:401
  11.4 6.5 %collective-permute-start.3 = (f32[8,64,128]{2,1,0:T(8,128)S(1)}, f32[8,64,128]{2,1,0:T(8,128)S(1)}, u32[]{:S(2)}, u32[]{:S(2)}) collective-permute-start(f32[8,64,128]{2,1,0:T(8,128)S(1)} %constant_dynamic-update-slice_fusion.own), channel_id=1, source_target_pairs={{0,1},{1,0},{2,3},{3,2},{4,5},{5,4},{6,7},{7,6},{8,9},{9,8},{10,11... | collective-permute-start | bytes 786440 | tf_op jit(solution)/shard_map/ppermute | solution.py:401
  11.4 5.0 %collective-permute-start.5 = (f32[4,64,128]{2,1,0:T(8,128)S(1)}, f32[4,64,128]{2,1,0:T(8,128)S(1)}, u32[]{:S(2)}, u32[]{:S(2)}) collective-permute-start(f32[4,64,128]{2,1,0:T(8,128)S(1)} %pad_maximum_fusion.2), channel_id=1, source_target_pairs={{0,8},{1,2},{2,1},{3,4},{4,3},{5,6},{6,5},{7,15},{8,0},{9,10},{10,... | collective-permute-start | bytes 393224 | tf_op jit(solution)/shard_map/ppermute | solution.py:401
  12.1 5.8 %collective-permute-start.4 = (f32[4,64,128]{2,1,0:T(8,128)S(1)}, f32[4,64,128]{2,1,0:T(8,128)S(1)}, u32[]{:S(2)}, u32[]{:S(2)}) collective-permute-start(f32[4,64,128]{2,1,0:T(8,128)S(1)} %pad_maximum_fusion.1), channel_id=1, source_target_pairs={{0,8},{1,2},{2,1},{3,4},{4,3},{5,6},{6,5},{7,15},{8,0},{9,10},{10,... | collective-permute-start | bytes 393224 | tf_op jit(solution)/shard_map/ppermute | solution.py:401
  18.9 5.1 %collective-permute-start.7 = (f32[2,64,128]{2,1,0:T(8,128)S(1)}, f32[2,64,128]{2,1,0:T(8,128)S(1)}, u32[]{:S(2)}, u32[]{:S(2)}) collective-permute-start(f32[2,64,128]{2,1,0:T(8,128)S(1)} %get-tuple-element.16), channel_id=1, source_target_pairs={{0,16},{1,17},{2,18},{3,19},{4,20},{5,21},{6,22},{7,23},{8,24},{9,... | collective-permute-start | bytes 196616 | tf_op jit(solution)/shard_map/ppermute | solution.py:401
  20.8 5.3 %collective-permute-start.8 = (f32[2,64,128]{2,1,0:T(8,128)S(1)}, f32[2,64,128]{2,1,0:T(8,128)S(1)}, u32[]{:S(2)}, u32[]{:S(2)}) collective-permute-start(f32[2,64,128]{2,1,0:T(8,128)S(1)} %get-tuple-element.16), channel_id=1, source_target_pairs={{0,24},{1,25},{2,26},{3,27},{4,28},{5,29},{6,30},{7,31},{8,16},{9,... | collective-permute-start | bytes 196616 | tf_op jit(solution)/shard_map/ppermute | solution.py:401
  22.5 4.3 %collective-permute-start.6 = (f32[2,64,128]{2,1,0:T(8,128)S(1)}, f32[2,64,128]{2,1,0:T(8,128)S(1)}, u32[]{:S(2)}, u32[]{:S(2)}) collective-permute-start(f32[2,64,128]{2,1,0:T(8,128)S(1)} %get-tuple-element.16), channel_id=1, source_target_pairs={{0,8},{1,9},{2,10},{3,11},{4,12},{5,13},{6,14},{7,15},{8,0},{9,1},... | collective-permute-start | bytes 196616 | tf_op jit(solution)/shard_map/ppermute | solution.py:401
  26.8 5.8 %collective-permute-start.9 = (f32[6,64,128]{2,1,0:T(8,128)S(1)}, f32[6,64,128]{2,1,0:T(8,128)S(1)}, u32[]{:S(2)}, u32[]{:S(2)}) collective-permute-start(f32[6,64,128]{2,1,0:T(8,128)S(1)} %pad_maximum_fusion.own), channel_id=1, source_target_pairs={{0,1},{1,0},{2,3},{3,2},{4,5},{5,4},{6,7},{7,6},{8,9},{9,8},{10,11... | collective-permute-start | bytes 589832 | tf_op jit(solution)/shard_map/ppermute | solution.py:401
  26.9 5.7 %collective-permute-start.10 = (f32[4,64,128]{2,1,0:T(8,128)S(1)}, f32[4,64,128]{2,1,0:T(8,128)S(1)}, u32[]{:S(2)}, u32[]{:S(2)}) collective-permute-start(f32[4,64,128]{2,1,0:T(8,128)S(1)} %pad_maximum_fusion.3), channel_id=1, source_target_pairs={{0,8},{1,2},{2,1},{3,4},{4,3},{5,6},{6,5},{7,15},{8,0},{9,10},{10,... | collective-permute-start | bytes 393224 | tf_op jit(solution)/shard_map/ppermute | solution.py:401
  28.1 4.5 %collective-permute-start.11 = (f32[2,64,128]{2,1,0:T(8,128)S(1)}, f32[2,64,128]{2,1,0:T(8,128)S(1)}, u32[]{:S(2)}, u32[]{:S(2)}) collective-permute-start(f32[2,64,128]{2,1,0:T(8,128)S(1)} %broadcast_select_fusion), channel_id=1, source_target_pairs={{0,8},{1,2},{2,1},{3,4},{4,3},{5,6},{6,5},{7,15},{8,0},{9,10},{10,... | collective-permute-start | bytes 196616 | tf_op jit(solution)/shard_map/ppermute | solution.py:401

commit v3 on v2

--- a/solution.py
+++ b/solution.py
@@ -41,8 +41,8 @@
     return pltpu.roll(x, shift % 8, 0)
 
 
-def tile(ref, q, t):
-    return ref[q, 8 * t : 8 * t + 8, :]
+def tile(ref, q, t, base=0):
+    return ref[q, base + 8 * t : base + 8 * t + 8, :]
 
 
 def bulk(ref, row):
@@ -55,10 +55,10 @@
     )
 
 
-def collide(src, dst, mask, rate, ready):
+def collide(src, base, dst, mask, rate, ready):
     for t in range(TILES):
         ready(t)
-        f = [tile(src, q, t) for q in range(19)]
+        f = [tile(src, q, t, base) for q in range(19)]
         density = f[0]
         for q in range(1, 19):
             density = density + f[q]
@@ -70,11 +70,11 @@
                 total = total + (f[q] - f[OPPOSITE[q]])
             velocity.append(total / density)
         speed = velocity[0] * velocity[0] + velocity[1] * velocity[1] + velocity[2] * velocity[2]
-        base = 1.0 - 1.5 * speed
+        still = 1.0 - 1.5 * speed
         fluid = mask[8 * t : 8 * t + 8, :] == 1
         keep = 1.0 - rate
         scaled = [rate * jnp.float32(w) * density for w in (WEIGHTS[0], WEIGHTS[1], WEIGHTS[7])]
-        out = keep * f[0] + scaled[0] * base
+        out = keep * f[0] + scaled[0] * still
         dst[0, 8 * t : 8 * t + 8, :] = jnp.where(fluid, out, f[0])
         for q in range(1, 19, 2):
             o = OPPOSITE[q]
@@ -85,7 +85,7 @@
                     term = velocity[a] if c > 0 else -velocity[a]
                     along = term if along is None else along + term
             weight = scaled[1] if q < 7 else scaled[2]
-            even = base + 4.5 * along * along
+            even = still + 4.5 * along * along
             odd = 3.0 * along
             dst[q, 8 * t : 8 * t + 8, :] = jnp.where(fluid, keep * f[q] + weight * (even + odd), f[o])
             dst[o, 8 * t : 8 * t + 8, :] = jnp.where(fluid, keep * f[o] + weight * (even - odd), f[q])
@@ -94,33 +94,37 @@
 def export(src, out):
     sub, lane = iotas()
     xl, yh = sub // 4, (sub // 2) % 2
+    z = lane & 15
+    own_x = ((lane >> 4) & 1) == xl
+    own_y = ((lane >> 3) & 1) == yh
     for j in range(6):
         axis, high = j // 2, j % 2 == 0
+        index = (lane & 7) * 16 + (15 - (lane >> 5) if high else lane >> 5)
         for i, q in enumerate(LISTS[j]):
-            if axis == 0:
-                v = tile(src, q, TILES - 1 if high else 0)
-                first = 4 if high else 0
-                for h in range(2):
-                    for b in range(2):
-                        s = first + 2 * h + b
-                        r = 10 * j + 5 * h + i
-                        out[b, r : r + 1, :] = v[s : s + 1, :]
-                continue
             for h in range(2):
-                total = jnp.zeros((8, 128), jnp.float32)
-                for k in range(4):
-                    if axis == 1:
-                        index = (lane & 15) + (112 if high else 0)
-                        here = (lane >> 4 == 2 * k + xl) & (yh == (1 if high else 0))
-                    else:
-                        index = (lane & 7) * 16 + (15 if high else 0)
-                        here = lane >> 3 == (2 * k + xl) * 2 + yh
-                    total = jnp.where(here, pick(tile(src, q, 4 * h + k), index), total)
-                total = total + subs(total, 4)
-                total = total + subs(total, 2)
+                r = 10 * j + 5 * h + i
+                if axis == 0:
+                    v = tile(src, q, TILES - 1 if high else 0)
+                    first = (4 if high else 0) + 2 * h
+                elif axis == 1:
+                    v = None
+                    for k in range(4):
+                        part = lanes(tile(src, q, 4 * h + k), 32 * k + (16 if high else 0))
+                        v = part if v is None else jnp.where(lane >> 5 == k, part, v)
+                    v = jnp.where(xl == 1, lanes(v, 16), v)
+                    v = jnp.where(own_x, v, subs(v, 4))
+                    first = 2 if high else 0
+                else:
+                    v = tile(src, q, 4 * h)
+                    for k in range(1, 4):
+                        part = lanes(tile(src, q, 4 * h + k), -k if high else k)
+                        v = jnp.where(z == (15 - k if high else k), part, v)
+                    v = pick(v, index)
+                    v = jnp.where(own_x, v, subs(v, 4))
+                    v = jnp.where(own_y, v, subs(v, 2))
+                    first = 0
                 for b in range(2):
-                    r = 10 * j + 5 * h + i
-                    out[b, r : r + 1, :] = total[b : b + 1, :]
+                    out[b, r : r + 1, :] = v[first + b : first + b + 1, :]
 
 
 def divide(x, n):
@@ -149,6 +153,7 @@
         return (one, two), source
 
     plan[0:1, 64:65] = jnp.full((1, 1), level, jnp.int32)
+    split = jnp.zeros((1, 1), jnp.int32)
     for block in range(blocks):
         near = near_ref[block : block + 1, :]
         near_slots, _ = placed(near)
@@ -161,6 +166,7 @@
         any_fine = jnp.max(jnp.where(fine, 1, 0), axis=0, keepdims=True)
         kind = jnp.where(quadrant >= 0, 1, jnp.where(any_fine > 0, 2, 3))
         kind = jnp.where(near[:, :6] >= 0, 0, kind)
+        split = jnp.maximum(split, jnp.max(jnp.where(kind == 2, 1, 0), axis=1, keepdims=True))
         for r in range(2):
             first = 32 * r
             plan[block : block + 1, first : first + 18] = jnp.where(near >= 0, near_slots[r], -1)
@@ -169,61 +175,61 @@
             plan[10 + block : 11 + block, first : first + 6] = chosen
             plan[12 + block : 13 + block, first : first + 6] = kind
             plan[14 + block : 15 + block, first : first + 6] = quadrant
+    plan[0:1, 65:66] = split
 
 
 def arrived(plan, base, table, halo, blocks):
     sub, lane = iotas()
     sub, lane = sub[:5], lane[:5]
+
+    def rows(slot, j, part):
+        first = 10 * (j ^ 1) + 5 * part
+        return table[slot, first : first + 5, :]
+
+    def whole(scalar):
+        return jnp.full((5, 128), scalar, jnp.int32)
+
+    spread = (lane >> 5) * 16 + ((lane & 15) >> 1)
     for block in range(blocks):
         for j in range(6):
+            kind = whole(plan[12 + block, base + j])
+            near = jnp.maximum(plan[block, base + j], 0)
+            slot = jnp.maximum(plan[10 + block, base + j], 0)
+            quadrant = whole(plan[14 + block, base + j])
+            source = jnp.where(quadrant < 2, rows(slot, j, 0), rows(slot, j, 1))
+            source = jnp.where((quadrant & 1) == 1, lanes(source, -8), source)
+            rest = [WEIGHTS[q] for q in LISTS[j ^ 1]]
+            straight = rest.index(WEIGHTS[1])
+            rest = jnp.where(sub == straight, jnp.float32(WEIGHTS[1]), jnp.float32(WEIGHTS[7]))
+            for h in range(2):
+                coarse = pick(lanes(source, 64) if h else source, spread)
+                value = jnp.where(kind == 0, rows(near, j, h), jnp.where(kind == 1, coarse, rest))
+                halo[block, 10 * j + 5 * h : 10 * j + 5 * h + 5, :] = value
+
+
+def arrived_fine(plan, base, table, halo, blocks):
+    _, lane = iotas()
+    lane = lane[:5]
+    odd_v, odd_u = (lane & 1) == 1, ((lane >> 4) & 1) == 1
+    gather = (2 * ((lane >> 4) & 3) + (lane >> 6)) * 16 + 2 * (lane & 7) + ((lane >> 3) & 1)
+    for block in range(blocks):
+        for j in range(6):
+            kind = jnp.full((5, 128), plan[12 + block, base + j], jnp.int32)
             first = 10 * (j ^ 1)
-            kind = plan[12 + block, base + j]
-
-            def rows(slot, part):
-                return table[slot, first + 5 * part : first + 5 * part + 5, :]
-
-            @pl.when(kind == 0)
-            def _():
-                halo[block, 10 * j : 10 * j + 10, :] = table[plan[block, base + j], first : first + 10, :]
-
-            @pl.when(kind == 1)
-            def _():
-                slot = plan[10 + block, base + j]
-                quadrant = plan[14 + block, base + j]
-                low = jnp.full((5, 128), quadrant, jnp.int32) < 2
-                source = jnp.where(low, rows(slot, 0), rows(slot, 1))
-                shift = 8 * (quadrant & 1)
+            for a in range(2):
+                pairs = []
                 for h in range(2):
-                    index = (4 * h + (lane >> 5)) * 16 + shift + ((lane & 15) >> 1)
-                    halo[block, 10 * j + 5 * h : 10 * j + 5 * h + 5, :] = pick(source, index)
-
-            @pl.when(kind == 2)
-            def _():
-                index = ((lane >> 4) & 3) * 32 + 2 * (lane & 7)
-                quads = []
-                for k in range(4):
-                    slot = plan[2 + 4 * block + k, base + j]
-                    scale = jnp.where(slot >= 0, jnp.float32(0.25), jnp.float32(0.0))
-                    slot = jnp.maximum(slot, 0)
-                    parts = []
-                    for h in range(2):
-                        v = rows(slot, h)
-                        v = v + lanes(v, -1)
-                        v = v + lanes(v, -16)
-                        parts.append(pick(v, index))
-                    quads.append(jnp.where(lane >= 64, parts[1], parts[0]) * scale)
-                for a in range(2):
-                    halo[block, 10 * j + 5 * a : 10 * j + 5 * a + 5, :] = jnp.where(
-                        lane & 8 == 0, quads[2 * a], quads[2 * a + 1]
-                    )
-
-            @pl.when(kind == 3)
-            def _():
-                rest = [WEIGHTS[q] for q in LISTS[j ^ 1]]
-                straight = rest.index(WEIGHTS[1])
-                value = jnp.where(sub == straight, jnp.float32(WEIGHTS[1]), jnp.float32(WEIGHTS[7]))
-                halo[block, 10 * j : 10 * j + 5, :] = value
-                halo[block, 10 * j + 5 : 10 * j + 10, :] = value
+                    sums = []
+                    for b in range(2):
+                        slot = plan[2 + 4 * block + 2 * a + b, base + j]
+                        scale = jnp.where(slot >= 0, jnp.float32(0.25), jnp.float32(0.0))
+                        v = table[jnp.maximum(slot, 0), first + 5 * h : first + 5 * h + 5, :] * scale
+                        sums.append(v + lanes(v, 1 if b else -1))
+                    v = jnp.where(odd_v, sums[1], sums[0])
+                    pairs.append(v + lanes(v, 16 if h else -16))
+                value = pick(jnp.where(odd_u, pairs[1], pairs[0]), gather)
+                r = 10 * j + 5 * a
+                halo[block, r : r + 5, :] = jnp.where(kind == 2, value, halo[block, r : r + 5, :])
 
 
 def stream(src, dst, plan, base, table, halo, blocks, done):
@@ -231,77 +237,79 @@
     odd = (sub & 1) == 1
     xl, yh = sub // 4, (sub // 2) % 2
     z = lane & 15
-    starts = [(2 * k + xl) * 16 for k in range(4)]
+
+    def both(one, two):
+        return jnp.where(odd, two, one)
 
     def plane(j, i, h):
-        return jnp.where(odd, bulk(halo.at[1], 10 * j + 5 * h + i), bulk(halo.at[0], 10 * j + 5 * h + i))
+        r = 10 * j + 5 * h + i
+        return both(bulk(halo.at[0], r), bulk(halo.at[1], r))
+
+    def edge_row(q, e, h):
+        a = [n for n in range(3) if VELOCITIES[q][n]][0]
+        j = 2 * a + (0 if VELOCITIES[q][a] > 0 else 1)
+        r = 10 * j + 5 * h + LISTS[j].index(q)
+        found = []
+        for block in range(blocks):
+            slot = plan[block, base + e]
+            good = jnp.full((8, 128), slot, jnp.int32) >= 0
+            found.append(jnp.where(good, bulk(table.at[jnp.maximum(slot, 0)], r), jnp.float32(WEIGHTS[q])))
+        return both(*found)
 
     for q in range(19):
         c = VELOCITIES[q]
         moving = [a for a in range(3) if c[a]]
-        values = [tile(src, q, t) for t in range(TILES)]
+        e = VELOCITIES.index(tuple(-v for v in c)) - 1
         planes = {}
         for a in moving:
             j = 2 * a + (0 if c[a] < 0 else 1)
             i = LISTS[j ^ 1].index(q)
             planes[a] = [plane(j, i, h) for h in range(2)]
-        line = None
-        if len(moving) == 2:
-            e = VELOCITIES.index(tuple(-v for v in c)) - 1
-            j = 2 * moving[0] + (0 if c[moving[0]] > 0 else 1)
-            i = LISTS[j].index(q)
-            found = []
-            for block in range(blocks):
-                slot = plan[block, base + e]
-                good = jnp.full((8, 128), slot, jnp.int32) >= 0
-                slot = jnp.maximum(slot, 0)
-                found.append(
-                    [jnp.where(good, bulk(table.at[slot], 10 * j + 5 * h + i), jnp.float32(WEIGHTS[q])) for h in range(2)]
-                )
-            line = [jnp.where(odd, found[1][h], found[0][h]) for h in range(2)]
-        outside = jnp.where(yh == 1, planes[0][1], planes[0][0]) if c[0] else None
-
-        if c[2]:
-            up = c[2] > 0
-            edge = z == (0 if up else 15)
-            values = [
-                jnp.where(edge, pick(planes[2][t // 4], starts[t % 4] + yh * 8 + (lane >> 4)), lanes(v, c[2]))
-                for t, v in enumerate(values)
-            ]
-            if c[0]:
-                spread = jnp.where(yh == 1, line[1], line[0])
-                outside = jnp.where(edge, lanes(spread, -15 if up else 15), lanes(outside, c[2]))
         if c[1]:
             up = c[1] > 0
-            edge = lane < 16 if up else lane >= 112
+            y_edge = lane >= 112 if up else lane < 16
             inner = yh == (1 if up else 0)
-
-            def moved(v, border):
-                rolled = lanes(v, 16 * c[1])
-                return jnp.where(edge, jnp.where(inner, subs(rolled, 2 * c[1]), border), rolled)
-
-            for t in range(TILES):
-                start, source = starts[t % 4], planes[1][t // 4]
-                if c[2]:
-                    if c[2] > 0:
-                        border = jnp.where(z == 0, pick(line[t // 4], start + 15), pick(source, start + jnp.maximum(z - 1, 0)))
-                    else:
-                        border = jnp.where(z == 15, pick(line[t // 4], start), pick(source, start + jnp.minimum(z + 1, 15)))
-                else:
-                    border = pick(source, start + z)
-                values[t] = moved(values[t], border)
-            if c[0]:
-                outside = moved(outside, lanes(line[1 if up else 0], 16 * c[1]))
+            beside = [jnp.where(xl == 0, v, lanes(v, -16)) for v in planes[1]]
+
+            def joined(v, border):
+                return jnp.where(y_edge, jnp.where(inner, subs(v, 2 * c[1]), border), v)
+
+        if c[2]:
+            z_edge = z == (0 if c[2] > 0 else 15)
+            tile_of = z & 3 if c[2] > 0 else (15 - z) & 3
+            index = (2 * tile_of + xl) * 16 + ((yh * 8 + (lane >> 4) - c[1]) & 15)
+            columns = []
+            for h in range(2):
+                v = planes[2][h]
+                if c[1]:
+                    line = edge_row(q, e, h)
+                    place, natural = (15 if c[1] > 0 else 0), (15 if c[2] > 0 else 0)
+                    if place != natural:
+                        line = lanes(line, place - natural)
+                    v = jnp.where(z == place, line, v)
+                columns.append(pick(v, index))
+        shift = 16 * c[1] + c[2]
+        first = 8 + 4 * c[0]
+        for t in range(TILES):
+            h, k = t // 4, t % 4
+            v = tile(src, q, t)
+            if c[1]:
+                turn = (112 if c[1] > 0 else 0) - 32 * k
+                v = joined(v, lanes(beside[h], turn) if turn % 128 else beside[h])
+            if shift:
+                v = lanes(v, shift)
+            if c[2]:
+                v = jnp.where(z_edge, lanes(columns[h], -k * c[2]) if k else columns[h], v)
+            dst[q, first + 8 * t : first + 8 * t + 8, :] = v
         if c[0]:
-            rolled = [subs(v, 4) for v in values]
-            if c[0] > 0:
-                values = [jnp.where(sub < 4, rolled[t - 1] if t else outside, rolled[t]) for t in range(TILES)]
-            else:
-                values = [
-                    jnp.where(sub >= 4, rolled[t + 1] if t < TILES - 1 else outside, rolled[t]) for t in range(TILES)
-                ]
-        for t in range(TILES):
-            dst[q, 8 * t : 8 * t + 8, :] = values[t]
+            v = jnp.where(yh == 1, planes[0][1], planes[0][0])
+            if c[1]:
+                v = lanes(joined(v, edge_row(q, e, 1 if c[1] > 0 else 0)), shift)
+            if c[2]:
+                line = jnp.where(yh == 1, edge_row(q, e, 1), edge_row(q, e, 0))
+                v = jnp.where(z_edge, lanes(line, -15 * c[2]), lanes(v, shift))
+            r = 8 if c[0] > 0 else 68
+            dst[q, r : r + 4, :] = v[:4]
         done(q)
 
 
@@ -330,7 +338,7 @@
 
     @pl.when(level >= 1)
     def _():
-        collide(pops, star, mask, relax_rate(level), lambda t: parts[t].wait())
+        collide(pops, 0, star, mask, relax_rate(level), lambda t: parts[t].wait())
 
     @pl.when(level < 1)
     def _():
@@ -352,22 +360,31 @@
     copy.wait()
 
 
-def middle_kernel(sizes, plan_ref, star, mask, own, chip, near, far, dst, out, plan, table, halo, sems):
+def middle_kernel(sizes, plan_ref, star, mask, own, chip, near, far, dst, out, plan, table, halo, moved, sems):
     gathered(plan_ref, plan, sems.at[0], (own, chip, near, far), table)
     level = plan[0, 64]
 
     @pl.when(level >= 1)
     def _():
         arrived(plan, 0, table, halo, sizes[2])
-        stream(star, dst, plan, 0, table, halo, sizes[2], nothing)
+
+        @pl.when(plan[0, 65] > 0)
+        def _():
+            arrived_fine(plan, 0, table, halo, sizes[2])
+
+        stream(star, moved, plan, 0, table, halo, sizes[2], nothing)
 
     @pl.when(level < 1)
     def _():
         dst[...] = star[...]
 
+    @pl.when(level == 1)
+    def _():
+        dst[...] = moved[:, 8 : 8 + ROWS, :]
+
     @pl.when(level == 2)
     def _():
-        collide(dst, dst, mask, relax_rate(level), nothing)
+        collide(moved, 8, dst, mask, relax_rate(level), nothing)
 
     export(dst, out)
 
@@ -378,7 +395,9 @@
 
     @pl.when(level == 2)
     def _():
-        copies = [pltpu.make_async_copy(moved.at[q], result.at[q], sems.at[q]) for q in range(19)]
+        copies = [
+            pltpu.make_async_copy(moved.at[q, 8 : 8 + ROWS], result.at[q], sems.at[q]) for q in range(19)
+        ]
         arrived(plan, 32, table, halo, sizes[2])
         stream(star, moved, plan, 32, table, halo, sizes[2], lambda q: copies[q].start())
         for copy in copies:
@@ -479,6 +498,7 @@
             plan_scratch,
             pltpu.VMEM((3 * sections * blocks, ROWS, 128), jnp.float32),
             halo,
+            pltpu.VMEM((19, ROWS + 16, 128), jnp.float32),
             pltpu.SemaphoreType.DMA((1,)),
         ],
         compiler_params=params,
@@ -494,7 +514,7 @@
             plan_scratch,
             pltpu.VMEM((3 * (sections - 1) * blocks, ROWS, 128), jnp.float32),
             halo,
-            pltpu.VMEM(pops.shape, jnp.float32),
+            pltpu.VMEM((19, ROWS + 16, 128), jnp.float32),
             pltpu.SemaphoreType.DMA((20,)),
         ],
         compiler_params=params,

time: 34.5 us -> 37.1 us (1.075)
  Pallas kernels: 4.27 us -> 6.05 us
  starting transfers between devices: 12.6 us -> 13.4 us
    pallas_call x1, Pallas kernels: 0.98 us -> 1.88 us  [body(): pl.pallas_call(functools.partial(middle_kernel, sizes), out_shape=(field,...]
    pallas_call x1, Pallas kernels: 1.61 us -> 2.49 us  [body(): pl.pallas_call(functools.partial(first_kernel, sizes), out_shape=(field,...]
    ppermute x12, starting transfers between devices: 12.6 us -> 13.4 us  [swap(): return lax.ppermute(x, ('section', 'member'), pairs)]
where the time goes in v3:
time: 37.1 us; the launch traced here: 36.9 us
  waiting for transfers between devices  17.3 us (47%)
  starting transfers between devices  13.4 us (36%)
  Pallas kernels  6.05 us (16%)
    ppermute x12, waiting for transfers between devices, swap(): return lax.ppermute(x, ('section', 'member'), pairs)  17.3 us
    ppermute x12, starting transfers between devices, swap(): return lax.ppermute(x, ('section', 'member'), pairs)  13.4 us
    pallas_call x1, Pallas kernels, body(): pl.pallas_call(functools.partial(first_kernel, sizes), out_shape=(field,...  2.49 us
    pallas_call x1, Pallas kernels, body(): pl.pallas_call(functools.partial(middle_kernel, sizes), out_shape=(field,...  1.88 us
    pallas_call x1, Pallas kernels, body(): pl.pallas_call(functools.partial(last_kernel, sizes), out_shape=field, in...  1.68 us
  transfers between devices with their start and end apart: 12, of which 9 were waited for; matrix products, arithmetic and copies ran while one was open for 0% of the time, Pallas kernels for 0%

profile of v3, /device:TPU:0, one launch (start us, length us, event | category | flops | bytes accessed | tf_op | source)
XLA Modules:
  0.0 36.9 jit_solution(13878486815181714883)
XLA Ops:
  0.0 2.5 %first.1 = (f32[19,64,128]{2,1,0:T(8,128)S(1)}, f32[2,64,128]{2,1,0:T(8,128)S(1)}, s32[16,128]{1,0:T(8,128)S(1)}, s32[64,128]{1,0:T(8,128)S(1)}) custom-call(s32[4]{0:T(128)} %level_hbm.1, s32[2,18]{1,0:T(2,128)} %near_hbm.1, s32[2,4,6]{2,1,0:T(4,128)} %bitcast.18, f32[19,64,128]{2,1,0:T(8,128)} %bitcast.16, s32[64,128]{1,0:T(8,128)} %bitcast.17), custom_call_target="tpu_custom_call" | custom-call | tf_op jit(solution)/shard_map/first/pallas_call | solution.py:476
  2.5 3.1 %collective-permute-start = (f32[2,64,128]{2,1,0:T(8,128)S(1)}, f32[2,64,128]{2,1,0:T(8,128)S(1)}, u32[]{:S(2)}, u32[]{:S(2)}) collective-permute-start(f32[2,64,128]{2,1,0:T(8,128)S(1)} %get-tuple-element.14), channel_id=1, source_target_pairs={{0,8},{1,9},{2,10},{3,11},{4,12},{5,13},{6,14},{7,15},{8,0},{9,1},... | collective-permute-start | bytes 196616 | tf_op jit(solution)/shard_map/ppermute | solution.py:420
  5.7 1.5 %collective-permute-start.1 = (f32[2,64,128]{2,1,0:T(8,128)S(1)}, f32[2,64,128]{2,1,0:T(8,128)S(1)}, u32[]{:S(2)}, u32[]{:S(2)}) collective-permute-start(f32[2,64,128]{2,1,0:T(8,128)S(1)} %get-tuple-element.14), channel_id=1, source_target_pairs={{0,16},{1,17},{2,18},{3,19},{4,20},{5,21},{6,22},{7,23},{8,24},{9,... | collective-permute-start | bytes 196616 | tf_op jit(solution)/shard_map/ppermute | solution.py:420
  7.2 0.0 collective-permute-start.2
  7.2 0.8 %collective-permute-done = f32[2,64,128]{2,1,0:T(8,128)S(1)} collective-permute-done((f32[2,64,128]{2,1,0:T(8,128)S(1)}, f32[2,64,128]{2,1,0:T(8,128)S(1)}, u32[]{:S(2)}, u32[]{:S(2)}) %collective-permute-start) | collective-permute-done | bytes 65568 | tf_op jit(solution)/shard_map/ppermute | solution.py:420
  8.0 1.9 %collective-permute-done.1 = f32[2,64,128]{2,1,0:T(8,128)S(1)} collective-permute-done((f32[2,64,128]{2,1,0:T(8,128)S(1)}, f32[2,64,128]{2,1,0:T(8,128)S(1)}, u32[]{:S(2)}, u32[]{:S(2)}) %collective-permute-start.1) | collective-permute-done | bytes 65568 | tf_op jit(solution)/shard_map/ppermute | solution.py:420
  9.9 2.4 %collective-permute-done.2 = f32[2,64,128]{2,1,0:T(8,128)S(1)} collective-permute-done((f32[2,64,128]{2,1,0:T(8,128)S(1)}, f32[2,64,128]{2,1,0:T(8,128)S(1)}, u32[]{:S(2)}, u32[]{:S(2)}) %collective-permute-start.2) | collective-permute-done | bytes 65568 | tf_op jit(solution)/shard_map/ppermute | solution.py:420
  12.3 0.0 collective-permute-start.3
  12.4 0.6 %collective-permute-start.5 = (f32[4,64,128]{2,1,0:T(8,128)S(1)}, f32[4,64,128]{2,1,0:T(8,128)S(1)}, u32[]{:S(2)}, u32[]{:S(2)}) collective-permute-start(f32[4,64,128]{2,1,0:T(8,128)S(1)} %pad_maximum_fusion.2), channel_id=1, source_target_pairs={{0,8},{1,2},{2,1},{3,4},{4,3},{5,6},{6,5},{7,15},{8,0},{9,10},{10,... | collective-permute-start | bytes 393224 | tf_op jit(solution)/shard_map/ppermute | solution.py:420
  13.0 1.6 %collective-permute-start.4 = (f32[4,64,128]{2,1,0:T(8,128)S(1)}, f32[4,64,128]{2,1,0:T(8,128)S(1)}, u32[]{:S(2)}, u32[]{:S(2)}) collective-permute-start(f32[4,64,128]{2,1,0:T(8,128)S(1)} %pad_maximum_fusion.1), channel_id=1, source_target_pairs={{0,8},{1,2},{2,1},{3,4},{4,3},{5,6},{6,5},{7,15},{8,0},{9,10},{10,... | collective-permute-start | bytes 393224 | tf_op jit(solution)/shard_map/ppermute | solution.py:420
  14.5 2.9 %collective-permute-done.5.far = f32[4,64,128]{2,1,0:T(8,128)S(1)} collective-permute-done((f32[4,64,128]{2,1,0:T(8,128)S(1)}, f32[4,64,128]{2,1,0:T(8,128)S(1)}, u32[]{:S(2)}, u32[]{:S(2)}) %collective-permute-start.5) | collective-permute-done | bytes 131104 | tf_op jit(solution)/shard_map/ppermute | solution.py:420
  17.4 1.4 %collective-permute-done.4.near = f32[4,64,128]{2,1,0:T(8,128)S(1)} collective-permute-done((f32[4,64,128]{2,1,0:T(8,128)S(1)}, f32[4,64,128]{2,1,0:T(8,128)S(1)}, u32[]{:S(2)}, u32[]{:S(2)}) %collective-permute-start.4) | collective-permute-done | bytes 131104 | tf_op jit(solution)/shard_map/ppermute | solution.py:420
  18.8 0.0 collective-permute-done.3.chip
  18.8 1.9 %middle.1 = (f32[19,64,128]{2,1,0:T(8,128)S(1)}, f32[2,64,128]{2,1,0:T(8,128)S(1)}) custom-call(s32[16,128]{1,0:T(8,128)S(1)} %get-tuple-element.11.plan_ref, f32[19,64,128]{2,1,0:T(8,128)S(1)} %get-tuple-element.12.star, s32[64,128]{1,0:T(8,128)S(1)} %get-tuple-element.13.mask, f32[8,64,128]{2,1,0:T(8,128)S(1)} %constant_dynamic-update-slice_fusion.own, ...), custom_call_target="tpu_custom_call" | custom-call | tf_op jit(solution)/shard_map/middle/pallas_call | solution.py:492
  20.7 2.8 %collective-permute-start.7 = (f32[2,64,128]{2,1,0:T(8,128)S(1)}, f32[2,64,128]{2,1,0:T(8,128)S(1)}, u32[]{:S(2)}, u32[]{:S(2)}) collective-permute-start(f32[2,64,128]{2,1,0:T(8,128)S(1)} %get-tuple-element.16), channel_id=1, source_target_pairs={{0,16},{1,17},{2,18},{3,19},{4,20},{5,21},{6,22},{7,23},{8,24},{9,... | collective-permute-start | bytes 196616 | tf_op jit(solution)/shard_map/ppermute | solution.py:420
  23.5 1.7 %collective-permute-start.8 = (f32[2,64,128]{2,1,0:T(8,128)S(1)}, f32[2,64,128]{2,1,0:T(8,128)S(1)}, u32[]{:S(2)}, u32[]{:S(2)}) collective-permute-start(f32[2,64,128]{2,1,0:T(8,128)S(1)} %get-tuple-element.16), channel_id=1, source_target_pairs={{0,24},{1,25},{2,26},{3,27},{4,28},{5,29},{6,30},{7,31},{8,16},{9,... | collective-permute-start | bytes 196616 | tf_op jit(solution)/shard_map/ppermute | solution.py:420
  25.1 0.0 collective-permute-start.6
  25.1 0.6 %collective-permute-done.7 = f32[2,64,128]{2,1,0:T(8,128)S(1)} collective-permute-done((f32[2,64,128]{2,1,0:T(8,128)S(1)}, f32[2,64,128]{2,1,0:T(8,128)S(1)}, u32[]{:S(2)}, u32[]{:S(2)}) %collective-permute-start.7) | collective-permute-done | bytes 65568 | tf_op jit(solution)/shard_map/ppermute | solution.py:420
  25.7 2.9 %collective-permute-done.8 = f32[2,64,128]{2,1,0:T(8,128)S(1)} collective-permute-done((f32[2,64,128]{2,1,0:T(8,128)S(1)}, f32[2,64,128]{2,1,0:T(8,128)S(1)}, u32[]{:S(2)}, u32[]{:S(2)}) %collective-permute-start.8) | collective-permute-done | bytes 65568 | tf_op jit(solution)/shard_map/ppermute | solution.py:420
  28.6 0.7 %collective-permute-done.6 = f32[2,64,128]{2,1,0:T(8,128)S(1)} collective-permute-done((f32[2,64,128]{2,1,0:T(8,128)S(1)}, f32[2,64,128]{2,1,0:T(8,128)S(1)}, u32[]{:S(2)}, u32[]{:S(2)}) %collective-permute-start.6) | collective-permute-done | bytes 65568 | tf_op jit(solution)/shard_map/ppermute | solution.py:420
  29.4 0.1 collective-permute-start.9
  29.5 1.0 %collective-permute-start.10 = (f32[4,64,128]{2,1,0:T(8,128)S(1)}, f32[4,64,128]{2,1,0:T(8,128)S(1)}, u32[]{:S(2)}, u32[]{:S(2)}) collective-permute-start(f32[4,64,128]{2,1,0:T(8,128)S(1)} %pad_maximum_fusion.3), channel_id=1, source_target_pairs={{0,8},{1,2},{2,1},{3,4},{4,3},{5,6},{6,5},{7,15},{8,0},{9,10},{10,... | collective-permute-start | bytes 393224 | tf_op jit(solution)/shard_map/ppermute | solution.py:420
  30.5 1.1 %collective-permute-start.11 = (f32[2,64,128]{2,1,0:T(8,128)S(1)}, f32[2,64,128]{2,1,0:T(8,128)S(1)}, u32[]{:S(2)}, u32[]{:S(2)}) collective-permute-start(f32[2,64,128]{2,1,0:T(8,128)S(1)} %broadcast_select_fusion), channel_id=1, source_target_pairs={{0,8},{1,2},{2,1},{3,4},{4,3},{5,6},{6,5},{7,15},{8,0},{9,10},{10,... | collective-permute-start | bytes 196616 | tf_op jit(solution)/shard_map/ppermute | solution.py:420
  31.6 3.6 %collective-permute-done.11.far = f32[2,64,128]{2,1,0:T(8,128)S(1)} collective-permute-done((f32[2,64,128]{2,1,0:T(8,128)S(1)}, f32[2,64,128]{2,1,0:T(8,128)S(1)}, u32[]{:S(2)}, u32[]{:S(2)}) %collective-permute-start.11) | collective-permute-done | bytes 65568 | tf_op jit(solution)/shard_map/ppermute | solution.py:420
  35.2 0.0 collective-permute-done.10.near
  35.2 0.0 collective-permute-done.9.chip
  35.2 1.7 %last.1 = f32[19,64,128]{2,1,0:T(8,128)} custom-call(s32[16,128]{1,0:T(8,128)S(1)} %get-tuple-element.11.plan_ref, f32[19,64,128]{2,1,0:T(8,128)S(1)} %get-tuple-element.15.star, f32[6,64,128]{2,1,0:T(8,128)S(1)} %pad_maximum_fusion.own, f32[6,64,128]{2,1,0:T(8,128)S(1)} %collective-permute-done.9.chip, f32[4,64,128]{2,1,0:T(8,128)S(1)} %collective-permute-done.10.near, ...), custom_call_target="tpu_custom_call" | custom-call | tf_op jit(solution)/shard_map/last/pallas_call | solution.py:508
  (9 shorter events, 0.1 us)
Async XLA Ops:
  2.5 5.5 %collective-permute-start = (f32[2,64,128]{2,1,0:T(8,128)S(1)}, f32[2,64,128]{2,1,0:T(8,128)S(1)}, u32[]{:S(2)}, u32[]{:S(2)}) collective-permute-start(f32[2,64,128]{2,1,0:T(8,128)S(1)} %get-tuple-element.14), channel_id=1, source_target_pairs={{0,8},{1,9},{2,10},{3,11},{4,12},{5,13},{6,14},{7,15},{8,0},{9,1},... | collective-permute-start | bytes 196616 | tf_op jit(solution)/shard_map/ppermute | solution.py:420
  5.7 4.3 %collective-permute-start.1 = (f32[2,64,128]{2,1,0:T(8,128)S(1)}, f32[2,64,128]{2,1,0:T(8,128)S(1)}, u32[]{:S(2)}, u32[]{:S(2)}) collective-permute-start(f32[2,64,128]{2,1,0:T(8,128)S(1)} %get-tuple-element.14), channel_id=1, source_target_pairs={{0,16},{1,17},{2,18},{3,19},{4,20},{5,21},{6,22},{7,23},{8,24},{9,... | collective-permute-start | bytes 196616 | tf_op jit(solution)/shard_map/ppermute | solution.py:420
  7.2 5.2 %collective-permute-start.2 = (f32[2,64,128]{2,1,0:T(8,128)S(1)}, f32[2,64,128]{2,1,0:T(8,128)S(1)}, u32[]{:S(2)}, u32[]{:S(2)}) collective-permute-start(f32[2,64,128]{2,1,0:T(8,128)S(1)} %get-tuple-element.14), channel_id=1, source_target_pairs={{0,24},{1,25},{2,26},{3,27},{4,28},{5,29},{6,30},{7,31},{8,16},{9,... | collective-permute-start | bytes 196616 | tf_op jit(solution)/shard_map/ppermute | solution.py:420
  12.3 6.5 %collective-permute-start.3 = (f32[8,64,128]{2,1,0:T(8,128)S(1)}, f32[8,64,128]{2,1,0:T(8,128)S(1)}, u32[]{:S(2)}, u32[]{:S(2)}) collective-permute-start(f32[8,64,128]{2,1,0:T(8,128)S(1)} %constant_dynamic-update-slice_fusion.own), channel_id=1, source_target_pairs={{0,1},{1,0},{2,3},{3,2},{4,5},{5,4},{6,7},{7,6},{8,9},{9,8},{10,11... | collective-permute-start | bytes 786440 | tf_op jit(solution)/shard_map/ppermute | solution.py:420
  12.4 5.0 %collective-permute-start.5 = (f32[4,64,128]{2,1,0:T(8,128)S(1)}, f32[4,64,128]{2,1,0:T(8,128)S(1)}, u32[]{:S(2)}, u32[]{:S(2)}) collective-permute-start(f32[4,64,128]{2,1,0:T(8,128)S(1)} %pad_maximum_fusion.2), channel_id=1, source_target_pairs={{0,8},{1,2},{2,1},{3,4},{4,3},{5,6},{6,5},{7,15},{8,0},{9,10},{10,... | collective-permute-start | bytes 393224 | tf_op jit(solution)/shard_map/ppermute | solution.py:420
  13.0 5.8 %collective-permute-start.4 = (f32[4,64,128]{2,1,0:T(8,128)S(1)}, f32[4,64,128]{2,1,0:T(8,128)S(1)}, u32[]{:S(2)}, u32[]{:S(2)}) collective-permute-start(f32[4,64,128]{2,1,0:T(8,128)S(1)} %pad_maximum_fusion.1), channel_id=1, source_target_pairs={{0,8},{1,2},{2,1},{3,4},{4,3},{5,6},{6,5},{7,15},{8,0},{9,10},{10,... | collective-permute-start | bytes 393224 | tf_op jit(solution)/shard_map/ppermute | solution.py:420
  20.7 5.0 %collective-permute-start.7 = (f32[2,64,128]{2,1,0:T(8,128)S(1)}, f32[2,64,128]{2,1,0:T(8,128)S(1)}, u32[]{:S(2)}, u32[]{:S(2)}) collective-permute-start(f32[2,64,128]{2,1,0:T(8,128)S(1)} %get-tuple-element.16), channel_id=1, source_target_pairs={{0,16},{1,17},{2,18},{3,19},{4,20},{5,21},{6,22},{7,23},{8,24},{9,... | collective-permute-start | bytes 196616 | tf_op jit(solution)/shard_map/ppermute | solution.py:420
  23.5 5.2 %collective-permute-start.8 = (f32[2,64,128]{2,1,0:T(8,128)S(1)}, f32[2,64,128]{2,1,0:T(8,128)S(1)}, u32[]{:S(2)}, u32[]{:S(2)}) collective-permute-start(f32[2,64,128]{2,1,0:T(8,128)S(1)} %get-tuple-element.16), channel_id=1, source_target_pairs={{0,24},{1,25},{2,26},{3,27},{4,28},{5,29},{6,30},{7,31},{8,16},{9,... | collective-permute-start | bytes 196616 | tf_op jit(solution)/shard_map/ppermute | solution.py:420
  25.1 4.3 %collective-permute-start.6 = (f32[2,64,128]{2,1,0:T(8,128)S(1)}, f32[2,64,128]{2,1,0:T(8,128)S(1)}, u32[]{:S(2)}, u32[]{:S(2)}) collective-permute-start(f32[2,64,128]{2,1,0:T(8,128)S(1)} %get-tuple-element.16), channel_id=1, source_target_pairs={{0,8},{1,9},{2,10},{3,11},{4,12},{5,13},{6,14},{7,15},{8,0},{9,1},... | collective-permute-start | bytes 196616 | tf_op jit(solution)/shard_map/ppermute | solution.py:420
  29.4 5.8 %collective-permute-start.9 = (f32[6,64,128]{2,1,0:T(8,128)S(1)}, f32[6,64,128]{2,1,0:T(8,128)S(1)}, u32[]{:S(2)}, u32[]{:S(2)}) collective-permute-start(f32[6,64,128]{2,1,0:T(8,128)S(1)} %pad_maximum_fusion.own), channel_id=1, source_target_pairs={{0,1},{1,0},{2,3},{3,2},{4,5},{5,4},{6,7},{7,6},{8,9},{9,8},{10,11... | collective-permute-start | bytes 589832 | tf_op jit(solution)/shard_map/ppermute | solution.py:420
  29.5 5.7 %collective-permute-start.10 = (f32[4,64,128]{2,1,0:T(8,128)S(1)}, f32[4,64,128]{2,1,0:T(8,128)S(1)}, u32[]{:S(2)}, u32[]{:S(2)}) collective-permute-start(f32[4,64,128]{2,1,0:T(8,128)S(1)} %pad_maximum_fusion.3), channel_id=1, source_target_pairs={{0,8},{1,2},{2,1},{3,4},{4,3},{5,6},{6,5},{7,15},{8,0},{9,10},{10,... | collective-permute-start | bytes 393224 | tf_op jit(solution)/shard_map/ppermute | solution.py:420
  30.5 4.8 %collective-permute-start.11 = (f32[2,64,128]{2,1,0:T(8,128)S(1)}, f32[2,64,128]{2,1,0:T(8,128)S(1)}, u32[]{:S(2)}, u32[]{:S(2)}) collective-permute-start(f32[2,64,128]{2,1,0:T(8,128)S(1)} %broadcast_select_fusion), channel_id=1, source_target_pairs={{0,8},{1,2},{2,1},{3,4},{4,3},{5,6},{6,5},{7,15},{8,0},{9,10},{10,... | collective-permute-start | bytes 196616 | tf_op jit(solution)/shard_map/ppermute | solution.py:420

commit v4 on v3

--- a/solution.py
+++ b/solution.py
@@ -94,12 +94,11 @@
 def export(src, out):
     sub, lane = iotas()
     xl, yh = sub // 4, (sub // 2) % 2
-    z = lane & 15
     own_x = ((lane >> 4) & 1) == xl
     own_y = ((lane >> 3) & 1) == yh
     for j in range(6):
         axis, high = j // 2, j % 2 == 0
-        index = (lane & 7) * 16 + (15 - (lane >> 5) if high else lane >> 5)
+        index = (lane & 7) * 16 + (15 if high else 0)
         for i, q in enumerate(LISTS[j]):
             for h in range(2):
                 r = 10 * j + 5 * h + i
@@ -107,19 +106,16 @@
                     v = tile(src, q, TILES - 1 if high else 0)
                     first = (4 if high else 0) + 2 * h
                 elif axis == 1:
-                    v = None
-                    for k in range(4):
-                        part = lanes(tile(src, q, 4 * h + k), 32 * k + (16 if high else 0))
-                        v = part if v is None else jnp.where(lane >> 5 == k, part, v)
-                    v = jnp.where(xl == 1, lanes(v, 16), v)
+                    edge = (lane & 15) + (112 if high else 0)
+                    v = pick(tile(src, q, 4 * h), edge)
+                    for k in range(1, 4):
+                        v = jnp.where(lane >> 5 == k, pick(tile(src, q, 4 * h + k), edge), v)
                     v = jnp.where(own_x, v, subs(v, 4))
                     first = 2 if high else 0
                 else:
-                    v = tile(src, q, 4 * h)
+                    v = pick(tile(src, q, 4 * h), index)
                     for k in range(1, 4):
-                        part = lanes(tile(src, q, 4 * h + k), -k if high else k)
-                        v = jnp.where(z == (15 - k if high else k), part, v)
-                    v = pick(v, index)
+                        v = jnp.where(lane >> 5 == k, pick(tile(src, q, 4 * h + k), index), v)
                     v = jnp.where(own_x, v, subs(v, 4))
                     v = jnp.where(own_y, v, subs(v, 2))
                     first = 0
@@ -178,7 +174,7 @@
     plan[0:1, 65:66] = split
 
 
-def arrived(plan, base, table, halo, blocks):
+def arrived(plan, base, table, halo, blocks, fine):
     sub, lane = iotas()
     sub, lane = sub[:5], lane[:5]
 
@@ -204,7 +200,10 @@
             for h in range(2):
                 coarse = pick(lanes(source, 64) if h else source, spread)
                 value = jnp.where(kind == 0, rows(near, j, h), jnp.where(kind == 1, coarse, rest))
-                halo[block, 10 * j + 5 * h : 10 * j + 5 * h + 5, :] = value
+                r = 10 * j + 5 * h
+                if fine:
+                    value = jnp.where(kind == 2, halo[block, r : r + 5, :], value)
+                halo[block, r : r + 5, :] = value
 
 
 def arrived_fine(plan, base, table, halo, blocks):
@@ -214,7 +213,6 @@
     gather = (2 * ((lane >> 4) & 3) + (lane >> 6)) * 16 + 2 * (lane & 7) + ((lane >> 3) & 1)
     for block in range(blocks):
         for j in range(6):
-            kind = jnp.full((5, 128), plan[12 + block, base + j], jnp.int32)
             first = 10 * (j ^ 1)
             for a in range(2):
                 pairs = []
@@ -227,9 +225,8 @@
                         sums.append(v + lanes(v, 1 if b else -1))
                     v = jnp.where(odd_v, sums[1], sums[0])
                     pairs.append(v + lanes(v, 16 if h else -16))
-                value = pick(jnp.where(odd_u, pairs[1], pairs[0]), gather)
                 r = 10 * j + 5 * a
-                halo[block, r : r + 5, :] = jnp.where(kind == 2, value, halo[block, r : r + 5, :])
+                halo[block, r : r + 5, :] = pick(jnp.where(odd_u, pairs[1], pairs[0]), gather)
 
 
 def stream(src, dst, plan, base, table, halo, blocks, done):
@@ -317,62 +314,78 @@
     pass
 
 
-def first_kernel(sizes, level_hbm, near_hbm, link_hbm, pops_hbm, mask_hbm, star, out, plan, mask, level_ref, near, links, pops, sems):
-    me = (lax.axis_index("section"), lax.axis_index("member"))
+def first_kernel(level_hbm, pops_hbm, mask_hbm, star, out, mask, level_ref, pops, sems):
+    def part(t):
+        here = pl.ds(8 * t, 8)
+        return pltpu.make_async_copy(pops_hbm.at[:, here, :], pops.at[:, here, :], sems.at[t])
+
     small = [
         pltpu.make_async_copy(level_hbm, level_ref, sems.at[TILES]),
-        pltpu.make_async_copy(near_hbm, near, sems.at[TILES + 1]),
-        pltpu.make_async_copy(link_hbm, links, sems.at[TILES + 2]),
-        pltpu.make_async_copy(mask_hbm, mask, sems.at[TILES + 3]),
+        pltpu.make_async_copy(mask_hbm, mask, sems.at[TILES + 1]),
     ]
-    parts = [
-        pltpu.make_async_copy(pops_hbm.at[:, 8 * t : 8 * t + 8, :], pops.at[:, 8 * t : 8 * t + 8, :], sems.at[t])
-        for t in range(TILES)
-    ]
+    parts = [part(t) for t in range(TILES)]
     for copy in small + parts:
         copy.start()
     for copy in small:
         copy.wait()
-    level = level_ref[me[0]]
+    level = level_ref[lax.axis_index("section")]
+
+    @pl.when(level >= 1)
+    def _():
+        collide(pops, 0, star, mask, relax_rate(level), lambda t: parts[t].wait())
+
+    @pl.when(level < 1)
+    def _():
+        for copy in parts:
+            copy.wait()
+        star[...] = pops[...]
+
+    export(star, out)
+
+
+def plan_kernel(sizes, level_hbm, near_hbm, link_hbm, plan, level_ref, near, links, sems):
+    copies = [
+        pltpu.make_async_copy(level_hbm, level_ref, sems.at[0]),
+        pltpu.make_async_copy(near_hbm, near, sems.at[1]),
+        pltpu.make_async_copy(link_hbm, links, sems.at[2]),
+    ]
+    for copy in copies:
+        copy.start()
+    for copy in copies:
+        copy.wait()
+    me = (lax.axis_index("section"), lax.axis_index("member"))
     plan_rows(level_ref, near, links, plan, me, sizes)
 
-    @pl.when(level >= 1)
-    def _():
-        collide(pops, 0, star, mask, relax_rate(level), lambda t: parts[t].wait())
-
-    @pl.when(level < 1)
-    def _():
-        for t in range(TILES):
-            parts[t].wait()
-        star[...] = pops[...]
-
-    export(star, out)
-
-
-def gathered(plan_ref, plan, sem, parts, table):
-    copy = pltpu.make_async_copy(plan_ref, plan, sem)
-    copy.start()
+
+def gathered(parts, table):
     row = 0
     for part in parts:
         for k in range(part.shape[0]):
             table[row] = part[k]
             row += 1
-    copy.wait()
-
-
-def middle_kernel(sizes, plan_ref, star, mask, own, chip, near, far, dst, out, plan, table, halo, moved, sems):
-    gathered(plan_ref, plan, sems.at[0], (own, chip, near, far), table)
+
+
+def settle_kernel(plan, star, result, sems):
+    @pl.when(plan[0, 64] < 2)
+    def _():
+        copy = pltpu.make_async_copy(star, result, sems.at[0])
+        copy.start()
+        copy.wait()
+
+
+def middle_kernel(blocks, plan, star, mask, own, chip, near, far, dst, out, table, halo, moved):
     level = plan[0, 64]
 
     @pl.when(level >= 1)
     def _():
-        arrived(plan, 0, table, halo, sizes[2])
+        gathered((own, chip, near, far), table)
 
         @pl.when(plan[0, 65] > 0)
         def _():
-            arrived_fine(plan, 0, table, halo, sizes[2])
-
-        stream(star, moved, plan, 0, table, halo, sizes[2], nothing)
+            arrived_fine(plan, 0, table, halo, blocks)
+
+        arrived(plan, 0, table, halo, blocks, True)
+        stream(star, moved, plan, 0, table, halo, blocks, nothing)
 
     @pl.when(level < 1)
     def _():
@@ -389,25 +402,17 @@
     export(dst, out)
 
 
-def last_kernel(sizes, plan_ref, star, own, chip, near, far, result, plan, table, halo, moved, sems):
-    gathered(plan_ref, plan, sems.at[19], (own, chip, near, far), table)
-    level = plan[0, 64]
-
-    @pl.when(level == 2)
+def last_kernel(blocks, plan, star, own, chip, near, far, settled, result, table, halo, moved, sems):
+    @pl.when(plan[0, 64] == 2)
     def _():
         copies = [
             pltpu.make_async_copy(moved.at[q, 8 : 8 + ROWS], result.at[q], sems.at[q]) for q in range(19)
         ]
-        arrived(plan, 32, table, halo, sizes[2])
-        stream(star, moved, plan, 32, table, halo, sizes[2], lambda q: copies[q].start())
+        gathered((own, chip, near, far), table)
+        arrived(plan, 32, table, halo, blocks, False)
+        stream(star, moved, plan, 32, table, halo, blocks, lambda q: copies[q].start())
         for copy in copies:
             copy.wait()
-
-    @pl.when(level < 2)
-    def _():
-        copy = pltpu.make_async_copy(star, result, sems.at[0])
-        copy.start()
-        copy.wait()
 
 
 def swap(x, sections, members, target):
@@ -456,7 +461,6 @@
 
 
 VMEM = pl.BlockSpec(memory_space=pltpu.VMEM)
-ANY = pl.BlockSpec(memory_space=pl.ANY)
 HBM = pl.BlockSpec(memory_space=pltpu.HBM)
 
 
@@ -470,56 +474,74 @@
     links = interface.transpose(0, 2, 1)
     field = jax.ShapeDtypeStruct(pops.shape, jnp.float32)
     planes = jax.ShapeDtypeStruct((blocks, ROWS, 128), jnp.float32)
-    plan = jax.ShapeDtypeStruct((16, 128), jnp.int32)
-    plan_scratch = pltpu.SMEM((16, 128), jnp.int32)
     halo = pltpu.VMEM((blocks, ROWS, 128), jnp.float32)
-    star, exports, plan, mask = pl.pallas_call(
-        functools.partial(first_kernel, sizes),
-        out_shape=(field, planes, plan, jax.ShapeDtypeStruct(mask.shape, jnp.int32)),
-        in_specs=[HBM] * 5,
-        out_specs=(VMEM,) * 4,
+    moved = pltpu.VMEM((19, ROWS + 16, 128), jnp.float32)
+
+    def fixed(*values):
+        return tuple(pltpu.with_memory_space_constraint(x, pltpu.HBM) for x in values)
+
+    star, exports, mask = pl.pallas_call(
+        first_kernel,
+        out_shape=(field, planes, jax.ShapeDtypeStruct(mask.shape, jnp.int32)),
+        in_specs=[HBM] * 3,
+        out_specs=(VMEM,) * 3,
+        scratch_shapes=[
+            pltpu.SMEM(section_level.shape, jnp.int32),
+            pltpu.VMEM(pops.shape, jnp.float32),
+            pltpu.SemaphoreType.DMA((TILES + 2,)),
+        ],
+        compiler_params=params,
+        name="first",
+    )(*fixed(section_level, pops, mask))
+    plan = pl.pallas_call(
+        functools.partial(plan_kernel, sizes),
+        out_shape=jax.ShapeDtypeStruct((16, 128), jnp.int32),
+        in_specs=[HBM] * 3,
+        out_specs=VMEM,
         scratch_shapes=[
             pltpu.SMEM(section_level.shape, jnp.int32),
             pltpu.VMEM(neighbours.shape, jnp.int32),
             pltpu.VMEM(links.shape, jnp.int32),
-            pltpu.VMEM(pops.shape, jnp.float32),
-            pltpu.SemaphoreType.DMA((TILES + 4,)),
+            pltpu.SemaphoreType.DMA((3,)),
         ],
         compiler_params=params,
-        name="first",
-    )(*(pltpu.with_memory_space_constraint(x, pltpu.HBM) for x in (section_level, neighbours, links, pops, mask)))
+        name="plan",
+    )(*fixed(section_level, neighbours, links))
     parts = exchange(exports, sections, members, False)
     star, exports = pl.pallas_call(
-        functools.partial(middle_kernel, sizes),
+        functools.partial(middle_kernel, blocks),
         out_shape=(field, planes),
-        in_specs=[ANY] + [VMEM] * 6,
+        in_specs=[VMEM] * 7,
         out_specs=(VMEM, VMEM),
-        scratch_shapes=[
-            plan_scratch,
-            pltpu.VMEM((3 * sections * blocks, ROWS, 128), jnp.float32),
-            halo,
-            pltpu.VMEM((19, ROWS + 16, 128), jnp.float32),
-            pltpu.SemaphoreType.DMA((1,)),
-        ],
+        scratch_shapes=[pltpu.VMEM((3 * sections * blocks, ROWS, 128), jnp.float32), halo, moved],
         compiler_params=params,
         name="middle",
     )(plan, star, mask, *parts)
+    settled = pl.pallas_call(
+        settle_kernel,
+        out_shape=field,
+        in_specs=[VMEM] * 2,
+        out_specs=HBM,
+        scratch_shapes=[pltpu.SemaphoreType.DMA((1,))],
+        compiler_params=params,
+        name="settled",
+    )(plan, star)
     parts = exchange(exports, sections, members, True)
     result = pl.pallas_call(
-        functools.partial(last_kernel, sizes),
+        functools.partial(last_kernel, blocks),
         out_shape=field,
-        in_specs=[ANY] + [VMEM] * 5,
+        in_specs=[VMEM] * 6 + [HBM],
         out_specs=HBM,
+        input_output_aliases={6: 0},
         scratch_shapes=[
-            plan_scratch,
             pltpu.VMEM((3 * (sections - 1) * blocks, ROWS, 128), jnp.float32),
             halo,
-            pltpu.VMEM((19, ROWS + 16, 128), jnp.float32),
-            pltpu.SemaphoreType.DMA((20,)),
+            moved,
+            pltpu.SemaphoreType.DMA((19,)),
         ],
         compiler_params=params,
         name="last",
-    )(plan, star, *parts)
+    )(plan, star, *parts, settled)
     out = result.reshape(19, cells // 128, blocks, 128).transpose(2, 0, 1, 3)
     return out.reshape(blocks, 19, cells)
 

time: 37.1 us -> 32.2 us (0.87)
  the two profiles are of different devices: /device:TPU:0 before, /device:TPU:7 now
where the time goes in v4:
time: 32.2 us; the launch traced here: 32 us
  starting transfers between devices  13.2 us (41%)
  waiting for transfers between devices  12.2 us (38%)
  Pallas kernels  6.44 us (20%)
    ppermute x12, starting transfers between devices, swap(): return lax.ppermute(x, ('section', 'member'), pairs)  13.2 us
    ppermute x12, waiting for transfers between devices, swap(): return lax.ppermute(x, ('section', 'member'), pairs)  12.2 us
    pallas_call x1, Pallas kernels, body(): pl.pallas_call(functools.partial(last_kernel, blocks), out_shape=field, i...  2.04 us
    pallas_call x1, Pallas kernels, body(): pl.pallas_call(functools.partial(middle_kernel, blocks), out_shape=(field...  1.74 us
    pallas_call x1, Pallas kernels, body(): pl.pallas_call(first_kernel, out_shape=(field, planes, jax.ShapeDtypeStru...  1.64 us
    pallas_call x1, Pallas kernels, body(): pl.pallas_call(functools.partial(plan_kernel, sizes), out_shape=jax.Shape...  0.91 us
  transfers between devices with their start and end apart: 12, of which 7 were waited for; matrix products, arithmetic and copies ran while one was open for 0% of the time, Pallas kernels for 3%

profile of v4, /device:TPU:7, one launch (start us, length us, event | category | flops | bytes accessed | tf_op | source)
XLA Modules:
  0.0 32.0 jit_solution(17930287484359336771)
XLA Ops:
  0.0 1.6 %first.1 = (f32[19,64,128]{2,1,0:T(8,128)S(1)}, f32[2,64,128]{2,1,0:T(8,128)S(1)}, s32[64,128]{1,0:T(8,128)S(1)}) custom-call(s32[4]{0:T(128)} %level_hbm.3, f32[19,64,128]{2,1,0:T(8,128)} %bitcast.16, s32[64,128]{1,0:T(8,128)} %bitcast.17), custom_call_target="tpu_custom_call" | custom-call | tf_op jit(solution)/shard_map/first/pallas_call | solution.py:483
  1.6 0.1 collective-permute-start.2
  1.7 1.4 %collective-permute-start.1 = (f32[2,64,128]{2,1,0:T(8,128)S(1)}, f32[2,64,128]{2,1,0:T(8,128)S(1)}, u32[]{:S(2)}, u32[]{:S(2)}) collective-permute-start(f32[2,64,128]{2,1,0:T(8,128)S(1)} %get-tuple-element.12), channel_id=1, source_target_pairs={{0,16},{1,17},{2,18},{3,19},{4,20},{5,21},{6,22},{7,23},{8,24},{9,... | collective-permute-start | bytes 196616 | tf_op jit(solution)/shard_map/ppermute | solution.py:425
  3.1 1.2 %collective-permute-start = (f32[2,64,128]{2,1,0:T(8,128)S(1)}, f32[2,64,128]{2,1,0:T(8,128)S(1)}, u32[]{:S(2)}, u32[]{:S(2)}) collective-permute-start(f32[2,64,128]{2,1,0:T(8,128)S(1)} %get-tuple-element.12), channel_id=1, source_target_pairs={{0,8},{1,9},{2,10},{3,11},{4,12},{5,13},{6,14},{7,15},{8,0},{9,1},... | collective-permute-start | bytes 196616 | tf_op jit(solution)/shard_map/ppermute | solution.py:425
  4.4 2.5 %collective-permute-done = f32[2,64,128]{2,1,0:T(8,128)S(1)} collective-permute-done((f32[2,64,128]{2,1,0:T(8,128)S(1)}, f32[2,64,128]{2,1,0:T(8,128)S(1)}, u32[]{:S(2)}, u32[]{:S(2)}) %collective-permute-start) | collective-permute-done | bytes 65568 | tf_op jit(solution)/shard_map/ppermute | solution.py:425
  6.9 0.0 collective-permute-done.1
  6.9 0.0 collective-permute-done.2
  7.0 1.8 %collective-permute-start.3 = (f32[8,64,128]{2,1,0:T(8,128)S(1)}, f32[8,64,128]{2,1,0:T(8,128)S(1)}, u32[]{:S(2)}, u32[]{:S(2)}) collective-permute-start(f32[8,64,128]{2,1,0:T(8,128)S(1)} %constant_dynamic-update-slice_fusion.own), channel_id=1, source_target_pairs={{0,1},{1,0},{2,3},{3,2},{4,5},{5,4},{6,7},{7,6},{8,9},{9,8},{10,11... | collective-permute-start | bytes 786440 | tf_op jit(solution)/shard_map/ppermute | solution.py:425
  8.8 1.3 %collective-permute-start.5 = (f32[4,64,128]{2,1,0:T(8,128)S(1)}, f32[4,64,128]{2,1,0:T(8,128)S(1)}, u32[]{:S(2)}, u32[]{:S(2)}) collective-permute-start(f32[4,64,128]{2,1,0:T(8,128)S(1)} %pad_maximum_fusion.2), channel_id=1, source_target_pairs={{0,8},{1,2},{2,1},{3,4},{4,3},{5,6},{6,5},{7,15},{8,0},{9,10},{10,... | collective-permute-start | bytes 393224 | tf_op jit(solution)/shard_map/ppermute | solution.py:425
  10.1 0.6 %collective-permute-start.4 = (f32[4,64,128]{2,1,0:T(8,128)S(1)}, f32[4,64,128]{2,1,0:T(8,128)S(1)}, u32[]{:S(2)}, u32[]{:S(2)}) collective-permute-start(f32[4,64,128]{2,1,0:T(8,128)S(1)} %pad_maximum_fusion.1), channel_id=1, source_target_pairs={{0,8},{1,2},{2,1},{3,4},{4,3},{5,6},{6,5},{7,15},{8,0},{9,10},{10,... | collective-permute-start | bytes 393224 | tf_op jit(solution)/shard_map/ppermute | solution.py:425
  10.7 0.9 %plan.1 = s32[16,128]{1,0:T(8,128)S(1)} custom-call(s32[4]{0:T(128)} %level_hbm.3, s32[2,18]{1,0:T(2,128)} %near_hbm.1, s32[2,4,6]{2,1,0:T(4,128)} %bitcast.18), custom_call_target="tpu_custom_call" | custom-call | tf_op jit(solution)/shard_map/plan/pallas_call | solution.py:496
  11.6 1.8 %collective-permute-done.5.far = f32[4,64,128]{2,1,0:T(8,128)S(1)} collective-permute-done((f32[4,64,128]{2,1,0:T(8,128)S(1)}, f32[4,64,128]{2,1,0:T(8,128)S(1)}, u32[]{:S(2)}, u32[]{:S(2)}) %collective-permute-start.5) | collective-permute-done | bytes 131104 | tf_op jit(solution)/shard_map/ppermute | solution.py:425
  13.4 1.5 %collective-permute-done.4.near = f32[4,64,128]{2,1,0:T(8,128)S(1)} collective-permute-done((f32[4,64,128]{2,1,0:T(8,128)S(1)}, f32[4,64,128]{2,1,0:T(8,128)S(1)}, u32[]{:S(2)}, u32[]{:S(2)}) %collective-permute-start.4) | collective-permute-done | bytes 131104 | tf_op jit(solution)/shard_map/ppermute | solution.py:425
  14.9 0.0 collective-permute-done.3.chip
  14.9 1.7 %middle.1 = (f32[19,64,128]{2,1,0:T(8,128)S(1)}, f32[2,64,128]{2,1,0:T(8,128)S(1)}) custom-call(s32[16,128]{1,0:T(8,128)S(1)} %plan.1, f32[19,64,128]{2,1,0:T(8,128)S(1)} %get-tuple-element.10.star, s32[64,128]{1,0:T(8,128)S(1)} %get-tuple-element.11.mask, f32[8,64,128]{2,1,0:T(8,128)S(1)} %constant_dynamic-update-slice_fusion.own, ...), custom_call_target="tpu_custom_call" | custom-call | tf_op jit(solution)/shard_map/middle/pallas_call | solution.py:511
  16.7 0.1 collective-permute-start.8
  16.8 2.1 %collective-permute-start.7 = (f32[2,64,128]{2,1,0:T(8,128)S(1)}, f32[2,64,128]{2,1,0:T(8,128)S(1)}, u32[]{:S(2)}, u32[]{:S(2)}) collective-permute-start(f32[2,64,128]{2,1,0:T(8,128)S(1)} %get-tuple-element.14), channel_id=1, source_target_pairs={{0,16},{1,17},{2,18},{3,19},{4,20},{5,21},{6,22},{7,23},{8,24},{9,... | collective-permute-start | bytes 196616 | tf_op jit(solution)/shard_map/ppermute | solution.py:425
  18.8 0.6 %collective-permute-start.6 = (f32[2,64,128]{2,1,0:T(8,128)S(1)}, f32[2,64,128]{2,1,0:T(8,128)S(1)}, u32[]{:S(2)}, u32[]{:S(2)}) collective-permute-start(f32[2,64,128]{2,1,0:T(8,128)S(1)} %get-tuple-element.14), channel_id=1, source_target_pairs={{0,8},{1,9},{2,10},{3,11},{4,12},{5,13},{6,14},{7,15},{8,0},{9,1},... | collective-permute-start | bytes 196616 | tf_op jit(solution)/shard_map/ppermute | solution.py:425
  19.4 1.5 %collective-permute-done.8 = f32[2,64,128]{2,1,0:T(8,128)S(1)} collective-permute-done((f32[2,64,128]{2,1,0:T(8,128)S(1)}, f32[2,64,128]{2,1,0:T(8,128)S(1)}, u32[]{:S(2)}, u32[]{:S(2)}) %collective-permute-start.8) | collective-permute-done | bytes 65568 | tf_op jit(solution)/shard_map/ppermute | solution.py:425
  20.9 1.2 %collective-permute-done.7 = f32[2,64,128]{2,1,0:T(8,128)S(1)} collective-permute-done((f32[2,64,128]{2,1,0:T(8,128)S(1)}, f32[2,64,128]{2,1,0:T(8,128)S(1)}, u32[]{:S(2)}, u32[]{:S(2)}) %collective-permute-start.7) | collective-permute-done | bytes 65568 | tf_op jit(solution)/shard_map/ppermute | solution.py:425
  22.0 0.2 collective-permute-done.6
  22.3 2.3 %collective-permute-start.9 = (f32[6,64,128]{2,1,0:T(8,128)S(1)}, f32[6,64,128]{2,1,0:T(8,128)S(1)}, u32[]{:S(2)}, u32[]{:S(2)}) collective-permute-start(f32[6,64,128]{2,1,0:T(8,128)S(1)} %pad_maximum_fusion.own), channel_id=1, source_target_pairs={{0,1},{1,0},{2,3},{3,2},{4,5},{5,4},{6,7},{7,6},{8,9},{9,8},{10,11... | collective-permute-start | bytes 589832 | tf_op jit(solution)/shard_map/ppermute | solution.py:425
  24.6 0.7 %collective-permute-start.10 = (f32[4,64,128]{2,1,0:T(8,128)S(1)}, f32[4,64,128]{2,1,0:T(8,128)S(1)}, u32[]{:S(2)}, u32[]{:S(2)}) collective-permute-start(f32[4,64,128]{2,1,0:T(8,128)S(1)} %pad_maximum_fusion.3), channel_id=1, source_target_pairs={{0,8},{1,2},{2,1},{3,4},{4,3},{5,6},{6,5},{7,15},{8,0},{9,10},{10,... | collective-permute-start | bytes 393224 | tf_op jit(solution)/shard_map/ppermute | solution.py:425
  25.3 1.1 %collective-permute-start.11 = (f32[2,64,128]{2,1,0:T(8,128)S(1)}, f32[2,64,128]{2,1,0:T(8,128)S(1)}, u32[]{:S(2)}, u32[]{:S(2)}) collective-permute-start(f32[2,64,128]{2,1,0:T(8,128)S(1)} %broadcast_select_fusion), channel_id=1, source_target_pairs={{0,8},{1,2},{2,1},{3,4},{4,3},{5,6},{6,5},{7,15},{8,0},{9,10},{10,... | collective-permute-start | bytes 196616 | tf_op jit(solution)/shard_map/ppermute | solution.py:425
  26.4 0.1 settled.1
  26.5 3.4 %collective-permute-done.11.far = f32[2,64,128]{2,1,0:T(8,128)S(1)} collective-permute-done((f32[2,64,128]{2,1,0:T(8,128)S(1)}, f32[2,64,128]{2,1,0:T(8,128)S(1)}, u32[]{:S(2)}, u32[]{:S(2)}) %collective-permute-start.11) | collective-permute-done | bytes 65568 | tf_op jit(solution)/shard_map/ppermute | solution.py:425
  30.0 0.0 collective-permute-done.10.near
  30.0 0.0 collective-permute-done.9.chip
  30.0 2.0 %last.1 = f32[19,64,128]{2,1,0:T(8,128)} custom-call(s32[16,128]{1,0:T(8,128)S(1)} %plan.1, f32[19,64,128]{2,1,0:T(8,128)S(1)} %get-tuple-element.13.star, f32[6,64,128]{2,1,0:T(8,128)S(1)} %pad_maximum_fusion.own, f32[6,64,128]{2,1,0:T(8,128)S(1)} %collective-permute-done.9.chip, ...), custom_call_target="tpu_custom_call", output_to_operand_aliasing={{}: (6, {})} | custom-call | tf_op jit(solution)/shard_map/last/pallas_call | solution.py:530
  (9 shorter events, 0.1 us)
Async XLA Ops:
  1.6 5.3 %collective-permute-start.2 = (f32[2,64,128]{2,1,0:T(8,128)S(1)}, f32[2,64,128]{2,1,0:T(8,128)S(1)}, u32[]{:S(2)}, u32[]{:S(2)}) collective-permute-start(f32[2,64,128]{2,1,0:T(8,128)S(1)} %get-tuple-element.12), channel_id=1, source_target_pairs={{0,24},{1,25},{2,26},{3,27},{4,28},{5,29},{6,30},{7,31},{8,16},{9,... | collective-permute-start | bytes 196616 | tf_op jit(solution)/shard_map/ppermute | solution.py:425
  1.7 5.2 %collective-permute-start.1 = (f32[2,64,128]{2,1,0:T(8,128)S(1)}, f32[2,64,128]{2,1,0:T(8,128)S(1)}, u32[]{:S(2)}, u32[]{:S(2)}) collective-permute-start(f32[2,64,128]{2,1,0:T(8,128)S(1)} %get-tuple-element.12), channel_id=1, source_target_pairs={{0,16},{1,17},{2,18},{3,19},{4,20},{5,21},{6,22},{7,23},{8,24},{9,... | collective-permute-start | bytes 196616 | tf_op jit(solution)/shard_map/ppermute | solution.py:425
  3.1 3.8 %collective-permute-start = (f32[2,64,128]{2,1,0:T(8,128)S(1)}, f32[2,64,128]{2,1,0:T(8,128)S(1)}, u32[]{:S(2)}, u32[]{:S(2)}) collective-permute-start(f32[2,64,128]{2,1,0:T(8,128)S(1)} %get-tuple-element.12), channel_id=1, source_target_pairs={{0,8},{1,9},{2,10},{3,11},{4,12},{5,13},{6,14},{7,15},{8,0},{9,1},... | collective-permute-start | bytes 196616 | tf_op jit(solution)/shard_map/ppermute | solution.py:425
  7.0 8.0 %collective-permute-start.3 = (f32[8,64,128]{2,1,0:T(8,128)S(1)}, f32[8,64,128]{2,1,0:T(8,128)S(1)}, u32[]{:S(2)}, u32[]{:S(2)}) collective-permute-start(f32[8,64,128]{2,1,0:T(8,128)S(1)} %constant_dynamic-update-slice_fusion.own), channel_id=1, source_target_pairs={{0,1},{1,0},{2,3},{3,2},{4,5},{5,4},{6,7},{7,6},{8,9},{9,8},{10,11... | collective-permute-start | bytes 786440 | tf_op jit(solution)/shard_map/ppermute | solution.py:425
  8.8 4.7 %collective-permute-start.5 = (f32[4,64,128]{2,1,0:T(8,128)S(1)}, f32[4,64,128]{2,1,0:T(8,128)S(1)}, u32[]{:S(2)}, u32[]{:S(2)}) collective-permute-start(f32[4,64,128]{2,1,0:T(8,128)S(1)} %pad_maximum_fusion.2), channel_id=1, source_target_pairs={{0,8},{1,2},{2,1},{3,4},{4,3},{5,6},{6,5},{7,15},{8,0},{9,10},{10,... | collective-permute-start | bytes 393224 | tf_op jit(solution)/shard_map/ppermute | solution.py:425
  10.1 4.9 %collective-permute-start.4 = (f32[4,64,128]{2,1,0:T(8,128)S(1)}, f32[4,64,128]{2,1,0:T(8,128)S(1)}, u32[]{:S(2)}, u32[]{:S(2)}) collective-permute-start(f32[4,64,128]{2,1,0:T(8,128)S(1)} %pad_maximum_fusion.1), channel_id=1, source_target_pairs={{0,8},{1,2},{2,1},{3,4},{4,3},{5,6},{6,5},{7,15},{8,0},{9,10},{10,... | collective-permute-start | bytes 393224 | tf_op jit(solution)/shard_map/ppermute | solution.py:425
  16.7 4.2 %collective-permute-start.8 = (f32[2,64,128]{2,1,0:T(8,128)S(1)}, f32[2,64,128]{2,1,0:T(8,128)S(1)}, u32[]{:S(2)}, u32[]{:S(2)}) collective-permute-start(f32[2,64,128]{2,1,0:T(8,128)S(1)} %get-tuple-element.14), channel_id=1, source_target_pairs={{0,24},{1,25},{2,26},{3,27},{4,28},{5,29},{6,30},{7,31},{8,16},{9,... | collective-permute-start | bytes 196616 | tf_op jit(solution)/shard_map/ppermute | solution.py:425
  16.8 5.3 %collective-permute-start.7 = (f32[2,64,128]{2,1,0:T(8,128)S(1)}, f32[2,64,128]{2,1,0:T(8,128)S(1)}, u32[]{:S(2)}, u32[]{:S(2)}) collective-permute-start(f32[2,64,128]{2,1,0:T(8,128)S(1)} %get-tuple-element.14), channel_id=1, source_target_pairs={{0,16},{1,17},{2,18},{3,19},{4,20},{5,21},{6,22},{7,23},{8,24},{9,... | collective-permute-start | bytes 196616 | tf_op jit(solution)/shard_map/ppermute | solution.py:425
  18.8 3.4 %collective-permute-start.6 = (f32[2,64,128]{2,1,0:T(8,128)S(1)}, f32[2,64,128]{2,1,0:T(8,128)S(1)}, u32[]{:S(2)}, u32[]{:S(2)}) collective-permute-start(f32[2,64,128]{2,1,0:T(8,128)S(1)} %get-tuple-element.14), channel_id=1, source_target_pairs={{0,8},{1,9},{2,10},{3,11},{4,12},{5,13},{6,14},{7,15},{8,0},{9,1},... | collective-permute-start | bytes 196616 | tf_op jit(solution)/shard_map/ppermute | solution.py:425
  22.3 7.7 %collective-permute-start.9 = (f32[6,64,128]{2,1,0:T(8,128)S(1)}, f32[6,64,128]{2,1,0:T(8,128)S(1)}, u32[]{:S(2)}, u32[]{:S(2)}) collective-permute-start(f32[6,64,128]{2,1,0:T(8,128)S(1)} %pad_maximum_fusion.own), channel_id=1, source_target_pairs={{0,1},{1,0},{2,3},{3,2},{4,5},{5,4},{6,7},{7,6},{8,9},{9,8},{10,11... | collective-permute-start | bytes 589832 | tf_op jit(solution)/shard_map/ppermute | solution.py:425
  24.6 5.4 %collective-permute-start.10 = (f32[4,64,128]{2,1,0:T(8,128)S(1)}, f32[4,64,128]{2,1,0:T(8,128)S(1)}, u32[]{:S(2)}, u32[]{:S(2)}) collective-permute-start(f32[4,64,128]{2,1,0:T(8,128)S(1)} %pad_maximum_fusion.3), channel_id=1, source_target_pairs={{0,8},{1,2},{2,1},{3,4},{4,3},{5,6},{6,5},{7,15},{8,0},{9,10},{10,... | collective-permute-start | bytes 393224 | tf_op jit(solution)/shard_map/ppermute | solution.py:425
  25.3 4.7 %collective-permute-start.11 = (f32[2,64,128]{2,1,0:T(8,128)S(1)}, f32[2,64,128]{2,1,0:T(8,128)S(1)}, u32[]{:S(2)}, u32[]{:S(2)}) collective-permute-start(f32[2,64,128]{2,1,0:T(8,128)S(1)} %broadcast_select_fusion), channel_id=1, source_target_pairs={{0,8},{1,2},{2,1},{3,4},{4,3},{5,6},{6,5},{7,15},{8,0},{9,10},{10,... | collective-permute-start | bytes 196616 | tf_op jit(solution)/shard_map/ppermute | solution.py:425

commit v5 on v4

--- a/solution.py
+++ b/solution.py
@@ -20,6 +20,7 @@
     for j in range(6)
 ]
 ROWS = 64
+PLANES = 60
 TILES = 8
 
 
@@ -47,6 +48,20 @@
 
 def bulk(ref, row):
     return jnp.broadcast_to(ref[row : row + 1, :], (8, 128))
+
+
+def entry(row, lane):
+    column = lane if lane < 32 else lane - 14 if lane < 64 else lane - 28
+    return 16 * column + row
+
+
+def number(plan, row, lane):
+    return plan[entry(row, lane), 0]
+
+
+def spread_rows(plan, row, lane, height):
+    r = entry(row, lane)
+    return jnp.broadcast_to(plan[r : r + 1, :], (height, 128))
 
 
 def relax_rate(level):
@@ -120,7 +135,7 @@
                     v = jnp.where(own_y, v, subs(v, 2))
                     first = 0
                 for b in range(2):
-                    out[b, r : r + 1, :] = v[first + b : first + b + 1, :]
+                    out[PLANES * b + r : PLANES * b + r + 1, :] = v[first + b : first + b + 1, :]
 
 
 def divide(x, n):
@@ -182,16 +197,13 @@
         first = 10 * (j ^ 1) + 5 * part
         return table[slot, first : first + 5, :]
 
-    def whole(scalar):
-        return jnp.full((5, 128), scalar, jnp.int32)
-
     spread = (lane >> 5) * 16 + ((lane & 15) >> 1)
     for block in range(blocks):
         for j in range(6):
-            kind = whole(plan[12 + block, base + j])
-            near = jnp.maximum(plan[block, base + j], 0)
-            slot = jnp.maximum(plan[10 + block, base + j], 0)
-            quadrant = whole(plan[14 + block, base + j])
+            kind = spread_rows(plan, 12 + block, base + j, 5)
+            near = jnp.maximum(number(plan, block, base + j), 0)
+            slot = jnp.maximum(number(plan, 10 + block, base + j), 0)
+            quadrant = spread_rows(plan, 14 + block, base + j, 5)
             source = jnp.where(quadrant < 2, rows(slot, j, 0), rows(slot, j, 1))
             source = jnp.where((quadrant & 1) == 1, lanes(source, -8), source)
             rest = [WEIGHTS[q] for q in LISTS[j ^ 1]]
@@ -219,9 +231,11 @@
                 for h in range(2):
                     sums = []
                     for b in range(2):
-                        slot = plan[2 + 4 * block + 2 * a + b, base + j]
-                        scale = jnp.where(slot >= 0, jnp.float32(0.25), jnp.float32(0.0))
-                        v = table[jnp.maximum(slot, 0), first + 5 * h : first + 5 * h + 5, :] * scale
+                        place = 2 + 4 * block + 2 * a + b
+                        slot = jnp.maximum(number(plan, place, base + j), 0)
+                        named = spread_rows(plan, place, base + j, 5) >= 0
+                        scale = jnp.where(named, jnp.float32(0.25), jnp.float32(0.0))
+                        v = table[slot, first + 5 * h : first + 5 * h + 5, :] * scale
                         sums.append(v + lanes(v, 1 if b else -1))
                     v = jnp.where(odd_v, sums[1], sums[0])
                     pairs.append(v + lanes(v, 16 if h else -16))
@@ -248,9 +262,9 @@
         r = 10 * j + 5 * h + LISTS[j].index(q)
         found = []
         for block in range(blocks):
-            slot = plan[block, base + e]
-            good = jnp.full((8, 128), slot, jnp.int32) >= 0
-            found.append(jnp.where(good, bulk(table.at[jnp.maximum(slot, 0)], r), jnp.float32(WEIGHTS[q])))
+            slot = jnp.maximum(number(plan, block, base + e), 0)
+            good = spread_rows(plan, block, base + e, 8) >= 0
+            found.append(jnp.where(good, bulk(table.at[slot], r), jnp.float32(WEIGHTS[q])))
         return both(*found)
 
     for q in range(19):
@@ -343,7 +357,7 @@
     export(star, out)
 
 
-def plan_kernel(sizes, level_hbm, near_hbm, link_hbm, plan, level_ref, near, links, sems):
+def plan_kernel(sizes, level_hbm, near_hbm, link_hbm, plan, level_ref, near, links, packed_plan, sems):
     copies = [
         pltpu.make_async_copy(level_hbm, level_ref, sems.at[0]),
         pltpu.make_async_copy(near_hbm, near, sems.at[1]),
@@ -354,19 +368,22 @@
     for copy in copies:
         copy.wait()
     me = (lax.axis_index("section"), lax.axis_index("member"))
-    plan_rows(level_ref, near, links, plan, me, sizes)
+    plan_rows(level_ref, near, links, packed_plan, me, sizes)
+    for lane in [*range(18), *range(32, 50), 64, 65]:
+        r = entry(0, lane)
+        plan[r : r + 16, :] = jnp.broadcast_to(packed_plan[:, lane : lane + 1], (16, 128))
 
 
 def gathered(parts, table):
-    row = 0
+    slot = 0
     for part in parts:
-        for k in range(part.shape[0]):
-            table[row] = part[k]
-            row += 1
+        for r in range(0, part.shape[0], PLANES):
+            table[slot, :PLANES] = part[r : r + PLANES, :]
+            slot += 1
 
 
 def settle_kernel(plan, star, result, sems):
-    @pl.when(plan[0, 64] < 2)
+    @pl.when(number(plan, 0, 64) < 2)
     def _():
         copy = pltpu.make_async_copy(star, result, sems.at[0])
         copy.start()
@@ -374,13 +391,13 @@
 
 
 def middle_kernel(blocks, plan, star, mask, own, chip, near, far, dst, out, table, halo, moved):
-    level = plan[0, 64]
+    level = number(plan, 0, 64)
 
     @pl.when(level >= 1)
     def _():
         gathered((own, chip, near, far), table)
 
-        @pl.when(plan[0, 65] > 0)
+        @pl.when(number(plan, 0, 65) > 0)
         def _():
             arrived_fine(plan, 0, table, halo, blocks)
 
@@ -403,7 +420,7 @@
 
 
 def last_kernel(blocks, plan, star, own, chip, near, far, settled, result, table, halo, moved, sems):
-    @pl.when(plan[0, 64] == 2)
+    @pl.when(number(plan, 0, 64) == 2)
     def _():
         copies = [
             pltpu.make_async_copy(moved.at[q, 8 : 8 + ROWS], result.at[q], sems.at[q]) for q in range(19)
@@ -473,7 +490,7 @@
     mask = packed(fluid_mask)[0]
     links = interface.transpose(0, 2, 1)
     field = jax.ShapeDtypeStruct(pops.shape, jnp.float32)
-    planes = jax.ShapeDtypeStruct((blocks, ROWS, 128), jnp.float32)
+    planes = jax.ShapeDtypeStruct((blocks * PLANES, 128), jnp.float32)
     halo = pltpu.VMEM((blocks, ROWS, 128), jnp.float32)
     moved = pltpu.VMEM((19, ROWS + 16, 128), jnp.float32)
 
@@ -495,13 +512,14 @@
     )(*fixed(section_level, pops, mask))
     plan = pl.pallas_call(
         functools.partial(plan_kernel, sizes),
-        out_shape=jax.ShapeDtypeStruct((16, 128), jnp.int32),
+        out_shape=jax.ShapeDtypeStruct((16 * 38, 128), jnp.int32),
         in_specs=[HBM] * 3,
         out_specs=VMEM,
         scratch_shapes=[
             pltpu.SMEM(section_level.shape, jnp.int32),
             pltpu.VMEM(neighbours.shape, jnp.int32),
             pltpu.VMEM(links.shape, jnp.int32),
+            pltpu.VMEM((16, 128), jnp.int32),
             pltpu.SemaphoreType.DMA((3,)),
         ],
         compiler_params=params,

time: 32.2 us -> 30.9 us (0.960)
  the two profiles are of different devices: /device:TPU:7 before, /device:TPU:0 now
where the time goes in v5:
time: 30.9 us; the launch traced here: 30.7 us
  starting transfers between devices  13.3 us (43%)
  waiting for transfers between devices  13.1 us (42%)
  Pallas kernels  4.13 us (13%)
    ppermute x12, starting transfers between devices, swap(): return lax.ppermute(x, ('section', 'member'), pairs)  13.3 us
    ppermute x12, waiting for transfers between devices, swap(): return lax.ppermute(x, ('section', 'member'), pairs)  13.1 us
    pallas_call x1, Pallas kernels, body(): pl.pallas_call(first_kernel, out_shape=(field, planes, jax.ShapeDtypeStru...  1.56 us
    pallas_call x1, Pallas kernels, body(): pl.pallas_call(functools.partial(plan_kernel, sizes), out_shape=jax.Shape...  1.14 us
    pallas_call x1, Pallas kernels, body(): pl.pallas_call(settle_kernel, out_shape=field, in_specs=[VMEM] * 2, out_s...  0.87 us
  transfers between devices with their start and end apart: 12, of which 7 were waited for; matrix products, arithmetic and copies ran while one was open for 0% of the time, Pallas kernels for 7%

profile of v5, /device:TPU:0, one launch (start us, length us, event | category | flops | bytes accessed | tf_op | source)
XLA Modules:
  0.0 30.7 jit_solution(217323684632008092)
XLA Ops:
  0.0 1.6 %first.1 = (f32[19,64,128]{2,1,0:T(8,128)S(1)}, f32[120,128]{1,0:T(8,128)S(1)}, s32[64,128]{1,0:T(8,128)S(1)}) custom-call(s32[4]{0:T(128)} %level_hbm.3, f32[19,64,128]{2,1,0:T(8,128)} %bitcast.16, s32[64,128]{1,0:T(8,128)} %bitcast.17), custom_call_target="tpu_custom_call" | custom-call | tf_op jit(solution)/shard_map/first/pallas_call | solution.py:500
  1.6 4.1 %collective-permute-start.2 = (f32[120,128]{1,0:T(8,128)S(1)}, f32[120,128]{1,0:T(8,128)S(1)}, u32[]{:S(2)}, u32[]{:S(2)}) collective-permute-start(f32[120,128]{1,0:T(8,128)S(1)} %get-tuple-element.12), channel_id=1, source_target_pairs={{0,24},{1,25},{2,26},{3,27},{4,28},{5,29},{6,30},{7,31},{8,16},{9,... | collective-permute-start | bytes 184328 | tf_op jit(solution)/shard_map/ppermute | solution.py:442
  5.6 0.5 %collective-permute-start.1 = (f32[120,128]{1,0:T(8,128)S(1)}, f32[120,128]{1,0:T(8,128)S(1)}, u32[]{:S(2)}, u32[]{:S(2)}) collective-permute-start(f32[120,128]{1,0:T(8,128)S(1)} %get-tuple-element.12), channel_id=1, source_target_pairs={{0,16},{1,17},{2,18},{3,19},{4,20},{5,21},{6,22},{7,23},{8,24},{9,... | collective-permute-start | bytes 184328 | tf_op jit(solution)/shard_map/ppermute | solution.py:442
  6.1 0.1 collective-permute-start
  6.3 4.1 %collective-permute-done = f32[120,128]{1,0:T(8,128)S(1)} collective-permute-done((f32[120,128]{1,0:T(8,128)S(1)}, f32[120,128]{1,0:T(8,128)S(1)}, u32[]{:S(2)}, u32[]{:S(2)}) %collective-permute-start) | collective-permute-done | bytes 61472 | tf_op jit(solution)/shard_map/ppermute | solution.py:442
  10.4 0.0 collective-permute-done.1
  10.4 0.0 collective-permute-done.2
  10.4 0.1 collective-permute-start.3
  10.5 0.4 %collective-permute-start.5 = (f32[240,128]{1,0:T(8,128)S(1)}, f32[240,128]{1,0:T(8,128)S(1)}, u32[]{:S(2)}, u32[]{:S(2)}) collective-permute-start(f32[240,128]{1,0:T(8,128)S(1)} %pad_maximum_fusion.2), channel_id=1, source_target_pairs={{0,8},{1,2},{2,1},{3,4},{4,3},{5,6},{6,5},{7,15},{8,0},{9,10},{10,... | collective-permute-start | bytes 368648 | tf_op jit(solution)/shard_map/ppermute | solution.py:442
  10.9 1.8 %collective-permute-start.4 = (f32[240,128]{1,0:T(8,128)S(1)}, f32[240,128]{1,0:T(8,128)S(1)}, u32[]{:S(2)}, u32[]{:S(2)}) collective-permute-start(f32[240,128]{1,0:T(8,128)S(1)} %pad_maximum_fusion.1), channel_id=1, source_target_pairs={{0,8},{1,2},{2,1},{3,4},{4,3},{5,6},{6,5},{7,15},{8,0},{9,10},{10,... | collective-permute-start | bytes 368648 | tf_op jit(solution)/shard_map/ppermute | solution.py:442
  12.7 1.1 %plan.1 = s32[608,128]{1,0:T(8,128)S(1)} custom-call(s32[4]{0:T(128)} %level_hbm.3, s32[2,18]{1,0:T(2,128)} %near_hbm.1, s32[2,4,6]{2,1,0:T(4,128)} %bitcast.18), custom_call_target="tpu_custom_call" | custom-call | tf_op jit(solution)/shard_map/plan/pallas_call | solution.py:513
  13.8 1.6 %collective-permute-done.5.far = f32[240,128]{1,0:T(8,128)S(1)} collective-permute-done((f32[240,128]{1,0:T(8,128)S(1)}, f32[240,128]{1,0:T(8,128)S(1)}, u32[]{:S(2)}, u32[]{:S(2)}) %collective-permute-start.5) | collective-permute-done | bytes 122912 | tf_op jit(solution)/shard_map/ppermute | solution.py:442
  15.5 1.3 %collective-permute-done.4.near = f32[240,128]{1,0:T(8,128)S(1)} collective-permute-done((f32[240,128]{1,0:T(8,128)S(1)}, f32[240,128]{1,0:T(8,128)S(1)}, u32[]{:S(2)}, u32[]{:S(2)}) %collective-permute-start.4) | collective-permute-done | bytes 122912 | tf_op jit(solution)/shard_map/ppermute | solution.py:442
  16.8 0.0 collective-permute-done.3.chip
  16.8 0.4 %middle.1 = (f32[19,64,128]{2,1,0:T(8,128)S(1)}, f32[120,128]{1,0:T(8,128)S(1)}) custom-call(s32[608,128]{1,0:T(8,128)S(1)} %plan.1, f32[19,64,128]{2,1,0:T(8,128)S(1)} %get-tuple-element.10.star, s32[64,128]{1,0:T(8,128)S(1)} %get-tuple-element.11.mask, f32[480,128]{1,0:T(8,128)S(1)} %constant_dynamic-update-slice_fusion.own, ...), custom_call_target="tpu_custom_call" | custom-call | tf_op jit(solution)/shard_map/middle/pallas_call | solution.py:529
  17.1 2.8 %collective-permute-start.8 = (f32[120,128]{1,0:T(8,128)S(1)}, f32[120,128]{1,0:T(8,128)S(1)}, u32[]{:S(2)}, u32[]{:S(2)}) collective-permute-start(f32[120,128]{1,0:T(8,128)S(1)} %get-tuple-element.14), channel_id=1, source_target_pairs={{0,24},{1,25},{2,26},{3,27},{4,28},{5,29},{6,30},{7,31},{8,16},{9,... | collective-permute-start | bytes 184328 | tf_op jit(solution)/shard_map/ppermute | solution.py:442
  19.9 0.7 %collective-permute-start.7 = (f32[120,128]{1,0:T(8,128)S(1)}, f32[120,128]{1,0:T(8,128)S(1)}, u32[]{:S(2)}, u32[]{:S(2)}) collective-permute-start(f32[120,128]{1,0:T(8,128)S(1)} %get-tuple-element.14), channel_id=1, source_target_pairs={{0,16},{1,17},{2,18},{3,19},{4,20},{5,21},{6,22},{7,23},{8,24},{9,... | collective-permute-start | bytes 184328 | tf_op jit(solution)/shard_map/ppermute | solution.py:442
  20.6 0.7 %collective-permute-start.6 = (f32[120,128]{1,0:T(8,128)S(1)}, f32[120,128]{1,0:T(8,128)S(1)}, u32[]{:S(2)}, u32[]{:S(2)}) collective-permute-start(f32[120,128]{1,0:T(8,128)S(1)} %get-tuple-element.14), channel_id=1, source_target_pairs={{0,8},{1,9},{2,10},{3,11},{4,12},{5,13},{6,14},{7,15},{8,0},{9,1},... | collective-permute-start | bytes 184328 | tf_op jit(solution)/shard_map/ppermute | solution.py:442
  21.3 1.0 %collective-permute-done.8 = f32[120,128]{1,0:T(8,128)S(1)} collective-permute-done((f32[120,128]{1,0:T(8,128)S(1)}, f32[120,128]{1,0:T(8,128)S(1)}, u32[]{:S(2)}, u32[]{:S(2)}) %collective-permute-start.8) | collective-permute-done | bytes 61472 | tf_op jit(solution)/shard_map/ppermute | solution.py:442
  22.3 1.8 %collective-permute-done.7 = f32[120,128]{1,0:T(8,128)S(1)} collective-permute-done((f32[120,128]{1,0:T(8,128)S(1)}, f32[120,128]{1,0:T(8,128)S(1)}, u32[]{:S(2)}, u32[]{:S(2)}) %collective-permute-start.7) | collective-permute-done | bytes 61472 | tf_op jit(solution)/shard_map/ppermute | solution.py:442
  24.1 0.7 %collective-permute-done.6 = f32[120,128]{1,0:T(8,128)S(1)} collective-permute-done((f32[120,128]{1,0:T(8,128)S(1)}, f32[120,128]{1,0:T(8,128)S(1)}, u32[]{:S(2)}, u32[]{:S(2)}) %collective-permute-start.6) | collective-permute-done | bytes 61472 | tf_op jit(solution)/shard_map/ppermute | solution.py:442
  24.8 0.1 collective-permute-start.9
  24.9 0.8 %collective-permute-start.10 = (f32[240,128]{1,0:T(8,128)S(1)}, f32[240,128]{1,0:T(8,128)S(1)}, u32[]{:S(2)}, u32[]{:S(2)}) collective-permute-start(f32[240,128]{1,0:T(8,128)S(1)} %pad_maximum_fusion.3), channel_id=1, source_target_pairs={{0,8},{1,2},{2,1},{3,4},{4,3},{5,6},{6,5},{7,15},{8,0},{9,10},{10,... | collective-permute-start | bytes 368648 | tf_op jit(solution)/shard_map/ppermute | solution.py:442
  25.7 1.3 %collective-permute-start.11 = (f32[120,128]{1,0:T(8,128)S(1)}, f32[120,128]{1,0:T(8,128)S(1)}, u32[]{:S(2)}, u32[]{:S(2)}) collective-permute-start(f32[120,128]{1,0:T(8,128)S(1)} %broadcast_select_fusion), channel_id=1, source_target_pairs={{0,8},{1,2},{2,1},{3,4},{4,3},{5,6},{6,5},{7,15},{8,0},{9,10},{10,... | collective-permute-start | bytes 184328 | tf_op jit(solution)/shard_map/ppermute | solution.py:442
  27.0 0.9 %settled.1 = f32[19,64,128]{2,1,0:T(8,128)} custom-call(s32[608,128]{1,0:T(8,128)S(1)} %plan.1, f32[19,64,128]{2,1,0:T(8,128)S(1)} %get-tuple-element.13.star), custom_call_target="tpu_custom_call" | custom-call | tf_op jit(solution)/shard_map/settled/pallas_call | solution.py:538
  27.9 2.6 %collective-permute-done.11.far = f32[120,128]{1,0:T(8,128)S(1)} collective-permute-done((f32[120,128]{1,0:T(8,128)S(1)}, f32[120,128]{1,0:T(8,128)S(1)}, u32[]{:S(2)}, u32[]{:S(2)}) %collective-permute-start.11) | collective-permute-done | bytes 61472 | tf_op jit(solution)/shard_map/ppermute | solution.py:442
  30.5 0.0 collective-permute-done.10.near
  30.5 0.0 collective-permute-done.9.chip
  30.5 0.2 last.1
  (9 shorter events, 0.1 us)
Async XLA Ops:
  1.6 8.8 %collective-permute-start.2 = (f32[120,128]{1,0:T(8,128)S(1)}, f32[120,128]{1,0:T(8,128)S(1)}, u32[]{:S(2)}, u32[]{:S(2)}) collective-permute-start(f32[120,128]{1,0:T(8,128)S(1)} %get-tuple-element.12), channel_id=1, source_target_pairs={{0,24},{1,25},{2,26},{3,27},{4,28},{5,29},{6,30},{7,31},{8,16},{9,... | collective-permute-start | bytes 184328 | tf_op jit(solution)/shard_map/ppermute | solution.py:442
  5.6 4.7 %collective-permute-start.1 = (f32[120,128]{1,0:T(8,128)S(1)}, f32[120,128]{1,0:T(8,128)S(1)}, u32[]{:S(2)}, u32[]{:S(2)}) collective-permute-start(f32[120,128]{1,0:T(8,128)S(1)} %get-tuple-element.12), channel_id=1, source_target_pairs={{0,16},{1,17},{2,18},{3,19},{4,20},{5,21},{6,22},{7,23},{8,24},{9,... | collective-permute-start | bytes 184328 | tf_op jit(solution)/shard_map/ppermute | solution.py:442
  6.1 4.2 %collective-permute-start = (f32[120,128]{1,0:T(8,128)S(1)}, f32[120,128]{1,0:T(8,128)S(1)}, u32[]{:S(2)}, u32[]{:S(2)}) collective-permute-start(f32[120,128]{1,0:T(8,128)S(1)} %get-tuple-element.12), channel_id=1, source_target_pairs={{0,8},{1,9},{2,10},{3,11},{4,12},{5,13},{6,14},{7,15},{8,0},{9,1},... | collective-permute-start | bytes 184328 | tf_op jit(solution)/shard_map/ppermute | solution.py:442
  10.4 6.4 %collective-permute-start.3 = (f32[480,128]{1,0:T(8,128)S(1)}, f32[480,128]{1,0:T(8,128)S(1)}, u32[]{:S(2)}, u32[]{:S(2)}) collective-permute-start(f32[480,128]{1,0:T(8,128)S(1)} %constant_dynamic-update-slice_fusion.own), channel_id=1, source_target_pairs={{0,1},{1,0},{2,3},{3,2},{4,5},{5,4},{6,7},{7,6},{8,9},{9,8},{10,11... | collective-permute-start | bytes 737288 | tf_op jit(solution)/shard_map/ppermute | solution.py:442
  10.5 4.9 %collective-permute-start.5 = (f32[240,128]{1,0:T(8,128)S(1)}, f32[240,128]{1,0:T(8,128)S(1)}, u32[]{:S(2)}, u32[]{:S(2)}) collective-permute-start(f32[240,128]{1,0:T(8,128)S(1)} %pad_maximum_fusion.2), channel_id=1, source_target_pairs={{0,8},{1,2},{2,1},{3,4},{4,3},{5,6},{6,5},{7,15},{8,0},{9,10},{10,... | collective-permute-start | bytes 368648 | tf_op jit(solution)/shard_map/ppermute | solution.py:442
  10.9 5.9 %collective-permute-start.4 = (f32[240,128]{1,0:T(8,128)S(1)}, f32[240,128]{1,0:T(8,128)S(1)}, u32[]{:S(2)}, u32[]{:S(2)}) collective-permute-start(f32[240,128]{1,0:T(8,128)S(1)} %pad_maximum_fusion.1), channel_id=1, source_target_pairs={{0,8},{1,2},{2,1},{3,4},{4,3},{5,6},{6,5},{7,15},{8,0},{9,10},{10,... | collective-permute-start | bytes 368648 | tf_op jit(solution)/shard_map/ppermute | solution.py:442
  17.1 5.2 %collective-permute-start.8 = (f32[120,128]{1,0:T(8,128)S(1)}, f32[120,128]{1,0:T(8,128)S(1)}, u32[]{:S(2)}, u32[]{:S(2)}) collective-permute-start(f32[120,128]{1,0:T(8,128)S(1)} %get-tuple-element.14), channel_id=1, source_target_pairs={{0,24},{1,25},{2,26},{3,27},{4,28},{5,29},{6,30},{7,31},{8,16},{9,... | collective-permute-start | bytes 184328 | tf_op jit(solution)/shard_map/ppermute | solution.py:442
  19.9 4.2 %collective-permute-start.7 = (f32[120,128]{1,0:T(8,128)S(1)}, f32[120,128]{1,0:T(8,128)S(1)}, u32[]{:S(2)}, u32[]{:S(2)}) collective-permute-start(f32[120,128]{1,0:T(8,128)S(1)} %get-tuple-element.14), channel_id=1, source_target_pairs={{0,16},{1,17},{2,18},{3,19},{4,20},{5,21},{6,22},{7,23},{8,24},{9,... | collective-permute-start | bytes 184328 | tf_op jit(solution)/shard_map/ppermute | solution.py:442
  20.6 4.2 %collective-permute-start.6 = (f32[120,128]{1,0:T(8,128)S(1)}, f32[120,128]{1,0:T(8,128)S(1)}, u32[]{:S(2)}, u32[]{:S(2)}) collective-permute-start(f32[120,128]{1,0:T(8,128)S(1)} %get-tuple-element.14), channel_id=1, source_target_pairs={{0,8},{1,9},{2,10},{3,11},{4,12},{5,13},{6,14},{7,15},{8,0},{9,1},... | collective-permute-start | bytes 184328 | tf_op jit(solution)/shard_map/ppermute | solution.py:442
  24.8 5.7 %collective-permute-start.9 = (f32[360,128]{1,0:T(8,128)S(1)}, f32[360,128]{1,0:T(8,128)S(1)}, u32[]{:S(2)}, u32[]{:S(2)}) collective-permute-start(f32[360,128]{1,0:T(8,128)S(1)} %pad_maximum_fusion.own), channel_id=1, source_target_pairs={{0,1},{1,0},{2,3},{3,2},{4,5},{5,4},{6,7},{7,6},{8,9},{9,8},{10,11... | collective-permute-start | bytes 552968 | tf_op jit(solution)/shard_map/ppermute | solution.py:442
  24.9 5.6 %collective-permute-start.10 = (f32[240,128]{1,0:T(8,128)S(1)}, f32[240,128]{1,0:T(8,128)S(1)}, u32[]{:S(2)}, u32[]{:S(2)}) collective-permute-start(f32[240,128]{1,0:T(8,128)S(1)} %pad_maximum_fusion.3), channel_id=1, source_target_pairs={{0,8},{1,2},{2,1},{3,4},{4,3},{5,6},{6,5},{7,15},{8,0},{9,10},{10,... | collective-permute-start | bytes 368648 | tf_op jit(solution)/shard_map/ppermute | solution.py:442
  25.7 4.8 %collective-permute-start.11 = (f32[120,128]{1,0:T(8,128)S(1)}, f32[120,128]{1,0:T(8,128)S(1)}, u32[]{:S(2)}, u32[]{:S(2)}) collective-permute-start(f32[120,128]{1,0:T(8,128)S(1)} %broadcast_select_fusion), channel_id=1, source_target_pairs={{0,8},{1,2},{2,1},{3,4},{4,3},{5,6},{6,5},{7,15},{8,0},{9,10},{10,... | collective-permute-start | bytes 184328 | tf_op jit(solution)/shard_map/ppermute | solution.py:442

commit v6 on v5

--- a/solution.py
+++ b/solution.py
@@ -390,12 +390,12 @@
         copy.wait()
 
 
-def middle_kernel(blocks, plan, star, mask, own, chip, near, far, dst, out, table, halo, moved):
+def middle_kernel(blocks, plan, star, mask, own, own2, chip, chip2, near, far, dst, out, table, halo, moved):
     level = number(plan, 0, 64)
 
     @pl.when(level >= 1)
     def _():
-        gathered((own, chip, near, far), table)
+        gathered((own, own2, chip, chip2, near, far), table)
 
         @pl.when(number(plan, 0, 65) > 0)
         def _():
@@ -419,13 +419,13 @@
     export(dst, out)
 
 
-def last_kernel(blocks, plan, star, own, chip, near, far, settled, result, table, halo, moved, sems):
+def last_kernel(blocks, plan, star, own, own2, chip, chip2, near, far, settled, result, table, halo, moved, sems):
     @pl.when(number(plan, 0, 64) == 2)
     def _():
         copies = [
             pltpu.make_async_copy(moved.at[q, 8 : 8 + ROWS], result.at[q], sems.at[q]) for q in range(19)
         ]
-        gathered((own, chip, near, far), table)
+        gathered((own, own2, chip, chip2, near, far), table)
         arrived(plan, 32, table, halo, blocks, False)
         stream(star, moved, plan, 32, table, halo, blocks, lambda q: copies[q].start())
         for copy in copies:
@@ -448,11 +448,21 @@
     def named(x, target):
         return swap(x, sections, members, target)
 
+    def across(d):
+        def target(s, m):
+            low, high = min(s, s ^ d), max(s, s ^ d)
+            needed = low >= 1 if last else (low, high) != (0, sections - 1)
+            return (s ^ d, m) if needed else (s, m ^ 1)
+
+        return target
+
     def beside(s, m):
+        if last and s < 2:
+            return (s, m ^ 1)
         t = ((m + 1) ^ 1) - 1
         return (s, t) if 0 <= t < members else (s ^ 1, m)
 
-    parts = [exports] + [named(exports, lambda s, m, d=d: (s ^ d, m)) for d in range(1, sections)]
+    parts = [exports] + [named(exports, across(d)) for d in range(1, sections)]
     first = jnp.concatenate(parts[:2], axis=0)
     if last:
         second = []
@@ -464,11 +474,11 @@
         second = jnp.concatenate(second, axis=0)
     else:
         second = jnp.concatenate(parts[2:], axis=0)
-    own = jnp.concatenate([first, second], axis=0)
     near = named(first, beside)
     far = named(second, beside)
-    chip = named(own, lambda s, m: (s, m ^ 1))
-    return own, chip, near, far
+    chip = named(first, lambda s, m: (s, m ^ 1))
+    rest = named(second, lambda s, m: (s, m ^ 1))
+    return first, second, chip, rest, near, far
 
 
 def packed(x):
@@ -529,7 +539,7 @@
     star, exports = pl.pallas_call(
         functools.partial(middle_kernel, blocks),
         out_shape=(field, planes),
-        in_specs=[VMEM] * 7,
+        in_specs=[VMEM] * 9,
         out_specs=(VMEM, VMEM),
         scratch_shapes=[pltpu.VMEM((3 * sections * blocks, ROWS, 128), jnp.float32), halo, moved],
         compiler_params=params,
@@ -548,9 +558,9 @@
     result = pl.pallas_call(
         functools.partial(last_kernel, blocks),
         out_shape=field,
-        in_specs=[VMEM] * 6 + [HBM],
+        in_specs=[VMEM] * 8 + [HBM],
         out_specs=HBM,
-        input_output_aliases={6: 0},
+        input_output_aliases={8: 0},
         scratch_shapes=[
             pltpu.VMEM((3 * (sections - 1) * blocks, ROWS, 128), jnp.float32),
             halo,

time: 30.9 us -> 29.6 us (0.958)
  the two profiles are of different devices: /device:TPU:0 before, /device:TPU:6 now
where the time goes in v6:
time: 29.6 us; the launch traced here: 29.4 us
  waiting for transfers between devices  13.4 us (45%)
  starting transfers between devices  10.1 us (34%)
  Pallas kernels  5.77 us (19%)
    ppermute x14, waiting for transfers between devices, swap(): return lax.ppermute(x, ('section', 'member'), pairs)  13.4 us
    ppermute x14, starting transfers between devices, swap(): return lax.ppermute(x, ('section', 'member'), pairs)  10.1 us
    pallas_call x1, Pallas kernels, body(): pl.pallas_call(first_kernel, out_shape=(field, planes, jax.ShapeDtypeStru...  1.64 us
    pallas_call x1, Pallas kernels, body(): pl.pallas_call(functools.partial(last_kernel, blocks), out_shape=field, i...  1.63 us
    pallas_call x1, Pallas kernels, body(): pl.pallas_call(functools.partial(middle_kernel, blocks), out_shape=(field...  1.31 us
    pallas_call x1, Pallas kernels, body(): pl.pallas_call(functools.partial(plan_kernel, sizes), out_shape=jax.Shape...  1.14 us
  transfers between devices with their start and end apart: 14, of which 5 were waited for; matrix products, arithmetic and copies ran while one was open for 0% of the time, Pallas kernels for 4%

profile of v6, /device:TPU:6, one launch (start us, length us, event | category | flops | bytes accessed | tf_op | source)
XLA Modules:
  0.0 29.4 jit_solution(2284508562691076446)
XLA Ops:
  0.0 1.6 %first.1 = (f32[19,64,128]{2,1,0:T(8,128)S(1)}, f32[120,128]{1,0:T(8,128)S(1)}, s32[64,128]{1,0:T(8,128)S(1)}) custom-call(s32[4]{0:T(128)} %level_hbm.3, f32[19,64,128]{2,1,0:T(8,128)} %bitcast.16, s32[64,128]{1,0:T(8,128)} %bitcast.17), custom_call_target="tpu_custom_call" | custom-call | tf_op jit(solution)/shard_map/first/pallas_call | solution.py:510
  1.6 0.1 collective-permute-start.2
  1.7 2.0 %collective-permute-start.1 = (f32[120,128]{1,0:T(8,128)S(1)}, f32[120,128]{1,0:T(8,128)S(1)}, u32[]{:S(2)}, u32[]{:S(2)}) collective-permute-start(f32[120,128]{1,0:T(8,128)S(1)} %get-tuple-element.12), channel_id=1, source_target_pairs={{0,16},{1,17},{2,18},{3,19},{4,20},{5,21},{6,22},{7,23},{8,24},{9,... | collective-permute-start | bytes 184328 | tf_op jit(solution)/shard_map/ppermute | solution.py:442
  3.7 0.0 collective-permute-start
  3.7 4.2 %collective-permute-done = f32[120,128]{1,0:T(8,128)S(1)} collective-permute-done((f32[120,128]{1,0:T(8,128)S(1)}, f32[120,128]{1,0:T(8,128)S(1)}, u32[]{:S(2)}, u32[]{:S(2)}) %collective-permute-start) | collective-permute-done | bytes 61472 | tf_op jit(solution)/shard_map/ppermute | solution.py:442
  7.9 0.0 collective-permute-start.5
  7.9 1.7 %collective-permute-start.3 = (f32[240,128]{1,0:T(8,128)S(1)}, f32[240,128]{1,0:T(8,128)S(1)}, u32[]{:S(2)}, u32[]{:S(2)}) collective-permute-start(f32[240,128]{1,0:T(8,128)S(1)} %constant_dynamic-update-slice_fusion.own), channel_id=1, source_target_pairs={{0,1},{1,0},{2,3},{3,2},{4,5},{5,4},{6,7},{7,6},{8,9},{9,8},{10,11... | collective-permute-start | bytes 368648 | tf_op jit(solution)/shard_map/ppermute | solution.py:442
  9.6 0.0 collective-permute-done.1
  9.6 0.0 collective-permute-done.2
  9.7 0.4 %collective-permute-start.6 = (f32[240,128]{1,0:T(8,128)S(1)}, f32[240,128]{1,0:T(8,128)S(1)}, u32[]{:S(2)}, u32[]{:S(2)}) collective-permute-start(f32[240,128]{1,0:T(8,128)S(1)} %constant_dynamic-update-slice_fusion.2.own2), channel_id=1, source_target_pairs={{0,8},{1,2},{2,1},{3,4},{4,3},{5,6},{6,5},{7,15},{8,0},{9,10},{10,... | collective-permute-start | bytes 368648 | tf_op jit(solution)/shard_map/ppermute | solution.py:442
  10.1 1.4 %collective-permute-start.4 = (f32[240,128]{1,0:T(8,128)S(1)}, f32[240,128]{1,0:T(8,128)S(1)}, u32[]{:S(2)}, u32[]{:S(2)}) collective-permute-start(f32[240,128]{1,0:T(8,128)S(1)} %constant_dynamic-update-slice_fusion.2.own2), channel_id=1, source_target_pairs={{0,1},{1,0},{2,3},{3,2},{4,5},{5,4},{6,7},{7,6},{8,9},{9,8},{10,11... | collective-permute-start | bytes 368648 | tf_op jit(solution)/shard_map/ppermute | solution.py:442
  11.4 1.1 %plan.1 = s32[608,128]{1,0:T(8,128)S(1)} custom-call(s32[4]{0:T(128)} %level_hbm.3, s32[2,18]{1,0:T(2,128)} %near_hbm.1, s32[2,4,6]{2,1,0:T(4,128)} %bitcast.18), custom_call_target="tpu_custom_call" | custom-call | tf_op jit(solution)/shard_map/plan/pallas_call | solution.py:523
  12.6 0.2 collective-permute-done.5.near
  12.8 0.0 collective-permute-done.3.chip
  12.8 1.8 %collective-permute-done.6.far = f32[240,128]{1,0:T(8,128)S(1)} collective-permute-done((f32[240,128]{1,0:T(8,128)S(1)}, f32[240,128]{1,0:T(8,128)S(1)}, u32[]{:S(2)}, u32[]{:S(2)}) %collective-permute-start.6) | collective-permute-done | bytes 122912 | tf_op jit(solution)/shard_map/ppermute | solution.py:442
  14.6 0.0 collective-permute-done.4.chip2
  14.6 1.3 %middle.1 = (f32[19,64,128]{2,1,0:T(8,128)S(1)}, f32[120,128]{1,0:T(8,128)S(1)}) custom-call(s32[608,128]{1,0:T(8,128)S(1)} %plan.1, f32[19,64,128]{2,1,0:T(8,128)S(1)} %get-tuple-element.10.star, s32[64,128]{1,0:T(8,128)S(1)} %get-tuple-element.11.mask, f32[240,128]{1,0:T(8,128)S(1)} %constant_dynamic-update-slice_fusion.own, ...), custom_call_target="tpu_custom_call" | custom-call | tf_op jit(solution)/shard_map/middle/pallas_call | solution.py:539
  15.9 0.1 collective-permute-start.9
  16.0 2.0 %collective-permute-start.8 = (f32[120,128]{1,0:T(8,128)S(1)}, f32[120,128]{1,0:T(8,128)S(1)}, u32[]{:S(2)}, u32[]{:S(2)}) collective-permute-start(f32[120,128]{1,0:T(8,128)S(1)} %get-tuple-element.14), channel_id=1, source_target_pairs={{0,1},{1,0},{2,3},{3,2},{4,5},{5,4},{6,7},{7,6},{8,24},{9,25},{10,... | collective-permute-start | bytes 184328 | tf_op jit(solution)/shard_map/ppermute | solution.py:442
  18.0 0.0 collective-permute-start.7
  18.0 4.2 %collective-permute-done.7 = f32[120,128]{1,0:T(8,128)S(1)} collective-permute-done((f32[120,128]{1,0:T(8,128)S(1)}, f32[120,128]{1,0:T(8,128)S(1)}, u32[]{:S(2)}, u32[]{:S(2)}) %collective-permute-start.7) | collective-permute-done | bytes 61472 | tf_op jit(solution)/shard_map/ppermute | solution.py:442
  22.2 0.2 collective-permute-start.12
  22.4 0.6 %collective-permute-start.10 = (f32[240,128]{1,0:T(8,128)S(1)}, f32[240,128]{1,0:T(8,128)S(1)}, u32[]{:S(2)}, u32[]{:S(2)}) collective-permute-start(f32[240,128]{1,0:T(8,128)S(1)} %constant_dynamic-update-slice_fusion.4.own), channel_id=1, source_target_pairs={{0,1},{1,0},{2,3},{3,2},{4,5},{5,4},{6,7},{7,6},{8,9},{9,8},{10,11... | collective-permute-start | bytes 368648 | tf_op jit(solution)/shard_map/ppermute | solution.py:442
  23.0 0.0 collective-permute-done.9
  23.0 0.0 collective-permute-done.8
  23.0 1.3 %collective-permute-start.13 = (f32[120,128]{1,0:T(8,128)S(1)}, f32[120,128]{1,0:T(8,128)S(1)}, u32[]{:S(2)}, u32[]{:S(2)}) collective-permute-start(f32[120,128]{1,0:T(8,128)S(1)} %broadcast_select_fusion.own2), channel_id=1, source_target_pairs={{0,1},{1,0},{2,3},{3,2},{4,5},{5,4},{6,7},{7,6},{8,9},{9,8},{10,11... | collective-permute-start | bytes 184328 | tf_op jit(solution)/shard_map/ppermute | solution.py:442
  24.3 0.4 %collective-permute-start.11 = (f32[120,128]{1,0:T(8,128)S(1)}, f32[120,128]{1,0:T(8,128)S(1)}, u32[]{:S(2)}, u32[]{:S(2)}) collective-permute-start(f32[120,128]{1,0:T(8,128)S(1)} %broadcast_select_fusion.own2), channel_id=1, source_target_pairs={{0,1},{1,0},{2,3},{3,2},{4,5},{5,4},{6,7},{7,6},{8,9},{9,8},{10,11... | collective-permute-start | bytes 184328 | tf_op jit(solution)/shard_map/ppermute | solution.py:442
  24.8 2.9 %collective-permute-done.13.far = f32[120,128]{1,0:T(8,128)S(1)} collective-permute-done((f32[120,128]{1,0:T(8,128)S(1)}, f32[120,128]{1,0:T(8,128)S(1)}, u32[]{:S(2)}, u32[]{:S(2)}) %collective-permute-start.13) | collective-permute-done | bytes 61472 | tf_op jit(solution)/shard_map/ppermute | solution.py:442
  27.7 0.0 collective-permute-done.11.chip2
  27.7 0.0 collective-permute-done.12.near
  27.7 0.0 collective-permute-done.10.chip
  27.8 1.6 %last.1 = f32[19,64,128]{2,1,0:T(8,128)} custom-call(s32[608,128]{1,0:T(8,128)S(1)} %plan.1, f32[19,64,128]{2,1,0:T(8,128)S(1)} %get-tuple-element.13.star, f32[240,128]{1,0:T(8,128)S(1)} %constant_dynamic-update-slice_fusion.4.own, f32[120,128]{1,0:T(8,128)S(1)} %broadcast_select_fusion.own2, ...), custom_call_target="tpu_custom_call", output_to_operand_aliasing={{}: (8, {})} | custom-call | tf_op jit(solution)/shard_map/last/pallas_call | solution.py:558
  (8 shorter events, 0.1 us)
Async XLA Ops:
  1.6 8.0 %collective-permute-start.2 = (f32[120,128]{1,0:T(8,128)S(1)}, f32[120,128]{1,0:T(8,128)S(1)}, u32[]{:S(2)}, u32[]{:S(2)}) collective-permute-start(f32[120,128]{1,0:T(8,128)S(1)} %get-tuple-element.12), channel_id=1, source_target_pairs={{0,1},{1,0},{2,3},{3,2},{4,5},{5,4},{6,7},{7,6},{8,16},{9,17},{10,... | collective-permute-start | bytes 184328 | tf_op jit(solution)/shard_map/ppermute | solution.py:442
  1.7 7.9 %collective-permute-start.1 = (f32[120,128]{1,0:T(8,128)S(1)}, f32[120,128]{1,0:T(8,128)S(1)}, u32[]{:S(2)}, u32[]{:S(2)}) collective-permute-start(f32[120,128]{1,0:T(8,128)S(1)} %get-tuple-element.12), channel_id=1, source_target_pairs={{0,16},{1,17},{2,18},{3,19},{4,20},{5,21},{6,22},{7,23},{8,24},{9,... | collective-permute-start | bytes 184328 | tf_op jit(solution)/shard_map/ppermute | solution.py:442
  3.7 4.2 %collective-permute-start = (f32[120,128]{1,0:T(8,128)S(1)}, f32[120,128]{1,0:T(8,128)S(1)}, u32[]{:S(2)}, u32[]{:S(2)}) collective-permute-start(f32[120,128]{1,0:T(8,128)S(1)} %get-tuple-element.12), channel_id=1, source_target_pairs={{0,8},{1,9},{2,10},{3,11},{4,12},{5,13},{6,14},{7,15},{8,0},{9,1},... | collective-permute-start | bytes 184328 | tf_op jit(solution)/shard_map/ppermute | solution.py:442
  7.9 4.9 %collective-permute-start.5 = (f32[240,128]{1,0:T(8,128)S(1)}, f32[240,128]{1,0:T(8,128)S(1)}, u32[]{:S(2)}, u32[]{:S(2)}) collective-permute-start(f32[240,128]{1,0:T(8,128)S(1)} %constant_dynamic-update-slice_fusion.own), channel_id=1, source_target_pairs={{0,8},{1,2},{2,1},{3,4},{4,3},{5,6},{6,5},{7,15},{8,0},{9,10},{10,... | collective-permute-start | bytes 368648 | tf_op jit(solution)/shard_map/ppermute | solution.py:442
  7.9 4.9 %collective-permute-start.3 = (f32[240,128]{1,0:T(8,128)S(1)}, f32[240,128]{1,0:T(8,128)S(1)}, u32[]{:S(2)}, u32[]{:S(2)}) collective-permute-start(f32[240,128]{1,0:T(8,128)S(1)} %constant_dynamic-update-slice_fusion.own), channel_id=1, source_target_pairs={{0,1},{1,0},{2,3},{3,2},{4,5},{5,4},{6,7},{7,6},{8,9},{9,8},{10,11... | collective-permute-start | bytes 368648 | tf_op jit(solution)/shard_map/ppermute | solution.py:442
  9.7 4.9 %collective-permute-start.6 = (f32[240,128]{1,0:T(8,128)S(1)}, f32[240,128]{1,0:T(8,128)S(1)}, u32[]{:S(2)}, u32[]{:S(2)}) collective-permute-start(f32[240,128]{1,0:T(8,128)S(1)} %constant_dynamic-update-slice_fusion.2.own2), channel_id=1, source_target_pairs={{0,8},{1,2},{2,1},{3,4},{4,3},{5,6},{6,5},{7,15},{8,0},{9,10},{10,... | collective-permute-start | bytes 368648 | tf_op jit(solution)/shard_map/ppermute | solution.py:442
  10.1 4.5 %collective-permute-start.4 = (f32[240,128]{1,0:T(8,128)S(1)}, f32[240,128]{1,0:T(8,128)S(1)}, u32[]{:S(2)}, u32[]{:S(2)}) collective-permute-start(f32[240,128]{1,0:T(8,128)S(1)} %constant_dynamic-update-slice_fusion.2.own2), channel_id=1, source_target_pairs={{0,1},{1,0},{2,3},{3,2},{4,5},{5,4},{6,7},{7,6},{8,9},{9,8},{10,11... | collective-permute-start | bytes 368648 | tf_op jit(solution)/shard_map/ppermute | solution.py:442
  15.9 7.1 %collective-permute-start.9 = (f32[120,128]{1,0:T(8,128)S(1)}, f32[120,128]{1,0:T(8,128)S(1)}, u32[]{:S(2)}, u32[]{:S(2)}) collective-permute-start(f32[120,128]{1,0:T(8,128)S(1)} %get-tuple-element.14), channel_id=1, source_target_pairs={{0,1},{1,0},{2,3},{3,2},{4,5},{5,4},{6,7},{7,6},{8,16},{9,17},{10,... | collective-permute-start | bytes 184328 | tf_op jit(solution)/shard_map/ppermute | solution.py:442
  16.0 7.0 %collective-permute-start.8 = (f32[120,128]{1,0:T(8,128)S(1)}, f32[120,128]{1,0:T(8,128)S(1)}, u32[]{:S(2)}, u32[]{:S(2)}) collective-permute-start(f32[120,128]{1,0:T(8,128)S(1)} %get-tuple-element.14), channel_id=1, source_target_pairs={{0,1},{1,0},{2,3},{3,2},{4,5},{5,4},{6,7},{7,6},{8,24},{9,25},{10,... | collective-permute-start | bytes 184328 | tf_op jit(solution)/shard_map/ppermute | solution.py:442
  18.0 4.2 %collective-permute-start.7 = (f32[120,128]{1,0:T(8,128)S(1)}, f32[120,128]{1,0:T(8,128)S(1)}, u32[]{:S(2)}, u32[]{:S(2)}) collective-permute-start(f32[120,128]{1,0:T(8,128)S(1)} %get-tuple-element.14), channel_id=1, source_target_pairs={{0,1},{1,0},{2,3},{3,2},{4,5},{5,4},{6,7},{7,6},{8,9},{9,8},{10,11... | collective-permute-start | bytes 184328 | tf_op jit(solution)/shard_map/ppermute | solution.py:442
  22.2 5.5 %collective-permute-start.12 = (f32[240,128]{1,0:T(8,128)S(1)}, f32[240,128]{1,0:T(8,128)S(1)}, u32[]{:S(2)}, u32[]{:S(2)}) collective-permute-start(f32[240,128]{1,0:T(8,128)S(1)} %constant_dynamic-update-slice_fusion.4.own), channel_id=1, source_target_pairs={{0,1},{1,0},{2,3},{3,2},{4,5},{5,4},{6,7},{7,6},{8,9},{9,8},{10,11... | collective-permute-start | bytes 368648 | tf_op jit(solution)/shard_map/ppermute | solution.py:442
  22.4 5.4 %collective-permute-start.10 = (f32[240,128]{1,0:T(8,128)S(1)}, f32[240,128]{1,0:T(8,128)S(1)}, u32[]{:S(2)}, u32[]{:S(2)}) collective-permute-start(f32[240,128]{1,0:T(8,128)S(1)} %constant_dynamic-update-slice_fusion.4.own), channel_id=1, source_target_pairs={{0,1},{1,0},{2,3},{3,2},{4,5},{5,4},{6,7},{7,6},{8,9},{9,8},{10,11... | collective-permute-start | bytes 368648 | tf_op jit(solution)/shard_map/ppermute | solution.py:442
  23.0 4.7 %collective-permute-start.13 = (f32[120,128]{1,0:T(8,128)S(1)}, f32[120,128]{1,0:T(8,128)S(1)}, u32[]{:S(2)}, u32[]{:S(2)}) collective-permute-start(f32[120,128]{1,0:T(8,128)S(1)} %broadcast_select_fusion.own2), channel_id=1, source_target_pairs={{0,1},{1,0},{2,3},{3,2},{4,5},{5,4},{6,7},{7,6},{8,9},{9,8},{10,11... | collective-permute-start | bytes 184328 | tf_op jit(solution)/shard_map/ppermute | solution.py:442
  24.3 3.4 %collective-permute-start.11 = (f32[120,128]{1,0:T(8,128)S(1)}, f32[120,128]{1,0:T(8,128)S(1)}, u32[]{:S(2)}, u32[]{:S(2)}) collective-permute-start(f32[120,128]{1,0:T(8,128)S(1)} %broadcast_select_fusion.own2), channel_id=1, source_target_pairs={{0,1},{1,0},{2,3},{3,2},{4,5},{5,4},{6,7},{7,6},{8,9},{9,8},{10,11... | collective-permute-start | bytes 184328 | tf_op jit(solution)/shard_map/ppermute | solution.py:442

commit v7 on v6

--- a/solution.py
+++ b/solution.py
@@ -330,14 +330,14 @@
 
 def first_kernel(level_hbm, pops_hbm, mask_hbm, star, out, mask, level_ref, pops, sems):
     def part(t):
-        here = pl.ds(8 * t, 8)
+        here = pl.ds(64 * t, 64)
         return pltpu.make_async_copy(pops_hbm.at[:, here, :], pops.at[:, here, :], sems.at[t])
 
     small = [
         pltpu.make_async_copy(level_hbm, level_ref, sems.at[TILES]),
         pltpu.make_async_copy(mask_hbm, mask, sems.at[TILES + 1]),
     ]
-    parts = [part(t) for t in range(TILES)]
+    parts = [part(t) for t in range(1)]
     for copy in small + parts:
         copy.start()
     for copy in small:
@@ -346,7 +346,7 @@
 
     @pl.when(level >= 1)
     def _():
-        collide(pops, 0, star, mask, relax_rate(level), lambda t: parts[t].wait())
+        collide(pops, 0, star, mask, relax_rate(level), lambda t: parts[t // 8].wait() if t % 8 == 0 else None)
 
     @pl.when(level < 1)
     def _():

time: 29.6 us -> 29.6 us (level)
  no operation moved by 1% of the time
where the time goes in v7:
time: 29.6 us; the launch traced here: 29.4 us
  waiting for transfers between devices  13.4 us (45%)
  starting transfers between devices  10.1 us (34%)
  Pallas kernels  5.81 us (20%)
    ppermute x14, waiting for transfers between devices, swap(): return lax.ppermute(x, ('section', 'member'), pairs)  13.4 us
    ppermute x14, starting transfers between devices, swap(): return lax.ppermute(x, ('section', 'member'), pairs)  10.1 us
    pallas_call x1, Pallas kernels, body(): pl.pallas_call(first_kernel, out_shape=(field, planes, jax.ShapeDtypeStru...  1.68 us
    pallas_call x1, Pallas kernels, body(): pl.pallas_call(functools.partial(last_kernel, blocks), out_shape=field, i...  1.63 us
    pallas_call x1, Pallas kernels, body(): pl.pallas_call(functools.partial(middle_kernel, blocks), out_shape=(field...  1.31 us
    pallas_call x1, Pallas kernels, body(): pl.pallas_call(functools.partial(plan_kernel, sizes), out_shape=jax.Shape...  1.14 us
  transfers between devices with their start and end apart: 14, of which 5 were waited for; matrix products, arithmetic and copies ran while one was open for 0% of the time, Pallas kernels for 4%

profile of v7, /device:TPU:6, one launch (start us, length us, event | category | flops | bytes accessed | tf_op | source)
XLA Modules:
  0.0 29.4 jit_solution(2888297756387582775)
XLA Ops:
  0.0 1.7 %first.1 = (f32[19,64,128]{2,1,0:T(8,128)S(1)}, f32[120,128]{1,0:T(8,128)S(1)}, s32[64,128]{1,0:T(8,128)S(1)}) custom-call(s32[4]{0:T(128)} %level_hbm.3, f32[19,64,128]{2,1,0:T(8,128)} %bitcast.16, s32[64,128]{1,0:T(8,128)} %bitcast.17), custom_call_target="tpu_custom_call" | custom-call | tf_op jit(solution)/shard_map/first/pallas_call | solution.py:510
  1.7 0.1 collective-permute-start.2
  1.8 2.0 %collective-permute-start.1 = (f32[120,128]{1,0:T(8,128)S(1)}, f32[120,128]{1,0:T(8,128)S(1)}, u32[]{:S(2)}, u32[]{:S(2)}) collective-permute-start(f32[120,128]{1,0:T(8,128)S(1)} %get-tuple-element.12), channel_id=1, source_target_pairs={{0,16},{1,17},{2,18},{3,19},{4,20},{5,21},{6,22},{7,23},{8,24},{9,... | collective-permute-start | bytes 184328 | tf_op jit(solution)/shard_map/ppermute | solution.py:442
  3.8 0.0 collective-permute-start
  3.8 4.2 %collective-permute-done = f32[120,128]{1,0:T(8,128)S(1)} collective-permute-done((f32[120,128]{1,0:T(8,128)S(1)}, f32[120,128]{1,0:T(8,128)S(1)}, u32[]{:S(2)}, u32[]{:S(2)}) %collective-permute-start) | collective-permute-done | bytes 61472 | tf_op jit(solution)/shard_map/ppermute | solution.py:442
  8.0 0.0 collective-permute-start.5
  8.0 1.7 %collective-permute-start.3 = (f32[240,128]{1,0:T(8,128)S(1)}, f32[240,128]{1,0:T(8,128)S(1)}, u32[]{:S(2)}, u32[]{:S(2)}) collective-permute-start(f32[240,128]{1,0:T(8,128)S(1)} %constant_dynamic-update-slice_fusion.own), channel_id=1, source_target_pairs={{0,1},{1,0},{2,3},{3,2},{4,5},{5,4},{6,7},{7,6},{8,9},{9,8},{10,11... | collective-permute-start | bytes 368648 | tf_op jit(solution)/shard_map/ppermute | solution.py:442
  9.7 0.0 collective-permute-done.1
  9.7 0.0 collective-permute-done.2
  9.7 0.4 %collective-permute-start.6 = (f32[240,128]{1,0:T(8,128)S(1)}, f32[240,128]{1,0:T(8,128)S(1)}, u32[]{:S(2)}, u32[]{:S(2)}) collective-permute-start(f32[240,128]{1,0:T(8,128)S(1)} %constant_dynamic-update-slice_fusion.2.own2), channel_id=1, source_target_pairs={{0,8},{1,2},{2,1},{3,4},{4,3},{5,6},{6,5},{7,15},{8,0},{9,10},{10,... | collective-permute-start | bytes 368648 | tf_op jit(solution)/shard_map/ppermute | solution.py:442
  10.1 1.4 %collective-permute-start.4 = (f32[240,128]{1,0:T(8,128)S(1)}, f32[240,128]{1,0:T(8,128)S(1)}, u32[]{:S(2)}, u32[]{:S(2)}) collective-permute-start(f32[240,128]{1,0:T(8,128)S(1)} %constant_dynamic-update-slice_fusion.2.own2), channel_id=1, source_target_pairs={{0,1},{1,0},{2,3},{3,2},{4,5},{5,4},{6,7},{7,6},{8,9},{9,8},{10,11... | collective-permute-start | bytes 368648 | tf_op jit(solution)/shard_map/ppermute | solution.py:442
  11.5 1.1 %plan.1 = s32[608,128]{1,0:T(8,128)S(1)} custom-call(s32[4]{0:T(128)} %level_hbm.3, s32[2,18]{1,0:T(2,128)} %near_hbm.1, s32[2,4,6]{2,1,0:T(4,128)} %bitcast.18), custom_call_target="tpu_custom_call" | custom-call | tf_op jit(solution)/shard_map/plan/pallas_call | solution.py:523
  12.6 0.2 collective-permute-done.5.near
  12.9 0.0 collective-permute-done.3.chip
  12.9 1.8 %collective-permute-done.6.far = f32[240,128]{1,0:T(8,128)S(1)} collective-permute-done((f32[240,128]{1,0:T(8,128)S(1)}, f32[240,128]{1,0:T(8,128)S(1)}, u32[]{:S(2)}, u32[]{:S(2)}) %collective-permute-start.6) | collective-permute-done | bytes 122912 | tf_op jit(solution)/shard_map/ppermute | solution.py:442
  14.7 0.0 collective-permute-done.4.chip2
  14.7 1.3 %middle.1 = (f32[19,64,128]{2,1,0:T(8,128)S(1)}, f32[120,128]{1,0:T(8,128)S(1)}) custom-call(s32[608,128]{1,0:T(8,128)S(1)} %plan.1, f32[19,64,128]{2,1,0:T(8,128)S(1)} %get-tuple-element.10.star, s32[64,128]{1,0:T(8,128)S(1)} %get-tuple-element.11.mask, f32[240,128]{1,0:T(8,128)S(1)} %constant_dynamic-update-slice_fusion.own, ...), custom_call_target="tpu_custom_call" | custom-call | tf_op jit(solution)/shard_map/middle/pallas_call | solution.py:539
  16.0 0.1 collective-permute-start.9
  16.1 2.0 %collective-permute-start.8 = (f32[120,128]{1,0:T(8,128)S(1)}, f32[120,128]{1,0:T(8,128)S(1)}, u32[]{:S(2)}, u32[]{:S(2)}) collective-permute-start(f32[120,128]{1,0:T(8,128)S(1)} %get-tuple-element.14), channel_id=1, source_target_pairs={{0,1},{1,0},{2,3},{3,2},{4,5},{5,4},{6,7},{7,6},{8,24},{9,25},{10,... | collective-permute-start | bytes 184328 | tf_op jit(solution)/shard_map/ppermute | solution.py:442
  18.0 0.0 collective-permute-start.7
  18.0 4.2 %collective-permute-done.7 = f32[120,128]{1,0:T(8,128)S(1)} collective-permute-done((f32[120,128]{1,0:T(8,128)S(1)}, f32[120,128]{1,0:T(8,128)S(1)}, u32[]{:S(2)}, u32[]{:S(2)}) %collective-permute-start.7) | collective-permute-done | bytes 61472 | tf_op jit(solution)/shard_map/ppermute | solution.py:442
  22.2 0.2 collective-permute-start.12
  22.4 0.6 %collective-permute-start.10 = (f32[240,128]{1,0:T(8,128)S(1)}, f32[240,128]{1,0:T(8,128)S(1)}, u32[]{:S(2)}, u32[]{:S(2)}) collective-permute-start(f32[240,128]{1,0:T(8,128)S(1)} %constant_dynamic-update-slice_fusion.4.own), channel_id=1, source_target_pairs={{0,1},{1,0},{2,3},{3,2},{4,5},{5,4},{6,7},{7,6},{8,9},{9,8},{10,11... | collective-permute-start | bytes 368648 | tf_op jit(solution)/shard_map/ppermute | solution.py:442
  23.0 0.0 collective-permute-done.9
  23.0 0.0 collective-permute-done.8
  23.0 1.3 %collective-permute-start.13 = (f32[120,128]{1,0:T(8,128)S(1)}, f32[120,128]{1,0:T(8,128)S(1)}, u32[]{:S(2)}, u32[]{:S(2)}) collective-permute-start(f32[120,128]{1,0:T(8,128)S(1)} %broadcast_select_fusion.own2), channel_id=1, source_target_pairs={{0,1},{1,0},{2,3},{3,2},{4,5},{5,4},{6,7},{7,6},{8,9},{9,8},{10,11... | collective-permute-start | bytes 184328 | tf_op jit(solution)/shard_map/ppermute | solution.py:442
  24.4 0.4 %collective-permute-start.11 = (f32[120,128]{1,0:T(8,128)S(1)}, f32[120,128]{1,0:T(8,128)S(1)}, u32[]{:S(2)}, u32[]{:S(2)}) collective-permute-start(f32[120,128]{1,0:T(8,128)S(1)} %broadcast_select_fusion.own2), channel_id=1, source_target_pairs={{0,1},{1,0},{2,3},{3,2},{4,5},{5,4},{6,7},{7,6},{8,9},{9,8},{10,11... | collective-permute-start | bytes 184328 | tf_op jit(solution)/shard_map/ppermute | solution.py:442
  24.9 2.9 %collective-permute-done.13.far = f32[120,128]{1,0:T(8,128)S(1)} collective-permute-done((f32[120,128]{1,0:T(8,128)S(1)}, f32[120,128]{1,0:T(8,128)S(1)}, u32[]{:S(2)}, u32[]{:S(2)}) %collective-permute-start.13) | collective-permute-done | bytes 61472 | tf_op jit(solution)/shard_map/ppermute | solution.py:442
  27.8 0.0 collective-permute-done.11.chip2
  27.8 0.0 collective-permute-done.12.near
  27.8 0.0 collective-permute-done.10.chip
  27.8 1.6 %last.1 = f32[19,64,128]{2,1,0:T(8,128)} custom-call(s32[608,128]{1,0:T(8,128)S(1)} %plan.1, f32[19,64,128]{2,1,0:T(8,128)S(1)} %get-tuple-element.13.star, f32[240,128]{1,0:T(8,128)S(1)} %constant_dynamic-update-slice_fusion.4.own, f32[120,128]{1,0:T(8,128)S(1)} %broadcast_select_fusion.own2, ...), custom_call_target="tpu_custom_call", output_to_operand_aliasing={{}: (8, {})} | custom-call | tf_op jit(solution)/shard_map/last/pallas_call | solution.py:558
  (8 shorter events, 0.1 us)
Async XLA Ops:
  1.7 8.0 %collective-permute-start.2 = (f32[120,128]{1,0:T(8,128)S(1)}, f32[120,128]{1,0:T(8,128)S(1)}, u32[]{:S(2)}, u32[]{:S(2)}) collective-permute-start(f32[120,128]{1,0:T(8,128)S(1)} %get-tuple-element.12), channel_id=1, source_target_pairs={{0,1},{1,0},{2,3},{3,2},{4,5},{5,4},{6,7},{7,6},{8,16},{9,17},{10,... | collective-permute-start | bytes 184328 | tf_op jit(solution)/shard_map/ppermute | solution.py:442
  1.8 7.9 %collective-permute-start.1 = (f32[120,128]{1,0:T(8,128)S(1)}, f32[120,128]{1,0:T(8,128)S(1)}, u32[]{:S(2)}, u32[]{:S(2)}) collective-permute-start(f32[120,128]{1,0:T(8,128)S(1)} %get-tuple-element.12), channel_id=1, source_target_pairs={{0,16},{1,17},{2,18},{3,19},{4,20},{5,21},{6,22},{7,23},{8,24},{9,... | collective-permute-start | bytes 184328 | tf_op jit(solution)/shard_map/ppermute | solution.py:442
  3.8 4.2 %collective-permute-start = (f32[120,128]{1,0:T(8,128)S(1)}, f32[120,128]{1,0:T(8,128)S(1)}, u32[]{:S(2)}, u32[]{:S(2)}) collective-permute-start(f32[120,128]{1,0:T(8,128)S(1)} %get-tuple-element.12), channel_id=1, source_target_pairs={{0,8},{1,9},{2,10},{3,11},{4,12},{5,13},{6,14},{7,15},{8,0},{9,1},... | collective-permute-start | bytes 184328 | tf_op jit(solution)/shard_map/ppermute | solution.py:442
  8.0 4.9 %collective-permute-start.5 = (f32[240,128]{1,0:T(8,128)S(1)}, f32[240,128]{1,0:T(8,128)S(1)}, u32[]{:S(2)}, u32[]{:S(2)}) collective-permute-start(f32[240,128]{1,0:T(8,128)S(1)} %constant_dynamic-update-slice_fusion.own), channel_id=1, source_target_pairs={{0,8},{1,2},{2,1},{3,4},{4,3},{5,6},{6,5},{7,15},{8,0},{9,10},{10,... | collective-permute-start | bytes 368648 | tf_op jit(solution)/shard_map/ppermute | solution.py:442
  8.0 4.9 %collective-permute-start.3 = (f32[240,128]{1,0:T(8,128)S(1)}, f32[240,128]{1,0:T(8,128)S(1)}, u32[]{:S(2)}, u32[]{:S(2)}) collective-permute-start(f32[240,128]{1,0:T(8,128)S(1)} %constant_dynamic-update-slice_fusion.own), channel_id=1, source_target_pairs={{0,1},{1,0},{2,3},{3,2},{4,5},{5,4},{6,7},{7,6},{8,9},{9,8},{10,11... | collective-permute-start | bytes 368648 | tf_op jit(solution)/shard_map/ppermute | solution.py:442
  9.7 4.9 %collective-permute-start.6 = (f32[240,128]{1,0:T(8,128)S(1)}, f32[240,128]{1,0:T(8,128)S(1)}, u32[]{:S(2)}, u32[]{:S(2)}) collective-permute-start(f32[240,128]{1,0:T(8,128)S(1)} %constant_dynamic-update-slice_fusion.2.own2), channel_id=1, source_target_pairs={{0,8},{1,2},{2,1},{3,4},{4,3},{5,6},{6,5},{7,15},{8,0},{9,10},{10,... | collective-permute-start | bytes 368648 | tf_op jit(solution)/shard_map/ppermute | solution.py:442
  10.1 4.5 %collective-permute-start.4 = (f32[240,128]{1,0:T(8,128)S(1)}, f32[240,128]{1,0:T(8,128)S(1)}, u32[]{:S(2)}, u32[]{:S(2)}) collective-permute-start(f32[240,128]{1,0:T(8,128)S(1)} %constant_dynamic-update-slice_fusion.2.own2), channel_id=1, source_target_pairs={{0,1},{1,0},{2,3},{3,2},{4,5},{5,4},{6,7},{7,6},{8,9},{9,8},{10,11... | collective-permute-start | bytes 368648 | tf_op jit(solution)/shard_map/ppermute | solution.py:442
  16.0 7.1 %collective-permute-start.9 = (f32[120,128]{1,0:T(8,128)S(1)}, f32[120,128]{1,0:T(8,128)S(1)}, u32[]{:S(2)}, u32[]{:S(2)}) collective-permute-start(f32[120,128]{1,0:T(8,128)S(1)} %get-tuple-element.14), channel_id=1, source_target_pairs={{0,1},{1,0},{2,3},{3,2},{4,5},{5,4},{6,7},{7,6},{8,16},{9,17},{10,... | collective-permute-start | bytes 184328 | tf_op jit(solution)/shard_map/ppermute | solution.py:442
  16.1 7.0 %collective-permute-start.8 = (f32[120,128]{1,0:T(8,128)S(1)}, f32[120,128]{1,0:T(8,128)S(1)}, u32[]{:S(2)}, u32[]{:S(2)}) collective-permute-start(f32[120,128]{1,0:T(8,128)S(1)} %get-tuple-element.14), channel_id=1, source_target_pairs={{0,1},{1,0},{2,3},{3,2},{4,5},{5,4},{6,7},{7,6},{8,24},{9,25},{10,... | collective-permute-start | bytes 184328 | tf_op jit(solution)/shard_map/ppermute | solution.py:442
  18.0 4.2 %collective-permute-start.7 = (f32[120,128]{1,0:T(8,128)S(1)}, f32[120,128]{1,0:T(8,128)S(1)}, u32[]{:S(2)}, u32[]{:S(2)}) collective-permute-start(f32[120,128]{1,0:T(8,128)S(1)} %get-tuple-element.14), channel_id=1, source_target_pairs={{0,1},{1,0},{2,3},{3,2},{4,5},{5,4},{6,7},{7,6},{8,9},{9,8},{10,11... | collective-permute-start | bytes 184328 | tf_op jit(solution)/shard_map/ppermute | solution.py:442
  22.2 5.5 %collective-permute-start.12 = (f32[240,128]{1,0:T(8,128)S(1)}, f32[240,128]{1,0:T(8,128)S(1)}, u32[]{:S(2)}, u32[]{:S(2)}) collective-permute-start(f32[240,128]{1,0:T(8,128)S(1)} %constant_dynamic-update-slice_fusion.4.own), channel_id=1, source_target_pairs={{0,1},{1,0},{2,3},{3,2},{4,5},{5,4},{6,7},{7,6},{8,9},{9,8},{10,11... | collective-permute-start | bytes 368648 | tf_op jit(solution)/shard_map/ppermute | solution.py:442
  22.4 5.4 %collective-permute-start.10 = (f32[240,128]{1,0:T(8,128)S(1)}, f32[240,128]{1,0:T(8,128)S(1)}, u32[]{:S(2)}, u32[]{:S(2)}) collective-permute-start(f32[240,128]{1,0:T(8,128)S(1)} %constant_dynamic-update-slice_fusion.4.own), channel_id=1, source_target_pairs={{0,1},{1,0},{2,3},{3,2},{4,5},{5,4},{6,7},{7,6},{8,9},{9,8},{10,11... | collective-permute-start | bytes 368648 | tf_op jit(solution)/shard_map/ppermute | solution.py:442
  23.0 4.7 %collective-permute-start.13 = (f32[120,128]{1,0:T(8,128)S(1)}, f32[120,128]{1,0:T(8,128)S(1)}, u32[]{:S(2)}, u32[]{:S(2)}) collective-permute-start(f32[120,128]{1,0:T(8,128)S(1)} %broadcast_select_fusion.own2), channel_id=1, source_target_pairs={{0,1},{1,0},{2,3},{3,2},{4,5},{5,4},{6,7},{7,6},{8,9},{9,8},{10,11... | collective-permute-start | bytes 184328 | tf_op jit(solution)/shard_map/ppermute | solution.py:442
  24.4 3.4 %collective-permute-start.11 = (f32[120,128]{1,0:T(8,128)S(1)}, f32[120,128]{1,0:T(8,128)S(1)}, u32[]{:S(2)}, u32[]{:S(2)}) collective-permute-start(f32[120,128]{1,0:T(8,128)S(1)} %broadcast_select_fusion.own2), channel_id=1, source_target_pairs={{0,1},{1,0},{2,3},{3,2},{4,5},{5,4},{6,7},{7,6},{8,9},{9,8},{10,11... | collective-permute-start | bytes 184328 | tf_op jit(solution)/shard_map/ppermute | solution.py:442

commit v8 on v7

--- a/solution.py
+++ b/solution.py
@@ -390,12 +390,12 @@
         copy.wait()
 
 
-def middle_kernel(blocks, plan, star, mask, own, own2, chip, chip2, near, far, dst, out, table, halo, moved):
+def middle_kernel(blocks, plan, star, mask, own, own2, chip, near, far, dst, out, table, halo, moved):
     level = number(plan, 0, 64)
 
     @pl.when(level >= 1)
     def _():
-        gathered((own, own2, chip, chip2, near, far), table)
+        gathered((own, own2, chip, near, far), table)
 
         @pl.when(number(plan, 0, 65) > 0)
         def _():
@@ -419,13 +419,13 @@
     export(dst, out)
 
 
-def last_kernel(blocks, plan, star, own, own2, chip, chip2, near, far, settled, result, table, halo, moved, sems):
+def last_kernel(blocks, plan, star, own, own2, chip, near, far, settled, result, table, halo, moved, sems):
     @pl.when(number(plan, 0, 64) == 2)
     def _():
         copies = [
             pltpu.make_async_copy(moved.at[q, 8 : 8 + ROWS], result.at[q], sems.at[q]) for q in range(19)
         ]
-        gathered((own, own2, chip, chip2, near, far), table)
+        gathered((own, own2, chip, near, far), table)
         arrived(plan, 32, table, halo, blocks, False)
         stream(star, moved, plan, 32, table, halo, blocks, lambda q: copies[q].start())
         for copy in copies:
@@ -476,9 +476,8 @@
         second = jnp.concatenate(parts[2:], axis=0)
     near = named(first, beside)
     far = named(second, beside)
-    chip = named(first, lambda s, m: (s, m ^ 1))
-    rest = named(second, lambda s, m: (s, m ^ 1))
-    return first, second, chip, rest, near, far
+    chip = named(jnp.concatenate([first, second], axis=0), lambda s, m: (s, m ^ 1))
+    return first, second, chip, near, far
 
 
 def packed(x):
@@ -539,7 +538,7 @@
     star, exports = pl.pallas_call(
         functools.partial(middle_kernel, blocks),
         out_shape=(field, planes),
-        in_specs=[VMEM] * 9,
+        in_specs=[VMEM] * 8,
         out_specs=(VMEM, VMEM),
         scratch_shapes=[pltpu.VMEM((3 * sections * blocks, ROWS, 128), jnp.float32), halo, moved],
         compiler_params=params,
@@ -558,9 +557,9 @@
     result = pl.pallas_call(
         functools.partial(last_kernel, blocks),
         out_shape=field,
-        in_specs=[VMEM] * 8 + [HBM],
+        in_specs=[VMEM] * 7 + [HBM],
         out_specs=HBM,
-        input_output_aliases={8: 0},
+        input_output_aliases={7: 0},
         scratch_shapes=[
             pltpu.VMEM((3 * (sections - 1) * blocks, ROWS, 128), jnp.float32),
             halo,

time: 29.6 us -> 30.1 us (1.017)
  the two profiles are of different devices: /device:TPU:6 before, /device:TPU:7 now
where the time goes in v8:
time: 30.1 us; the launch traced here: 30 us
  starting transfers between devices  13 us (43%)
  waiting for transfers between devices  11 us (37%)
  Pallas kernels  5.8 us (19%)
    ppermute x12, starting transfers between devices, swap(): return lax.ppermute(x, ('section', 'member'), pairs)  13 us
    ppermute x12, waiting for transfers between devices, swap(): return lax.ppermute(x, ('section', 'member'), pairs)  11 us
    pallas_call x1, Pallas kernels, body(): pl.pallas_call(first_kernel, out_shape=(field, planes, jax.ShapeDtypeStru...  1.68 us
    pallas_call x1, Pallas kernels, body(): pl.pallas_call(functools.partial(last_kernel, blocks), out_shape=field, i...  1.63 us
    pallas_call x1, Pallas kernels, body(): pl.pallas_call(functools.partial(middle_kernel, blocks), out_shape=(field...  1.31 us
    pallas_call x1, Pallas kernels, body(): pl.pallas_call(functools.partial(plan_kernel, sizes), out_shape=jax.Shape...  1.14 us
  transfers between devices with their start and end apart: 12, of which 5 were waited for; matrix products, arithmetic and copies ran while one was open for 0% of the time, Pallas kernels for 4%

profile of v8, /device:TPU:7, one launch (start us, length us, event | category | flops | bytes accessed | tf_op | source)
XLA Modules:
  0.0 30.0 jit_solution(13700242910198750225)
XLA Ops:
  0.0 1.7 %first.1 = (f32[19,64,128]{2,1,0:T(8,128)S(1)}, f32[120,128]{1,0:T(8,128)S(1)}, s32[64,128]{1,0:T(8,128)S(1)}) custom-call(s32[4]{0:T(128)} %level_hbm.3, f32[19,64,128]{2,1,0:T(8,128)} %bitcast.16, s32[64,128]{1,0:T(8,128)} %bitcast.17), custom_call_target="tpu_custom_call" | custom-call | tf_op jit(solution)/shard_map/first/pallas_call | solution.py:509
  1.7 0.7 %collective-permute-start.2 = (f32[120,128]{1,0:T(8,128)S(1)}, f32[120,128]{1,0:T(8,128)S(1)}, u32[]{:S(2)}, u32[]{:S(2)}) collective-permute-start(f32[120,128]{1,0:T(8,128)S(1)} %get-tuple-element.12), channel_id=1, source_target_pairs={{0,1},{1,0},{2,3},{3,2},{4,5},{5,4},{6,7},{7,6},{8,16},{9,17},{10,... | collective-permute-start | bytes 184328 | tf_op jit(solution)/shard_map/ppermute | solution.py:442
  2.4 0.8 %collective-permute-start.1 = (f32[120,128]{1,0:T(8,128)S(1)}, f32[120,128]{1,0:T(8,128)S(1)}, u32[]{:S(2)}, u32[]{:S(2)}) collective-permute-start(f32[120,128]{1,0:T(8,128)S(1)} %get-tuple-element.12), channel_id=1, source_target_pairs={{0,16},{1,17},{2,18},{3,19},{4,20},{5,21},{6,22},{7,23},{8,24},{9,... | collective-permute-start | bytes 184328 | tf_op jit(solution)/shard_map/ppermute | solution.py:442
  3.2 0.0 collective-permute-start
  3.2 3.4 %collective-permute-done = f32[120,128]{1,0:T(8,128)S(1)} collective-permute-done((f32[120,128]{1,0:T(8,128)S(1)}, f32[120,128]{1,0:T(8,128)S(1)}, u32[]{:S(2)}, u32[]{:S(2)}) %collective-permute-start) | collective-permute-done | bytes 61472 | tf_op jit(solution)/shard_map/ppermute | solution.py:442
  6.6 3.3 %collective-permute-start.4 = (f32[240,128]{1,0:T(8,128)S(1)}, f32[240,128]{1,0:T(8,128)S(1)}, u32[]{:S(2)}, u32[]{:S(2)}) collective-permute-start(f32[240,128]{1,0:T(8,128)S(1)} %constant_dynamic-update-slice_fusion.own), channel_id=1, source_target_pairs={{0,8},{1,2},{2,1},{3,4},{4,3},{5,6},{6,5},{7,15},{8,0},{9,10},{10,... | collective-permute-start | bytes 368648 | tf_op jit(solution)/shard_map/ppermute | solution.py:442
  9.8 0.0 collective-permute-done.2
  9.8 0.0 collective-permute-done.1
  9.9 0.1 collective-permute-start.3
  10.0 1.7 %collective-permute-start.5 = (f32[240,128]{1,0:T(8,128)S(1)}, f32[240,128]{1,0:T(8,128)S(1)}, u32[]{:S(2)}, u32[]{:S(2)}) collective-permute-start(f32[240,128]{1,0:T(8,128)S(1)} %constant_dynamic-update-slice_fusion.2.own2), channel_id=1, source_target_pairs={{0,8},{1,2},{2,1},{3,4},{4,3},{5,6},{6,5},{7,15},{8,0},{9,10},{10,... | collective-permute-start | bytes 368648 | tf_op jit(solution)/shard_map/ppermute | solution.py:442
  11.7 1.1 %plan.1 = s32[608,128]{1,0:T(8,128)S(1)} custom-call(s32[4]{0:T(128)} %level_hbm.3, s32[2,18]{1,0:T(2,128)} %near_hbm.1, s32[2,4,6]{2,1,0:T(4,128)} %bitcast.18), custom_call_target="tpu_custom_call" | custom-call | tf_op jit(solution)/shard_map/plan/pallas_call | solution.py:522
  12.9 0.0 collective-permute-done.4.near
  12.9 1.8 %collective-permute-done.5.far = f32[240,128]{1,0:T(8,128)S(1)} collective-permute-done((f32[240,128]{1,0:T(8,128)S(1)}, f32[240,128]{1,0:T(8,128)S(1)}, u32[]{:S(2)}, u32[]{:S(2)}) %collective-permute-start.5) | collective-permute-done | bytes 122912 | tf_op jit(solution)/shard_map/ppermute | solution.py:442
  14.6 0.0 collective-permute-done.3.chip
  14.6 1.3 %middle.1 = (f32[19,64,128]{2,1,0:T(8,128)S(1)}, f32[120,128]{1,0:T(8,128)S(1)}) custom-call(s32[608,128]{1,0:T(8,128)S(1)} %plan.1, f32[19,64,128]{2,1,0:T(8,128)S(1)} %get-tuple-element.10.star, s32[64,128]{1,0:T(8,128)S(1)} %get-tuple-element.11.mask, f32[240,128]{1,0:T(8,128)S(1)} %constant_dynamic-update-slice_fusion.own, ...), custom_call_target="tpu_custom_call" | custom-call | tf_op jit(solution)/shard_map/middle/pallas_call | solution.py:538
  16.0 0.8 %collective-permute-start.8 = (f32[120,128]{1,0:T(8,128)S(1)}, f32[120,128]{1,0:T(8,128)S(1)}, u32[]{:S(2)}, u32[]{:S(2)}) collective-permute-start(f32[120,128]{1,0:T(8,128)S(1)} %get-tuple-element.14), channel_id=1, source_target_pairs={{0,1},{1,0},{2,3},{3,2},{4,5},{5,4},{6,7},{7,6},{8,16},{9,17},{10,... | collective-permute-start | bytes 184328 | tf_op jit(solution)/shard_map/ppermute | solution.py:442
  16.8 0.7 %collective-permute-start.7 = (f32[120,128]{1,0:T(8,128)S(1)}, f32[120,128]{1,0:T(8,128)S(1)}, u32[]{:S(2)}, u32[]{:S(2)}) collective-permute-start(f32[120,128]{1,0:T(8,128)S(1)} %get-tuple-element.14), channel_id=1, source_target_pairs={{0,1},{1,0},{2,3},{3,2},{4,5},{5,4},{6,7},{7,6},{8,24},{9,25},{10,... | collective-permute-start | bytes 184328 | tf_op jit(solution)/shard_map/ppermute | solution.py:442
  17.5 1.0 %collective-permute-start.6 = (f32[120,128]{1,0:T(8,128)S(1)}, f32[120,128]{1,0:T(8,128)S(1)}, u32[]{:S(2)}, u32[]{:S(2)}) collective-permute-start(f32[120,128]{1,0:T(8,128)S(1)} %get-tuple-element.14), channel_id=1, source_target_pairs={{0,1},{1,0},{2,3},{3,2},{4,5},{5,4},{6,7},{7,6},{8,9},{9,8},{10,11... | collective-permute-start | bytes 184328 | tf_op jit(solution)/shard_map/ppermute | solution.py:442
  18.5 0.0 collective-permute-done.8
  18.5 1.8 %collective-permute-done.7 = f32[120,128]{1,0:T(8,128)S(1)} collective-permute-done((f32[120,128]{1,0:T(8,128)S(1)}, f32[120,128]{1,0:T(8,128)S(1)}, u32[]{:S(2)}, u32[]{:S(2)}) %collective-permute-start.7) | collective-permute-done | bytes 61472 | tf_op jit(solution)/shard_map/ppermute | solution.py:442
  20.3 0.6 %collective-permute-done.6 = f32[120,128]{1,0:T(8,128)S(1)} collective-permute-done((f32[120,128]{1,0:T(8,128)S(1)}, f32[120,128]{1,0:T(8,128)S(1)}, u32[]{:S(2)}, u32[]{:S(2)}) %collective-permute-start.6) | collective-permute-done | bytes 61472 | tf_op jit(solution)/shard_map/ppermute | solution.py:442
  20.9 2.2 %collective-permute-start.9 = (f32[360,128]{1,0:T(8,128)S(1)}, f32[360,128]{1,0:T(8,128)S(1)}, u32[]{:S(2)}, u32[]{:S(2)}) collective-permute-start(f32[360,128]{1,0:T(8,128)S(1)} %pad_maximum_fusion.1), channel_id=1, source_target_pairs={{0,1},{1,0},{2,3},{3,2},{4,5},{5,4},{6,7},{7,6},{8,9},{9,8},{10,11... | collective-permute-start | bytes 552968 | tf_op jit(solution)/shard_map/ppermute | solution.py:442
  23.1 0.3 %collective-permute-start.10 = (f32[240,128]{1,0:T(8,128)S(1)}, f32[240,128]{1,0:T(8,128)S(1)}, u32[]{:S(2)}, u32[]{:S(2)}) collective-permute-start(f32[240,128]{1,0:T(8,128)S(1)} %constant_dynamic-update-slice_fusion.4.own), channel_id=1, source_target_pairs={{0,1},{1,0},{2,3},{3,2},{4,5},{5,4},{6,7},{7,6},{8,9},{9,8},{10,11... | collective-permute-start | bytes 368648 | tf_op jit(solution)/shard_map/ppermute | solution.py:442
  23.4 1.4 %collective-permute-start.11 = (f32[120,128]{1,0:T(8,128)S(1)}, f32[120,128]{1,0:T(8,128)S(1)}, u32[]{:S(2)}, u32[]{:S(2)}) collective-permute-start(f32[120,128]{1,0:T(8,128)S(1)} %broadcast_select_fusion.own2), channel_id=1, source_target_pairs={{0,1},{1,0},{2,3},{3,2},{4,5},{5,4},{6,7},{7,6},{8,9},{9,8},{10,11... | collective-permute-start | bytes 184328 | tf_op jit(solution)/shard_map/ppermute | solution.py:442
  24.9 3.4 %collective-permute-done.11.far = f32[120,128]{1,0:T(8,128)S(1)} collective-permute-done((f32[120,128]{1,0:T(8,128)S(1)}, f32[120,128]{1,0:T(8,128)S(1)}, u32[]{:S(2)}, u32[]{:S(2)}) %collective-permute-start.11) | collective-permute-done | bytes 61472 | tf_op jit(solution)/shard_map/ppermute | solution.py:442
  28.3 0.0 collective-permute-done.10.near
  28.3 0.0 collective-permute-done.9.chip
  28.3 1.6 %last.1 = f32[19,64,128]{2,1,0:T(8,128)} custom-call(s32[608,128]{1,0:T(8,128)S(1)} %plan.1, f32[19,64,128]{2,1,0:T(8,128)S(1)} %get-tuple-element.13.star, f32[240,128]{1,0:T(8,128)S(1)} %constant_dynamic-update-slice_fusion.4.own, f32[120,128]{1,0:T(8,128)S(1)} %broadcast_select_fusion.own2, ...), custom_call_target="tpu_custom_call", output_to_operand_aliasing={{}: (7, {})} | custom-call | tf_op jit(solution)/shard_map/last/pallas_call | solution.py:557
  (10 shorter events, 0.1 us)
Async XLA Ops:
  1.7 8.2 %collective-permute-start.2 = (f32[120,128]{1,0:T(8,128)S(1)}, f32[120,128]{1,0:T(8,128)S(1)}, u32[]{:S(2)}, u32[]{:S(2)}) collective-permute-start(f32[120,128]{1,0:T(8,128)S(1)} %get-tuple-element.12), channel_id=1, source_target_pairs={{0,1},{1,0},{2,3},{3,2},{4,5},{5,4},{6,7},{7,6},{8,16},{9,17},{10,... | collective-permute-start | bytes 184328 | tf_op jit(solution)/shard_map/ppermute | solution.py:442
  2.4 7.4 %collective-permute-start.1 = (f32[120,128]{1,0:T(8,128)S(1)}, f32[120,128]{1,0:T(8,128)S(1)}, u32[]{:S(2)}, u32[]{:S(2)}) collective-permute-start(f32[120,128]{1,0:T(8,128)S(1)} %get-tuple-element.12), channel_id=1, source_target_pairs={{0,16},{1,17},{2,18},{3,19},{4,20},{5,21},{6,22},{7,23},{8,24},{9,... | collective-permute-start | bytes 184328 | tf_op jit(solution)/shard_map/ppermute | solution.py:442
  3.2 3.4 %collective-permute-start = (f32[120,128]{1,0:T(8,128)S(1)}, f32[120,128]{1,0:T(8,128)S(1)}, u32[]{:S(2)}, u32[]{:S(2)}) collective-permute-start(f32[120,128]{1,0:T(8,128)S(1)} %get-tuple-element.12), channel_id=1, source_target_pairs={{0,8},{1,9},{2,10},{3,11},{4,12},{5,13},{6,14},{7,15},{8,0},{9,1},... | collective-permute-start | bytes 184328 | tf_op jit(solution)/shard_map/ppermute | solution.py:442
  6.6 6.3 %collective-permute-start.4 = (f32[240,128]{1,0:T(8,128)S(1)}, f32[240,128]{1,0:T(8,128)S(1)}, u32[]{:S(2)}, u32[]{:S(2)}) collective-permute-start(f32[240,128]{1,0:T(8,128)S(1)} %constant_dynamic-update-slice_fusion.own), channel_id=1, source_target_pairs={{0,8},{1,2},{2,1},{3,4},{4,3},{5,6},{6,5},{7,15},{8,0},{9,10},{10,... | collective-permute-start | bytes 368648 | tf_op jit(solution)/shard_map/ppermute | solution.py:442
  9.9 4.8 %collective-permute-start.3 = (f32[480,128]{1,0:T(8,128)S(1)}, f32[480,128]{1,0:T(8,128)S(1)}, u32[]{:S(2)}, u32[]{:S(2)}) collective-permute-start(f32[480,128]{1,0:T(8,128)S(1)} %pad_maximum_fusion), channel_id=1, source_target_pairs={{0,1},{1,0},{2,3},{3,2},{4,5},{5,4},{6,7},{7,6},{8,9},{9,8},{10,11... | collective-permute-start | bytes 737288 | tf_op jit(solution)/shard_map/ppermute | solution.py:442
  10.0 4.7 %collective-permute-start.5 = (f32[240,128]{1,0:T(8,128)S(1)}, f32[240,128]{1,0:T(8,128)S(1)}, u32[]{:S(2)}, u32[]{:S(2)}) collective-permute-start(f32[240,128]{1,0:T(8,128)S(1)} %constant_dynamic-update-slice_fusion.2.own2), channel_id=1, source_target_pairs={{0,8},{1,2},{2,1},{3,4},{4,3},{5,6},{6,5},{7,15},{8,0},{9,10},{10,... | collective-permute-start | bytes 368648 | tf_op jit(solution)/shard_map/ppermute | solution.py:442
  16.0 2.5 %collective-permute-start.8 = (f32[120,128]{1,0:T(8,128)S(1)}, f32[120,128]{1,0:T(8,128)S(1)}, u32[]{:S(2)}, u32[]{:S(2)}) collective-permute-start(f32[120,128]{1,0:T(8,128)S(1)} %get-tuple-element.14), channel_id=1, source_target_pairs={{0,1},{1,0},{2,3},{3,2},{4,5},{5,4},{6,7},{7,6},{8,16},{9,17},{10,... | collective-permute-start | bytes 184328 | tf_op jit(solution)/shard_map/ppermute | solution.py:442
  16.8 3.5 %collective-permute-start.7 = (f32[120,128]{1,0:T(8,128)S(1)}, f32[120,128]{1,0:T(8,128)S(1)}, u32[]{:S(2)}, u32[]{:S(2)}) collective-permute-start(f32[120,128]{1,0:T(8,128)S(1)} %get-tuple-element.14), channel_id=1, source_target_pairs={{0,1},{1,0},{2,3},{3,2},{4,5},{5,4},{6,7},{7,6},{8,24},{9,25},{10,... | collective-permute-start | bytes 184328 | tf_op jit(solution)/shard_map/ppermute | solution.py:442
  17.5 3.5 %collective-permute-start.6 = (f32[120,128]{1,0:T(8,128)S(1)}, f32[120,128]{1,0:T(8,128)S(1)}, u32[]{:S(2)}, u32[]{:S(2)}) collective-permute-start(f32[120,128]{1,0:T(8,128)S(1)} %get-tuple-element.14), channel_id=1, source_target_pairs={{0,1},{1,0},{2,3},{3,2},{4,5},{5,4},{6,7},{7,6},{8,9},{9,8},{10,11... | collective-permute-start | bytes 184328 | tf_op jit(solution)/shard_map/ppermute | solution.py:442
  20.9 7.4 %collective-permute-start.9 = (f32[360,128]{1,0:T(8,128)S(1)}, f32[360,128]{1,0:T(8,128)S(1)}, u32[]{:S(2)}, u32[]{:S(2)}) collective-permute-start(f32[360,128]{1,0:T(8,128)S(1)} %pad_maximum_fusion.1), channel_id=1, source_target_pairs={{0,1},{1,0},{2,3},{3,2},{4,5},{5,4},{6,7},{7,6},{8,9},{9,8},{10,11... | collective-permute-start | bytes 552968 | tf_op jit(solution)/shard_map/ppermute | solution.py:442
  23.1 5.2 %collective-permute-start.10 = (f32[240,128]{1,0:T(8,128)S(1)}, f32[240,128]{1,0:T(8,128)S(1)}, u32[]{:S(2)}, u32[]{:S(2)}) collective-permute-start(f32[240,128]{1,0:T(8,128)S(1)} %constant_dynamic-update-slice_fusion.4.own), channel_id=1, source_target_pairs={{0,1},{1,0},{2,3},{3,2},{4,5},{5,4},{6,7},{7,6},{8,9},{9,8},{10,11... | collective-permute-start | bytes 368648 | tf_op jit(solution)/shard_map/ppermute | solution.py:442
  23.4 4.9 %collective-permute-start.11 = (f32[120,128]{1,0:T(8,128)S(1)}, f32[120,128]{1,0:T(8,128)S(1)}, u32[]{:S(2)}, u32[]{:S(2)}) collective-permute-start(f32[120,128]{1,0:T(8,128)S(1)} %broadcast_select_fusion.own2), channel_id=1, source_target_pairs={{0,1},{1,0},{2,3},{3,2},{4,5},{5,4},{6,7},{7,6},{8,9},{9,8},{10,11... | collective-permute-start | bytes 184328 | tf_op jit(solution)/shard_map/ppermute | solution.py:442
